TPU v7x, 256 devices: a whole 4x4x8 slice. The times are simulated.
256 devices in a mesh: ka: 64 (over z, y_lo, x), ga: 4 (over y_hi, core).
Axes of the slice: x: 4, y: 4 (y_hi: 2, y_lo: 2; y = y_hi * 2 + y_lo), z: 8, core: 2. Of those that a mesh axis runs over, the one named last changes fastest.
Arguments:
- orbitals: bfloat16 [2, 256, 128, 4096], P(None, 'ka', None, 'ga')
- gauge: bfloat16 [2, 256, 128, 128], P(None, 'ka'), may hold values from -0.5 to 0.5
- neighbour: int32 [256, 3], replicated, may hold values from 0 to 255, as said below
- wrap_shift: int32 [256, 3, 3], replicated, may hold values from 0 to 1, as said below
Outputs:
- forward: float32 [3, 2, 256, 128, 128], P(None, None, 'ka')
- backward: float32 [3, 2, 256, 128, 128], P(None, None, 'ka')
Inputs may be any that keep to these rules, and one draw needn't show every extreme that they name: The k point k lies on device k // 4 of ka, whose index is d = j * 4 + i. For each direction b the map k -> neighbour[k, b] is a permutation; neighbour[k, 0] lies on the same device, neighbour[k, 1] on device j * 4 + (i + 1) % 4, neighbour[k, 2] on device (d + 4) % 64. wrap_shift[k, b, d] is zero for d != b.
All inputs are finite; a program needn't handle non-finite values.
Results may differ from a plain program's by a relative error of at most 0.00084.
Values may be sent and summed in bfloat16 or wider, within the bound.
No kernel may reach another device: no remote copies, remote signals or barrier semaphores. Data moves between devices by JAX's collectives and lax.ppermute only.
A program may use at most 64 MiB of HBM per device.

v0:
```python
import math

import jax
import jax.numpy as jnp
from jax import lax
from jax.sharding import PartitionSpec as P

KRING = 4
GY = 32
GZ = 32


def from_behind(array, axis, by):
    size = lax.axis_size(axis)
    return lax.ppermute(array, axis, [(i, (i + by) % size) for i in range(size)])


def grid_fractions(plane_first, plane_count, plane_total):
    point_index = jnp.arange(plane_count * GY * GZ, dtype=jnp.int32)
    plane = point_index // (GY * GZ) + plane_first
    middle = point_index // GZ % GY
    inner = point_index % GZ
    return [
        plane.astype(jnp.float32) / jnp.float32(plane_total),
        middle.astype(jnp.float32) / jnp.float32(GY),
        inner.astype(jnp.float32) / jnp.float32(GZ),
    ]


def phase_angles(shift_rows, direction, mesh_counts, fractions):
    total = jnp.zeros((shift_rows.shape[0], fractions[0].shape[0]), jnp.float32)
    for lattice in range(3):
        step = 1.0 / mesh_counts[lattice] if lattice == direction else 0.0
        wave = shift_rows[:, lattice].astype(jnp.float32) + jnp.float32(step)
        total = total + wave[:, None] * fractions[lattice][None, :]
    return jnp.float32(2.0 * math.pi) * total


def phase_apply(angles, source):
    cosine = jnp.cos(angles)[:, None, :]
    sine = jnp.sin(angles)[:, None, :]
    source_re = source[0].astype(jnp.float32)
    source_im = source[1].astype(jnp.float32)
    return jnp.stack(
        [cosine * source_re + sine * source_im, cosine * source_im - sine * source_re]
    ).astype(jnp.bfloat16)


def split_parts(values):
    high = values.astype(jnp.bfloat16)
    back = lax.optimization_barrier(high).astype(jnp.float32)
    low = (values - back).astype(jnp.bfloat16)
    return (high, low)


def rotate_blocks(blocks, left, right):

    def times(first, second):
        high, low = split_parts(first)
        return jnp.einsum(
            "kab,kbc->kac", high, second, preferred_element_type=jnp.float32
        ) + jnp.einsum("kab,kbc->kac", low, second, preferred_element_type=jnp.float32)

    def adjoint(first, second):
        high, low = split_parts(second)
        return jnp.einsum(
            "kba,kbc->kac", first, high, preferred_element_type=jnp.float32
        ) + jnp.einsum("kba,kbc->kac", first, low, preferred_element_type=jnp.float32)

    temp_re = times(blocks[0], right[0]) - times(blocks[1], right[1])
    temp_im = times(blocks[0], right[1]) + times(blocks[1], right[0])
    out_re = adjoint(left[0], temp_re) + adjoint(left[1], temp_im)
    out_im = adjoint(left[0], temp_im) - adjoint(left[1], temp_re)
    return jnp.stack([out_re, out_im])


def correlation_terms(own, phased):

    def product(first, second):
        return jnp.einsum("kag,kbg->kab", first, second, preferred_element_type=jnp.float32)

    block_re = product(own[0], phased[0]) + product(own[1], phased[1])
    block_im = product(own[0], phased[1]) - product(own[1], phased[0])
    return jnp.stack([block_re, block_im])


def rotate_all(blocks, lefts, rights):
    rotated = []
    for direction in range(3):
        right = rights[direction]
        rotated.append(rotate_blocks(blocks[direction], lefts, right))
    return jnp.stack(rotated)


def partner_slots(neighbour, partner_dev, direction, my_rows, kloc):
    rows = lax.dynamic_slice_in_dim(neighbour[:, direction], partner_dev * kloc, kloc, 0)
    equal = rows[None, :] == my_rows[:, None]
    return jnp.sum(jnp.where(equal, jnp.arange(kloc, dtype=jnp.int32)[None, :], 0), axis=1)


def shards(orbitals, gauge, neighbour, wrap_shift):
    kloc = orbitals.shape[1]
    grid_points = orbitals.shape[3]
    ka_count = lax.axis_size("ka")
    ga_count = lax.axis_size("ga")
    device = lax.axis_index("ka")
    grid_part = lax.axis_index("ga")
    plane_count = grid_points // (GY * GZ)
    fractions = grid_fractions(grid_part * plane_count, plane_count, plane_count * ga_count)
    counts = (kloc, KRING, ka_count // KRING)
    cycle_pos = device % KRING
    my_rows = device * kloc + jnp.arange(kloc, dtype=jnp.int32)
    my_table = lax.dynamic_slice_in_dim(neighbour, device * kloc, kloc, 0)
    my_shift = lax.dynamic_slice_in_dim(wrap_shift, device * kloc, kloc, 0)

    def fetch_forward(offset):
        return from_behind((orbitals, gauge), "ka", offset)

    ahead = fetch_forward(-1)
    beside_all = fetch_forward(KRING - 1)
    beyond = fetch_forward(-KRING)
    cycle_slab = tuple(
        (
            jnp.where(cycle_pos == KRING - 1, wrapped, plain)
            for plain, wrapped in zip(ahead, beside_all)
        )
    )
    sources = [(orbitals, gauge), cycle_slab, beyond]
    partials = []
    rights = []
    for direction in range(3):
        slots = my_table[:, direction] % kloc
        source_orb = jnp.take(sources[direction][0], slots, axis=1)
        source_gauge = jnp.take(sources[direction][1], slots, axis=1)
        angles = phase_angles(my_shift[:, direction, :], direction, counts, fractions)
        partials.append(correlation_terms(orbitals, phase_apply(angles, source_orb)))
        rights.append(source_gauge)
    forward_raw = jnp.stack(partials)
    right_gauge = jnp.stack(rights)
    partner_devs = [
        device,
        jnp.where(cycle_pos == 0, device + KRING - 1, device - 1),
        (device - KRING + ka_count) % ka_count,
    ]
    pslots = [
        partner_slots(neighbour, partner_devs[direction], direction, my_rows, kloc)
        for direction in range(3)
    ]
    raw = (forward_raw,)
    summed = lax.psum((raw[0],), "ga")
    pieces = (rotate_all(summed[0], gauge, right_gauge),)
    forward = pieces[0]

    def fetch_block(block, offset):
        return from_behind(block, "ka", offset)

    first_back = jnp.take(forward[0], pslots[0], axis=1)
    cycle_prev = fetch_block(forward[1], 1)
    cycle_wrap = fetch_block(forward[1], 1 - KRING)
    second_back = jnp.take(jnp.where(cycle_pos == 0, cycle_wrap, cycle_prev), pslots[1], axis=1)
    third_back = jnp.take(fetch_block(forward[2], KRING), pslots[2], axis=1)
    back_blocks = jnp.stack([first_back, second_back, third_back])
    backward = jnp.stack(
        [jnp.swapaxes(back_blocks[:, 0], -1, -2), -jnp.swapaxes(back_blocks[:, 1], -1, -2)], axis=1
    )
    return (forward, backward)


def solution(mesh):
    in_specs = (P(None, "ka", None, "ga"), P(None, "ka", None, None), P(), P())
    out_specs = (P(None, None, "ka", None, None), P(None, None, "ka", None, None))
    return jax.shard_map(shards, mesh=mesh, in_specs=in_specs, out_specs=out_specs, check_vma=False)
```

profile of v0, /device:TPU:1, one launch (start us, length us, event | category | flops | bytes accessed | tf_op | source)
XLA Modules:
  0.0 275.7 jit_solution(855758753109980142)
XLA Ops:
  7.2 3.4 %collective-permute-start = (bf16[2,4,128,1024]{3,2,1,0:T(8,128)(2,1)}, bf16[2,4,128,1024]{3,2,1,0:T(8,128)(2,1)}, u32[]{:S(2)}, u32[]{:S(2)}) collective-permute-start(bf16[2,4,128,1024]{3,2,1,0:T(8,128)(2,1)} %param.10), channel_id=1, source_target_pairs={{0,12},{4,16},{8,20},{12,24},{16,28},{20,32},{24,36},{28,40},{32,4... | collective-permute-start | bytes 6291464 | tf_op jit(solution)/shard_map/ppermute | solution.py:15
  10.6 6.4 %collective-permute-start.1 = (bf16[2,4,128,1024]{3,2,1,0:T(8,128)(2,1)}, bf16[2,4,128,1024]{3,2,1,0:T(8,128)(2,1)}, u32[]{:S(2)}, u32[]{:S(2)}) collective-permute-start(bf16[2,4,128,1024]{3,2,1,0:T(8,128)(2,1)} %param.10), channel_id=1, source_target_pairs={{0,252},{4,0},{8,4},{12,8},{16,12},{20,16},{24,20},{28,24},{32,28}... | collective-permute-start | bytes 6291464 | tf_op jit(solution)/shard_map/ppermute | solution.py:15
  17.0 1.6 collective-permute-start.2
  18.6 2.5 collective-permute-start.4
  21.1 0.8 fusion.196
  21.9 0.8 constant_dynamic-slice_fusion.5
  22.7 0.8 constant_dynamic-slice_fusion.1
  24.1 0.3 convert_reduce_fusion.1
  24.7 0.4 fusion.131
  25.1 2.3 gather_fusion
  27.4 0.3 select_bitcast_fusion.2
  27.7 1.3 copy-done.2
  29.0 0.6 fusion.56
  29.6 0.6 fusion.58
  30.1 0.6 fusion.34
  30.7 0.6 fusion.35
  31.4 68.7 %collective-permute-done = bf16[2,4,128,1024]{3,2,1,0:T(8,128)(2,1)} collective-permute-done((bf16[2,4,128,1024]{3,2,1,0:T(8,128)(2,1)}, bf16[2,4,128,1024]{3,2,1,0:T(8,128)(2,1)}, u32[]{:S(2)}, u32[]{:S(2)}) %collective-permute-start) | collective-permute-done | bytes 2097184 | tf_op jit(solution)/shard_map/ppermute | solution.py:15
  100.2 0.7 collective-permute-done.1
  100.9 3.1 %broadcast_select_fusion = bf16[2,4,128,1024]{3,2,1,0:T(8,128)(2,1)} fusion(bf16[2,4,128,1024]{3,2,1,0:T(8,128)(2,1)} %collective-permute-done, bf16[2,4,128,1024]{3,2,1,0:T(8,128)(2,1)} %collective-permute-done.1, pred[]{:T(512)S(6)} %eq.59), kind=kLoop, calls=%fused_computation.36 | loop fusion | flops 1048576 | bytes 6291457 | tf_op jit(solution)/shard_map/jit(_where)/select_n | solution.py:124
  104.0 2.3 gather_fusion.1
  106.3 38.1 %collective-permute-done.2 = bf16[2,4,128,1024]{3,2,1,0:T(8,128)(2,1)} collective-permute-done((bf16[2,4,128,1024]{3,2,1,0:T(8,128)(2,1)}, bf16[2,4,128,1024]{3,2,1,0:T(8,128)(2,1)}, u32[]{:S(2)}, u32[]{:S(2)}) %collective-permute-start.2) | collective-permute-done | bytes 2097184 | tf_op jit(solution)/shard_map/ppermute | solution.py:15
  144.4 3.6 %gather_fusion.2 = bf16[4,2,128,1024]{3,2,1,0:T(8,128)(2,1)} fusion(bf16[2,4,128,1024]{3,2,1,0:T(8,128)(2,1)} %collective-permute-done.2, s32[1024]{0:T(1024)S(1)} %pad_clamp_fusion.3), kind=kCustom, calls=%fused_computation.4.clone | custom fusion | bytes 4194320 | tf_op jit(solution)/shard_map/jit(_take)/gather | solution.py:133
  148.0 2.2 select_bitcast_fusion
  150.2 0.6 fusion.54
  150.8 0.6 fusion.52
  151.4 0.6 fusion.50
  152.0 0.6 fusion.48
  152.6 0.6 fusion.33
  153.2 0.6 fusion.32
  153.8 0.6 fusion.31
  154.4 0.6 fusion.30
  155.1 1.2 pad_maximum_fusion
  156.3 0.6 gather_fusion.3
  157.1 1.0 broadcast_select_fusion.2
  158.1 0.6 gather_fusion.4
  158.8 0.6 gather_fusion.5
  159.5 63.8 %all-reduce.2.cloned.1.call-done = f32[3,2,4,128,128]{3,4,2,1,0:T(8,128)} async-done(((f32[3,2,4,128,128]{3,4,2,1,0:T(8,128)}), f32[3,2,4,128,128]{3,4,2,1,0:T(8,128)}) %all-reduce.2.cloned.1.call-update) | async-done | bytes 1572880 | tf_op jit(solution)/shard_map/psum | solution.py:150
  223.3 1.6 fusion.77
  225.7 0.2 fusion.200
  226.9 0.2 fusion.199
  228.4 0.2 fusion.21
  228.6 0.2 fusion.19
  228.9 0.9 pad_maximum_fusion.5
  229.8 4.0 %collective-permute-start.6 = (f32[2,4,128,128]{2,3,1,0:T(8,128)}, f32[2,4,128,128]{2,3,1,0:T(8,128)}, u32[]{:S(2)}, u32[]{:S(2)}) collective-permute-start(f32[2,4,128,128]{2,3,1,0:T(8,128)} %get-tuple-element.39), channel_id=1, source_target_pairs={{0,244},{4,248},{8,252},{12,0},{16,4},{20,8},{24,12},{28,16},{32,2... | collective-permute-start | bytes 1572872 | tf_op jit(solution)/shard_map/ppermute | solution.py:15
  233.7 1.2 collective-permute-start.7
  235.6 0.2 fusion.202
  236.9 0.2 fusion.201
  238.6 0.2 fusion.198
  239.8 0.2 fusion.197
  241.0 0.2 convolution_add_fusion.1
  241.3 0.2 fusion.15
  241.5 0.2 fusion.13
  241.8 0.9 pad_maximum_fusion.6
  243.2 0.2 fusion.27
  243.4 0.2 fusion.25
  243.8 0.6 gather_fusion.6
  244.4 0.9 select_bitcast_fusion.5
  245.4 1.6 copy.172
  247.0 8.0 %collective-permute-done.7 = f32[2,4,128,128]{2,3,1,0:T(8,128)} collective-permute-done((f32[2,4,128,128]{2,3,1,0:T(8,128)}, f32[2,4,128,128]{2,3,1,0:T(8,128)}, u32[]{:S(2)}, u32[]{:S(2)}) %collective-permute-start.7) | collective-permute-done | bytes 524320 | tf_op jit(solution)/shard_map/ppermute | solution.py:15
  255.1 1.1 broadcast_select_fusion.1
  256.2 0.6 gather_fusion.7
  256.9 8.5 %collective-permute-done.8 = f32[2,4,128,128]{2,3,1,0:T(8,128)} collective-permute-done((f32[2,4,128,128]{2,3,1,0:T(8,128)}, f32[2,4,128,128]{2,3,1,0:T(8,128)}, u32[]{:S(2)}, u32[]{:S(2)}) %collective-permute-start.8) | collective-permute-done | bytes 524320 | tf_op jit(solution)/shard_map/ppermute | solution.py:15
  265.4 1.6 gather_fusion.8
  267.6 1.3 copy.173
  (88 shorter events, 10.6 us)
Async XLA Ops:
  7.2 216.2 %all-reduce.2.cloned.1.call-start = ((), (), s32[]{:S(2)}) async-start(), calls=%async_computation | async-start | bytes 3145728 | tf_op jit(solution)/shard_map/psum | solution.py:150
  7.2 92.9 %collective-permute-start = (bf16[2,4,128,1024]{3,2,1,0:T(8,128)(2,1)}, bf16[2,4,128,1024]{3,2,1,0:T(8,128)(2,1)}, u32[]{:S(2)}, u32[]{:S(2)}) collective-permute-start(bf16[2,4,128,1024]{3,2,1,0:T(8,128)(2,1)} %param.10), channel_id=1, source_target_pairs={{0,12},{4,16},{8,20},{12,24},{16,28},{20,32},{24,36},{28,40},{32,4... | collective-permute-start | bytes 6291464 | tf_op jit(solution)/shard_map/ppermute | solution.py:15
  10.6 90.3 %collective-permute-start.1 = (bf16[2,4,128,1024]{3,2,1,0:T(8,128)(2,1)}, bf16[2,4,128,1024]{3,2,1,0:T(8,128)(2,1)}, u32[]{:S(2)}, u32[]{:S(2)}) collective-permute-start(bf16[2,4,128,1024]{3,2,1,0:T(8,128)(2,1)} %param.10), channel_id=1, source_target_pairs={{0,252},{4,0},{8,4},{12,8},{16,12},{20,16},{24,20},{28,24},{32,28}... | collective-permute-start | bytes 6291464 | tf_op jit(solution)/shard_map/ppermute | solution.py:15
  17.0 127.5 %collective-permute-start.2 = (bf16[2,4,128,1024]{3,2,1,0:T(8,128)(2,1)}, bf16[2,4,128,1024]{3,2,1,0:T(8,128)(2,1)}, u32[]{:S(2)}, u32[]{:S(2)}) collective-permute-start(bf16[2,4,128,1024]{3,2,1,0:T(8,128)(2,1)} %param.10), channel_id=1, source_target_pairs={{0,240},{4,244},{8,248},{12,252},{16,0},{20,4},{24,8},{28,12},{32,... | collective-permute-start | bytes 6291464 | tf_op jit(solution)/shard_map/ppermute | solution.py:15
  18.6 138.5 %collective-permute-start.3 = (bf16[2,4,128,128]{3,2,1,0:T(8,128)(2,1)}, bf16[2,4,128,128]{3,2,1,0:T(8,128)(2,1)S(1)}, u32[]{:S(2)}, u32[]{:S(2)}) collective-permute-start(bf16[2,4,128,128]{3,2,1,0:T(8,128)(2,1)} %param.11), channel_id=1, source_target_pairs={{0,12},{4,16},{8,20},{12,24},{16,28},{20,32},{24,36},{28,40},{32,4... | collective-permute-start | bytes 786440 | tf_op jit(solution)/shard_map/ppermute | solution.py:15
  18.6 138.5 %collective-permute-start.4 = (bf16[2,4,128,128]{3,2,1,0:T(8,128)(2,1)}, bf16[2,4,128,128]{3,2,1,0:T(8,128)(2,1)}, u32[]{:S(2)}, u32[]{:S(2)}) collective-permute-start(bf16[2,4,128,128]{3,2,1,0:T(8,128)(2,1)} %param.11), channel_id=1, source_target_pairs={{0,252},{4,0},{8,4},{12,8},{16,12},{20,16},{24,20},{28,24},{32,28}... | collective-permute-start | bytes 786440 | tf_op jit(solution)/shard_map/ppermute | solution.py:15
  27.4 1.6 copy-start.2
  30.7 69.4 %copy-start = (bf16[2,4,128,128]{3,2,1,0:T(8,128)(2,1)S(1)}, bf16[2,4,128,128]{3,2,1,0:T(8,128)(2,1)}, u32[]{:S(2)}) copy-start(bf16[2,4,128,128]{3,2,1,0:T(8,128)(2,1)} %param.11) | copy-start | bytes 786436
  100.2 58.6 %collective-permute-start.5 = (bf16[2,4,128,128]{3,2,1,0:T(8,128)(2,1)S(1)}, bf16[2,4,128,128]{3,2,1,0:T(8,128)(2,1)S(1)}, u32[]{:S(2)}, u32[]{:S(2)}) collective-permute-start(bf16[2,4,128,128]{3,2,1,0:T(8,128)(2,1)S(1)} %copy-done), channel_id=1, source_target_pairs={{0,240},{4,244},{8,248},{12,252},{16,0},{20,4},{24,8},{28,12},{32,... | collective-permute-start | bytes 786440 | tf_op jit(solution)/shard_map/ppermute | solution.py:15
  148.0 2.2 copy-start.3
  223.3 2.1 copy-start.1
  229.8 17.3 %collective-permute-start.6 = (f32[2,4,128,128]{2,3,1,0:T(8,128)}, f32[2,4,128,128]{2,3,1,0:T(8,128)}, u32[]{:S(2)}, u32[]{:S(2)}) collective-permute-start(f32[2,4,128,128]{2,3,1,0:T(8,128)} %get-tuple-element.39), channel_id=1, source_target_pairs={{0,244},{4,248},{8,252},{12,0},{16,4},{20,8},{24,12},{28,16},{32,2... | collective-permute-start | bytes 1572872 | tf_op jit(solution)/shard_map/ppermute | solution.py:15
  233.7 21.3 %collective-permute-start.7 = (f32[2,4,128,128]{2,3,1,0:T(8,128)}, f32[2,4,128,128]{2,3,1,0:T(8,128)}, u32[]{:S(2)}, u32[]{:S(2)}) collective-permute-start(f32[2,4,128,128]{2,3,1,0:T(8,128)} %get-tuple-element.39), channel_id=1, source_target_pairs={{0,4},{4,8},{8,12},{12,16},{16,20},{20,24},{24,28},{28,32},{32,36}... | collective-permute-start | bytes 1572872 | tf_op jit(solution)/shard_map/ppermute | solution.py:15
  242.7 22.8 %collective-permute-start.8 = (f32[2,4,128,128]{2,3,1,0:T(8,128)}, f32[2,4,128,128]{2,3,1,0:T(8,128)}, u32[]{:S(2)}, u32[]{:S(2)}) collective-permute-start(f32[2,4,128,128]{2,3,1,0:T(8,128)} %get-tuple-element.41), channel_id=1, source_target_pairs={{0,16},{4,20},{8,24},{12,28},{16,32},{20,36},{24,40},{28,44},{32,4... | collective-permute-start | bytes 1572872 | tf_op jit(solution)/shard_map/ppermute | solution.py:15
  256.2 11.0 %copy-start.4 = (f32[1,2,4,128,128]{3,4,1,2,0:T(8,128)S(1)}, f32[1,2,4,128,128]{3,4,1,2,0:T(8,128)}, u32[]{:S(2)}) copy-start(f32[1,2,4,128,128]{3,4,1,2,0:T(8,128)} %select_bitcast_fusion.5) | copy-start | bytes 1572868
Sparse Core Ops, SparseCore 0:
  156.5 66.8 all-reduce.1
where the time goes:
time: 277 us; the launch traced here: 276 us
  waiting for transfers between devices  188 us (68%)
  local copies, waits for them, and re-layouts  21.4 us (8%)
  starting transfers between devices  19.1 us (7%)
  matrix products  18.3 us (7%)
  between operations  14.8 us (5%)
  other arithmetic  14 us (5%)
    ppermute x9, waiting for transfers between devices, from_behind(): lax.ppermute(array, axis, [(i, (i + by) % size) for i in range(size)])  124 us
    psum x1, waiting for transfers between devices, shards(): summed = lax.psum((raw[0],), 'ga')  63.8 us
    ppermute x9, starting transfers between devices, from_behind(): lax.ppermute(array, axis, [(i, (i + by) % size) for i in range(size)])  19 us
    gather x3, local copies, waits for them, and re-layouts, shards(): source_orb = jnp.take(sources[direction][0], slots, axis=1)  8.12 us
    dot_general x12, matrix products, product(): jnp.einsum('kag,kbg->kab', first, second, preferred_element_type=jnp.floa...  6.97 us
  transfers between devices with their start and end apart: 10, of which 6 were waited for; matrix products, arithmetic and copies ran while one was open for 15% of the time, Pallas kernels for 0%

commit v1 on v0

v1 whole, which is shorter than its diff:
```python
import math

import jax
import jax.numpy as jnp
from jax import lax
from jax.experimental import pallas as pl
from jax.experimental.pallas import tpu as pltpu
from jax.sharding import PartitionSpec as P

KRING = 4
GY = 32
GZ = 32
F32 = jnp.float32
BF16 = jnp.bfloat16
CONTRACT_LAST = (((1,), (1,)), ((), ()))
CONTRACT_FIRST = (((0,), (0,)), ((), ()))


def grid_fractions(plane_first, plane_count, plane_total):
    point_index = jnp.arange(plane_count * GY * GZ, dtype=jnp.int32)
    plane = point_index // (GY * GZ) + plane_first
    middle = point_index // GZ % GY
    inner = point_index % GZ
    return [
        plane.astype(F32) / F32(plane_total),
        middle.astype(F32) / F32(GY),
        inner.astype(F32) / F32(GZ),
    ]


def phase_angles(shift_rows, direction, mesh_counts, fractions):
    total = jnp.zeros((shift_rows.shape[0], fractions[0].shape[0]), F32)
    for lattice in range(3):
        step = 1.0 / mesh_counts[lattice] if lattice == direction else 0.0
        wave = shift_rows[:, lattice].astype(F32) + F32(step)
        total = total + wave[:, None] * fractions[lattice][None, :]
    return F32(2.0 * math.pi) * total


def correlate_pair(own, source, twiddle, slot, k, phased):
    nb = own.shape[2]
    cosine = twiddle[0:1, :]
    sine = twiddle[1:2, :]
    source_re = source[0, slot].astype(F32)
    source_im = source[1, slot].astype(F32)
    phased[0:nb, :] = (cosine * source_re + sine * source_im).astype(BF16)
    phased[nb:, :] = (cosine * source_im - sine * source_re).astype(BF16)
    left = jnp.concatenate([own[0, k], own[1, k]], axis=0)
    full = lax.dot_general(left, phased[...], CONTRACT_LAST, preferred_element_type=F32)
    return full[:nb, :nb] + full[nb:, nb:], full[:nb, nb:] - full[nb:, :nb]


def correlate_own_body(meta, twiddle, orbitals, give, keep, own, phased, sem):
    copy = pltpu.make_async_copy(orbitals, own, sem)
    copy.start()
    copy.wait()
    for p in range(4):
        k = meta[1, p]
        out = give if p < 2 else keep
        out[p % 2, 0], out[p % 2, 1] = correlate_pair(own, own, twiddle.at[k], meta[0, p], k, phased.at[p % 2])


def correlate_own(meta, twiddle, orbitals):
    nb, points = orbitals.shape[2:]
    half = jax.ShapeDtypeStruct((2, 2, nb, nb), F32)
    vmem = pl.BlockSpec(memory_space=pltpu.VMEM)
    return pl.pallas_call(
        correlate_own_body,
        out_shape=(half, half, pltpu.VMEM(orbitals.shape, BF16)),
        in_specs=[pl.BlockSpec(memory_space=pltpu.SMEM), vmem, pl.BlockSpec(memory_space=pl.ANY)],
        out_specs=(vmem, vmem, vmem),
        scratch_shapes=[pltpu.VMEM((2, 2 * nb, points), BF16), pltpu.SemaphoreType.DMA],
        cost_estimate=pl.CostEstimate(flops=4 * 8 * nb * nb * points, bytes_accessed=2**22, transcendentals=0),
    )(meta, twiddle, orbitals)


def correlate_body(meta, twiddle_x, twiddle_y, own, beside, beyond, give, keep, source, phased, sems):
    copies = [pltpu.make_async_copy(a, source.at[n], sems.at[n]) for n, a in enumerate((beside, beyond))]
    for copy in copies:
        copy.start()
    for n, twiddle in enumerate((twiddle_x, twiddle_y)):
        copies[n].wait()
        for p in (n, 2 + n):
            k = meta[1, p]
            out = give if p < 2 else keep
            out[n, 0], out[n, 1] = correlate_pair(own, source.at[n], twiddle.at[k], meta[0, p], k, phased.at[p // 2])


def correlate(meta, twiddle_x, twiddle_y, own, beside, beyond):
    nb, points = own.shape[2:]
    half = jax.ShapeDtypeStruct((2, 2, nb, nb), F32)
    vmem = pl.BlockSpec(memory_space=pltpu.VMEM)
    hbm = pl.BlockSpec(memory_space=pl.ANY)
    return pl.pallas_call(
        correlate_body,
        out_shape=(half, half),
        in_specs=[pl.BlockSpec(memory_space=pltpu.SMEM), vmem, vmem, vmem, hbm, hbm],
        out_specs=(vmem, vmem),
        scratch_shapes=[
            pltpu.VMEM((2, *beside.shape), BF16),
            pltpu.VMEM((2, 2 * nb, points), BF16),
            pltpu.SemaphoreType.DMA((2,)),
        ],
        cost_estimate=pl.CostEstimate(flops=4 * 8 * nb * nb * points, bytes_accessed=2**22, transcendentals=0),
    )(meta, twiddle_x, twiddle_y, own, beside, beyond)


def split_parts(values):
    high = values.astype(BF16)
    low = (values - high.astype(F32)).astype(BF16)
    return high, low


def rotate_pair(raw_parts, left, right):
    nb = left[0].shape[0]
    raw_re, raw_im = [jnp.concatenate(split_parts(part), axis=1) for part in raw_parts]
    raw = jnp.concatenate([raw_re, raw_im], axis=0)
    wide = jnp.concatenate(right, axis=1)
    prod = jnp.dot(raw, jnp.concatenate([wide, wide], axis=0), preferred_element_type=F32)
    temp_re = prod[:nb, :nb] - prod[nb:, nb:]
    temp_im = prod[:nb, nb:] + prod[nb:, :nb]
    re_high, re_low = split_parts(temp_re)
    im_high, im_low = split_parts(temp_im)
    temp = jnp.concatenate(
        [jnp.concatenate([re_high, im_high], axis=1), jnp.concatenate([re_low, im_low], axis=1)], axis=0
    )
    tall = jnp.concatenate(left, axis=1)
    prod = lax.dot_general(
        jnp.concatenate([tall, tall], axis=0), temp, CONTRACT_FIRST, preferred_element_type=F32
    )
    return prod[:nb, :nb] + prod[nb:, nb:], prod[:nb, nb:] - prod[nb:, :nb]


def rotate(meta, mine, other, left, rights, right_of, layout):
    nb = left.shape[2]
    pairs = len(right_of)
    vmem = pl.BlockSpec(memory_space=pltpu.VMEM)

    def body(slots, mine, other, left, *refs):
        rights_in, outs = refs[: len(rights)], refs[len(rights) :]
        for p in range(pairs):
            k = slots[1, p]
            n = slots[2, p]
            right = rights_in[right_of[p]]
            out_re, out_im = rotate_pair(
                [mine[p, c] + other[p, c] for c in range(2)],
                [left[c, k] for c in range(2)],
                [right[c, n] for c in range(2)],
            )
            for out, rows in zip(outs, layout):
                for row, (pair, adjoint) in enumerate(rows):
                    if pair == p and adjoint:
                        out[row, 0] = out_re.T
                        out[row, 1] = -out_im.T
                    elif pair == p:
                        out[row, 0] = out_re
                        out[row, 1] = out_im

    return pl.pallas_call(
        body,
        out_shape=tuple(jax.ShapeDtypeStruct((len(rows), 2, nb, nb), F32) for rows in layout),
        in_specs=[pl.BlockSpec(memory_space=pltpu.SMEM)] + [vmem] * (3 + len(rights)),
        out_specs=(vmem,) * len(layout),
        cost_estimate=pl.CostEstimate(flops=pairs * 4 * 256**3, bytes_accessed=pairs * 2**19, transcendentals=0),
    )(meta, mine, other, left, *rights)


def place(targets, meta, blocks, outs):
    nb = blocks[0].shape[-1]
    shape = jax.ShapeDtypeStruct((3, 2, 4, nb, nb), F32)
    previous = () if outs is None else tuple(outs)
    vmem = pl.BlockSpec(memory_space=pltpu.VMEM)
    hbm = pl.BlockSpec(memory_space=pl.ANY)

    def body(slots, *refs):
        sems = refs[-1]
        into = refs[-3:-1]
        copies = []
        for block, rows in zip(refs, targets):
            for n, (output, direction, slot) in enumerate(rows):
                target = into[output].at[direction, :, slots[slot]]
                copies.append(pltpu.make_async_copy(block.at[n], target, sems.at[len(copies)]))
        for copy in copies:
            copy.start()
        for copy in copies:
            copy.wait()

    count = len(blocks)
    total = sum(len(rows) for rows in targets)
    return pl.pallas_call(
        body,
        out_shape=(shape, shape),
        in_specs=[pl.BlockSpec(memory_space=pltpu.SMEM)] + [vmem] * count + [hbm] * len(previous),
        out_specs=(hbm, hbm),
        scratch_shapes=[pltpu.SemaphoreType.DMA((total,))],
        input_output_aliases={1 + count: 0, 2 + count: 1} if previous else {},
        cost_estimate=pl.CostEstimate(flops=0, bytes_accessed=total * 2**18, transcendentals=0),
    )(meta, *blocks, *previous)


def shards(orbitals, gauge, neighbour, wrap_shift):
    kloc = orbitals.shape[1]
    nb = orbitals.shape[2]
    grid_points = orbitals.shape[3]
    ka_count = lax.axis_size("ka")
    ga_count = lax.axis_size("ga")
    device = lax.axis_index("ka")
    grid_part = lax.axis_index("ga")
    core = grid_part % 2
    plane_count = grid_points // (GY * GZ)
    counts = (kloc, KRING, ka_count // KRING)

    ring_back = [(d, d // KRING * KRING + (d - 1) % KRING) for d in range(ka_count)]
    outer_back = [(d, (d - KRING) % ka_count) for d in range(ka_count)]
    ring_ahead = [(t, s) for s, t in ring_back]
    outer_ahead = [(t, s) for s, t in outer_back]
    sibling = [(g, g ^ 1) for g in range(ga_count)]
    ring_ahead_sibling = [
        (s * ga_count + g, t * ga_count + (g ^ 1)) for s, t in ring_ahead for g in range(ga_count)
    ]
    across = [(g, g ^ 2) for g in range(ga_count)]

    gauge_half = lax.dynamic_index_in_dim(gauge.reshape(2, 2, 2, nb, nb), core, 2, keepdims=False)
    gauge_beside = lax.ppermute(gauge_half, "ka", ring_back)
    gauge_beyond = lax.ppermute(gauge_half, "ka", outer_back)
    front = orbitals[:, :2]
    rear = orbitals[:, 2:]
    beyond_front = lax.ppermute(front, "ka", outer_back)
    beside_front = lax.ppermute(front, "ka", ring_back)
    beyond_rear = lax.ppermute(rear, "ka", outer_back)
    beside_rear = lax.ppermute(rear, "ka", ring_back)

    fractions = grid_fractions(grid_part * plane_count, plane_count, plane_count * ga_count)
    my_table = lax.dynamic_slice_in_dim(neighbour, device * kloc, kloc, 0) % kloc
    my_shift = lax.dynamic_slice_in_dim(wrap_shift, device * kloc, kloc, 0)
    slots = jnp.arange(kloc, dtype=jnp.int32)
    local = jnp.stack([1 - core, 1 - core, core, core]).astype(jnp.int32)

    def k_slots(direction, wanted):
        match = my_table[:, direction][:, None] == wanted[None, :]
        return jnp.sum(jnp.where(match, slots[:, None], 0), axis=0)

    pair_is_first = slots % 2 == 0
    order = local + jnp.where(pair_is_first, 0, 2)
    meta_own = jnp.stack([order, k_slots(0, order), order, order])

    def meta_of(part):
        wanted = local + 2 * part
        k = jnp.where(pair_is_first, k_slots(1, wanted), k_slots(2, wanted))
        return jnp.stack([local, k, jnp.full((kloc,), part, jnp.int32), wanted])

    angles = [phase_angles(my_shift[:, b, :], b, counts, fractions) for b in range(3)]
    twiddles = [jnp.stack([jnp.cos(a), jnp.sin(a)], axis=1) for a in angles]

    def gather_sum(give, keep):
        return keep + lax.ppermute(give, "ga", sibling)

    give, keep, own = correlate_own(meta_own, twiddles[0], orbitals)
    got = lax.ppermute(give, "ga", sibling)
    meta_front, meta_rear = meta_of(0), meta_of(1)
    give_front, keep_front = correlate(meta_front, twiddles[1], twiddles[2], own, beside_front, beyond_front)
    got_front = lax.ppermute(give_front, "ga", sibling)
    chip = jnp.concatenate([keep + got, keep_front + got_front], axis=0)
    other = lax.ppermute(chip, "ga", across)

    chip, beside_rear, beyond_rear = lax.optimization_barrier((chip, beside_rear, beyond_rear))
    give, keep = correlate(meta_rear, twiddles[1], twiddles[2], own, beside_rear, beyond_rear)
    chip_rear = keep + lax.ppermute(give, "ga", sibling)
    other_rear = lax.ppermute(chip_rear, "ga", across)

    other, chip_rear = lax.optimization_barrier((other, chip_rear))
    meta_first = jnp.concatenate([meta_own[:, 2:], meta_front[:, 2:]], axis=1)
    first, adj_x, adj_y = rotate(
        meta_first, chip, other, gauge, (gauge, gauge_beside, gauge_beyond), (0, 0, 1, 2),
        [[(0, 0), (1, 0), (2, 0), (3, 0), (0, 1), (1, 1)], [(2, 1)], [(3, 1)]],
    )

    def deliver(fwd, adj_x, adj_y):
        adj_y = lax.ppermute(adj_y, "ka", outer_ahead)
        adj_x, adj_x_sib = lax.ppermute(adj_x, "ka", ring_ahead), lax.ppermute(adj_x, ("ka", "ga"), ring_ahead_sibling)
        fwd_sib = lax.ppermute(fwd, "ga", sibling)
        return fwd, fwd_sib, adj_x, adj_x_sib, adj_y, lax.ppermute(adj_y, "ga", sibling)

    blocks = deliver(first, adj_x, adj_y)
    meta_second = meta_rear[:, 2:]
    last, adj_x, adj_y = rotate(
        meta_second, chip_rear, other_rear, gauge, (gauge_beside, gauge_beyond), (0, 1),
        [[(0, 0), (1, 0)], [(0, 1)], [(1, 1)]],
    )
    last, *blocks = lax.optimization_barrier((last, *blocks))
    blocks_rear = deliver(last, adj_x, adj_y)

    k_own, k_front, k_rear = meta_own[1], meta_front[1], meta_rear[1]
    s_own, s_front, s_rear = meta_own[3], meta_front[3], meta_rear[3]
    where = jnp.concatenate([k_own, s_own, k_front, s_front])
    targets = []
    for base in (2, 0):
        targets.append(
            [(0, 0, base), (0, 0, base + 1), (0, 1, base + 8), (0, 2, base + 9), (1, 0, base + 4), (1, 0, base + 5)]
        )
    targets += [[(1, 1, 14)], [(1, 1, 12)], [(1, 2, 15)], [(1, 2, 13)]]
    outs = place(targets, where, blocks, None)
    where = jnp.concatenate([k_rear, s_rear])
    targets = [[(0, 1, 2), (0, 2, 3)], [(0, 1, 0), (0, 2, 1)], [(1, 1, 6)], [(1, 1, 4)], [(1, 2, 7)], [(1, 2, 5)]]
    return tuple(place(targets, where, blocks_rear, outs))


def solution(mesh):
    in_specs = (P(None, "ka", None, "ga"), P(None, "ka", None, None), P(), P())
    out_specs = (P(None, None, "ka", None, None), P(None, None, "ka", None, None))
    return jax.shard_map(shards, mesh=mesh, in_specs=in_specs, out_specs=out_specs, check_vma=False)
```

time: 277 us -> 110 us (0.40)
  waiting for transfers between devices: 188 us -> 32.6 us
  Pallas kernels: 0 us -> 24.4 us
  matrix products: 18.3 us -> 0 us
  starting transfers between devices: 19.1 us -> 33.3 us
  between operations: 14.8 us -> 1.17 us
  local copies, waits for them, and re-layouts: 21.4 us -> 9.52 us
  other arithmetic: 14 us -> 8.22 us
    ppermute x9 -> x21, waiting for transfers between devices: 124 us -> 32.6 us  [the longest x2 7.2 us: deliver(): adj_y = lax.ppermute(adj_y, 'ka', outer_ahead)]
    psum x1 -> x0, waiting for transfers between devices: 63.8 us -> none  [shards(): summed = lax.psum((raw[0],), 'ga')]
    pallas_call x0 -> x7, Pallas kernels: none -> 24.4 us  [the longest x2 9.63 us: correlate(): pl.pallas_call(correlate_body, out_shape=(half, half), in_specs=[pl.Block...]
    dot_general x60 -> x0, matrix products: 18.3 us -> none  [the longest x12 6.97 us: product(): jnp.einsum('kag,kbg->kab', first, second, preferred_element_type=jnp.floa...]
    ppermute x9 -> x21, starting transfers between devices: 19 us -> 33.3 us  [the longest x1 6.59 us: shards(): beyond_front = lax.ppermute(front, 'ka', outer_back)]
    gather x9 -> x0, local copies, waits for them, and re-layouts: 12.7 us -> none  [the longest x3 8.12 us: shards(): source_orb = jnp.take(sources[direction][0], slots, axis=1)]
    select_n x10 -> x5, other arithmetic: 7.89 us -> 0.1 us  [the longest x1 0.08 us: shards(): lax.dynamic_slice_in_dim(neighbour, device * kloc, kloc, 0) % kloc]
  transfers between devices with their start and end apart: 10 -> 21, of which waited for: 6 -> 10; matrix products, arithmetic and copies ran while one was open for 15% -> 10% of each run, Pallas kernels for 0% -> 18%
where the time goes in v1:
time: 110 us; the launch traced here: 109 us
  starting transfers between devices  33.3 us (30%)
  waiting for transfers between devices  32.6 us (30%)
  Pallas kernels  24.4 us (22%)
  local copies, waits for them, and re-layouts  9.52 us (9%)
  other arithmetic  8.22 us (7%)
  between operations  1.17 us (1%)
    pallas_call x2, Pallas kernels, correlate(): pl.pallas_call(correlate_body, out_shape=(half, half), in_specs=[pl.Block...  9.63 us
    ppermute x2, waiting for transfers between devices, deliver(): adj_y = lax.ppermute(adj_y, 'ka', outer_ahead)  7.2 us
    ppermute x1, starting transfers between devices, shards(): beyond_front = lax.ppermute(front, 'ka', outer_back)  6.59 us
    ppermute x1, waiting for transfers between devices, shards(): beyond_rear = lax.ppermute(rear, 'ka', outer_back)  6.31 us
    ppermute x1, waiting for transfers between devices, shards(): beyond_front = lax.ppermute(front, 'ka', outer_back)  6.27 us
    pallas_call x2, Pallas kernels, rotate(): pl.pallas_call(body, out_shape=tuple((jax.ShapeDtypeStruct((len(rows), 2,...  5.51 us
    ppermute x1, waiting for transfers between devices, shards(): other_rear = lax.ppermute(chip_rear, 'ga', across)  5.51 us
    pallas_call x2, Pallas kernels, place(): pl.pallas_call(body, out_shape=(shape, shape), in_specs=[pl.BlockSpec(mem...  5.19 us
  transfers between devices with their start and end apart: 21, of which 10 were waited for; matrix products, arithmetic and copies ran while one was open for 10% of the time, Pallas kernels for 18%

profile of v1, /device:TPU:1, one launch (start us, length us, event | category | flops | bytes accessed | tf_op | source)
XLA Modules:
  0.0 109.3 jit_solution(12526589611609554165)
XLA Ops:
  0.6 2.8 %fusion.27 = (bf16[2,2,128,1024]{3,2,1,0:T(8,128)(2,1)S(1)}, bf16[2,2,128,1024]{3,2,1,0:T(8,128)(2,1)}) fusion(bf16[2,4,128,1024]{3,2,1,0:T(8,128)(2,1)} %orbitals.1), kind=kLoop, calls=%fused_computation.84 | loop fusion | bytes 4194304 | tf_op jit(solution)/shard_map/slice | solution.py:227
  3.4 3.3 %collective-permute-start.1 = (bf16[2,2,128,1024]{3,2,1,0:T(8,128)(2,1)}, bf16[2,2,128,1024]{3,2,1,0:T(8,128)(2,1)}, u32[]{:S(2)}, u32[]{:S(2)}) collective-permute-start(bf16[2,2,128,1024]{3,2,1,0:T(8,128)(2,1)} %get-tuple-element.80), channel_id=1, source_target_pairs={{0,12},{4,0},{8,4},{12,8},{16,28},{20,16},{24,20},{28,24},{32,44},... | collective-permute-start | bytes 3145736 | tf_op jit(solution)/shard_map/ppermute | solution.py:229
  6.7 6.6 %collective-permute-start.2 = (bf16[2,2,128,1024]{3,2,1,0:T(8,128)(2,1)}, bf16[2,2,128,1024]{3,2,1,0:T(8,128)(2,1)}, u32[]{:S(2)}, u32[]{:S(2)}) collective-permute-start(bf16[2,2,128,1024]{3,2,1,0:T(8,128)(2,1)} %get-tuple-element.80), channel_id=1, source_target_pairs={{0,240},{4,244},{8,248},{12,252},{16,0},{20,4},{24,8},{28,12},{32,... | collective-permute-start | bytes 3145736 | tf_op jit(solution)/shard_map/ppermute | solution.py:228
  13.3 0.5 collective-permute-start.5
  13.9 0.2 collective-permute-start.6
  14.1 0.1 constant_dynamic-slice_fusion.1
  14.2 0.1 copy.20
  14.2 0.2 convert_reduce_fusion.5
  14.5 0.1 copy.24
  14.6 0.2 convert_reduce_fusion
  14.8 0.1 copy.22
  14.9 0.2 add_reduce_fusion.1
  15.1 1.4 %fusion.24 = (f32[4,1,1024]{2,1,0:T(1,128)S(1)}, f32[4,1,1024]{2,1,0:T(1,128)S(1)}, f32[4,1,1024]{2,1,0:T(1,128)S(1)}, f32[4,1,1024]{2,1,0:T(1,128)S(1)}, f32[4,...) fusion(f32[1024]{0:T(1024)S(1)} %fusion.11, f32[4]{0:T(128)S(1)} %get-tuple-element.57, f32[1024]{0:T(1024)S(1)} %fusion.9, ...), kind=kLoop, calls=%fused_computation.81 | loop fusion | flops 73728 | bytes 110736 | tf_op jit(solution)/shard_map/cos | solution.py:253
  16.6 0.4 sin.30
  17.1 0.1 add_select_fusion.4
  17.2 0.6 pad_maximum_fusion.1.twiddle
  17.9 0.1 select_reduce_fusion.1
  18.0 0.6 pad_add_fusion.2.meta
  18.6 4.1 %shard_map.59 = (f32[2,2,128,128]{3,2,1,0:T(8,128)}, f32[2,2,128,128]{3,2,1,0:T(8,128)}, bf16[2,4,128,1024]{3,2,1,0:T(8,128)(2,1)S(1)}) custom-call(s32[4,4]{1,0:T(4,128)} %pad_add_fusion.2.meta, f32[4,2,1024]{2,1,0:T(2,128)} %pad_maximum_fusion.1.twiddle, bf16[2,4,128,1024]{3,2,1,0:T(8,128)(2,1)} %orbitals.1), custom_call_target="tpu_custom_call" | custom-call | flops 536870912 | bytes 4194304 | tf_op jit(solution)/shard_map/pallas_call | solution.py:67
  22.7 1.3 %copy-done = bf16[2,4,128,1024]{3,2,1,0:T(8,128)(2,1)} copy-done((bf16[2,4,128,1024]{3,2,1,0:T(8,128)(2,1)}, bf16[2,4,128,1024]{3,2,1,0:T(8,128)(2,1)S(1)}, u32[]{:S(2)}) %copy-start) | copy-done | bytes 2097176
  24.1 1.8 %collective-permute-start = (f32[2,2,128,128]{3,2,1,0:T(8,128)}, f32[2,2,128,128]{3,2,1,0:T(8,128)S(1)}, u32[]{:S(2)}, u32[]{:S(2)}) collective-permute-start(f32[2,2,128,128]{3,2,1,0:T(8,128)} %get-tuple-element.30), channel_id=1, source_target_pairs={{0,1},{1,0},{2,3},{3,2},{4,5},{5,4},{6,7},{7,6},{8,9},{9,8},{10,11... | collective-permute-start | bytes 786440 | tf_op jit(solution)/shard_map/ppermute | solution.py:259
  25.8 0.4 sin.31
  26.3 0.4 sin.32
  26.8 0.6 fusion.18
  27.4 0.7 pad_maximum_fusion.2
  28.1 0.8 collective-permute-done.1.beside
  28.9 6.3 %collective-permute-done.2.beyond = bf16[2,2,128,1024]{3,2,1,0:T(8,128)(2,1)} collective-permute-done((bf16[2,2,128,1024]{3,2,1,0:T(8,128)(2,1)}, bf16[2,2,128,1024]{3,2,1,0:T(8,128)(2,1)}, u32[]{:S(2)}, u32[]{:S(2)}) %collective-permute-start.2) | collective-permute-done | bytes 1048608 | tf_op jit(solution)/shard_map/ppermute | solution.py:228
  35.1 4.8 %shard_map.60 = (f32[2,2,128,128]{3,2,1,0:T(8,128)}, f32[2,2,128,128]{3,2,1,0:T(8,128)}) custom-call(s32[4,4]{1,0:T(4,128)} %get-tuple-element.91.meta, f32[4,2,1024]{2,1,0:T(2,128)} %get-tuple-element.94.twiddle_x, f32[4,2,1024]{2,1,0:T(2,128)} %get-tuple-element.95.twiddle_y, bf16[2,4,128,1024]{3,2,1,0:T(8,128)(2,1)} %copy-done, ...), custom_call_target="tpu_custom_call" | custom-call | flops 536870912 | bytes 4194304 | tf_op jit(solution)/shard_map/pallas_call | solution.py:94
  40.0 3.4 %collective-permute-start.3 = (f32[2,2,128,128]{3,2,1,0:T(8,128)}, f32[2,2,128,128]{3,2,1,0:T(8,128)S(1)}, u32[]{:S(2)}, u32[]{:S(2)}) collective-permute-start(f32[2,2,128,128]{3,2,1,0:T(8,128)} %get-tuple-element.33), channel_id=1, source_target_pairs={{0,1},{1,0},{2,3},{3,2},{4,5},{5,4},{6,7},{7,6},{8,9},{9,8},{10,11... | collective-permute-start | bytes 786440 | tf_op jit(solution)/shard_map/ppermute | solution.py:262
  43.4 1.3 %collective-permute-done.3 = f32[2,2,128,128]{3,2,1,0:T(8,128)S(1)} collective-permute-done((f32[2,2,128,128]{3,2,1,0:T(8,128)}, f32[2,2,128,128]{3,2,1,0:T(8,128)S(1)}, u32[]{:S(2)}, u32[]{:S(2)}) %collective-permute-start.3) | collective-permute-done | bytes 262176 | tf_op jit(solution)/shard_map/ppermute | solution.py:262
  44.7 1.0 add.259
  45.8 2.7 %collective-permute-start.4 = (f32[4,2,128,128]{3,2,1,0:T(8,128)S(1)}, f32[4,2,128,128]{3,2,1,0:T(8,128)S(1)}, u32[]{:S(2)}, u32[]{:S(2)}) collective-permute-start(f32[4,2,128,128]{3,2,1,0:T(8,128)S(1)} %pad_maximum_fusion.mine), channel_id=1, source_target_pairs={{0,2},{1,3},{2,0},{3,1},{4,6},{5,7},{6,4},{7,5},{8,10},{9,11},{10,... | collective-permute-start | bytes 1572872 | tf_op jit(solution)/shard_map/ppermute | solution.py:264
  48.5 2.7 %collective-permute-done.5.beside = bf16[2,2,128,1024]{3,2,1,0:T(8,128)(2,1)} collective-permute-done((bf16[2,2,128,1024]{3,2,1,0:T(8,128)(2,1)S(1)}, bf16[2,2,128,1024]{3,2,1,0:T(8,128)(2,1)}, u32[]{:S(2)}, u32[]{:S(2)}) %collective-permute-start.5) | collective-permute-done | bytes 1048608 | tf_op jit(solution)/shard_map/ppermute | solution.py:231
  51.2 6.3 %collective-permute-done.6.beyond = bf16[2,2,128,1024]{3,2,1,0:T(8,128)(2,1)} collective-permute-done((bf16[2,2,128,1024]{3,2,1,0:T(8,128)(2,1)S(1)}, bf16[2,2,128,1024]{3,2,1,0:T(8,128)(2,1)}, u32[]{:S(2)}, u32[]{:S(2)}) %collective-permute-start.6) | collective-permute-done | bytes 1048608 | tf_op jit(solution)/shard_map/ppermute | solution.py:230
  57.6 4.8 %shard_map.61 = (f32[2,2,128,128]{3,2,1,0:T(8,128)}, f32[2,2,128,128]{3,2,1,0:T(8,128)}) custom-call(s32[4,4]{1,0:T(4,128)} %get-tuple-element.92.meta, f32[4,2,1024]{2,1,0:T(2,128)} %get-tuple-element.94.twiddle_x, f32[4,2,1024]{2,1,0:T(2,128)} %get-tuple-element.95.twiddle_y, bf16[2,4,128,1024]{3,2,1,0:T(8,128)(2,1)} %copy-done, ...), custom_call_target="tpu_custom_call" | custom-call | flops 536870912 | bytes 4194304 | tf_op jit(solution)/shard_map/pallas_call | solution.py:94
  62.4 2.1 %collective-permute-start.7 = (f32[2,2,128,128]{3,2,1,0:T(8,128)}, f32[2,2,128,128]{3,2,1,0:T(8,128)S(1)}, u32[]{:S(2)}, u32[]{:S(2)}) collective-permute-start(f32[2,2,128,128]{3,2,1,0:T(8,128)} %get-tuple-element.37), channel_id=1, source_target_pairs={{0,1},{1,0},{2,3},{3,2},{4,5},{5,4},{6,7},{7,6},{8,9},{9,8},{10,11... | collective-permute-start | bytes 786440 | tf_op jit(solution)/shard_map/ppermute | solution.py:268
  64.6 4.6 %collective-permute-start.10 = (bf16[2,2,128,128]{3,2,1,0:T(8,128)(2,1)S(1)}, bf16[2,2,128,128]{3,2,1,0:T(8,128)(2,1)S(1)}, u32[]{:S(2)}, u32[]{:S(2)}) collective-permute-start(bf16[2,2,128,128]{3,2,1,0:T(8,128)(2,1)S(1)} %dynamic-slice_bitcast_fusion), channel_id=1, source_target_pairs={{0,240},{4,244},{8,248},{12,252},{16,0},{20,4},{24,8},{28,12},{32,... | collective-permute-start | bytes 393224 | tf_op jit(solution)/shard_map/ppermute | solution.py:225
  69.1 0.5 collective-permute-start.9
  69.8 0.6 pad_add_fusion.3.slots
  70.4 1.0 add.260.mine
  71.4 0.5 collective-permute-done.4.other
  71.9 0.1 collective-permute-done.10.refs_1_.refs_2_
  72.0 1.8 %collective-permute-done.9.refs_0_.refs_1_ = bf16[2,2,128,128]{3,2,1,0:T(8,128)(2,1)S(1)} collective-permute-done((bf16[2,2,128,128]{3,2,1,0:T(8,128)(2,1)S(1)}, bf16[2,2,128,128]{3,2,1,0:T(8,128)(2,1)S(1)}, u32[]{:S(2)}, u32[]{:S(2)}) %collective-permute-start.9) | collective-permute-done | bytes 131104 | tf_op jit(solution)/shard_map/ppermute | solution.py:224
  73.9 0.6 copy-done.7
  74.5 3.0 %shard_map.63 = (f32[6,2,128,128]{3,2,1,0:T(8,128)}, f32[1,2,128,128]{3,2,1,0:T(8,128)}, f32[1,2,128,128]{3,2,1,0:T(8,128)}) custom-call(s32[4,4]{1,0:T(4,128)} %pad_add_fusion.3.slots, f32[4,2,128,128]{3,2,1,0:T(8,128)} %copy-done.2, f32[4,2,128,128]{3,2,1,0:T(8,128)} %copy-done.5, bf16[2,4,128,128]{3,2,1,0:T(8,128)(2,1)} %refs_0_.1, ...), custom_call_target="tpu_custom_call" | custom-call | flops 268435456 | bytes 2097152 | tf_op jit(solution)/shard_map/pallas_call | solution.py:159
  77.6 1.1 %collective-permute-start.11 = (f32[6,2,128,128]{3,2,1,0:T(8,128)}, f32[6,2,128,128]{3,2,1,0:T(8,128)S(1)}, u32[]{:S(2)}, u32[]{:S(2)}) collective-permute-start(f32[6,2,128,128]{3,2,1,0:T(8,128)} %get-tuple-element.48.refs_0_), channel_id=1, source_target_pairs={{0,1},{1,0},{2,3},{3,2},{4,5},{5,4},{6,7},{7,6},{8,9},{9,8},{10,11... | collective-permute-start | bytes 2359304 | tf_op jit(solution)/shard_map/ppermute | solution.py:281
  78.7 2.6 %collective-permute-start.8 = (f32[2,2,128,128]{3,2,1,0:T(8,128)S(1)}, f32[2,2,128,128]{3,2,1,0:T(8,128)S(1)}, u32[]{:S(2)}, u32[]{:S(2)}) collective-permute-start(f32[2,2,128,128]{3,2,1,0:T(8,128)S(1)} %add.260.mine), channel_id=1, source_target_pairs={{0,2},{1,3},{2,0},{3,1},{4,6},{5,7},{6,4},{7,5},{8,10},{9,11},{10,... | collective-permute-start | bytes 786440 | tf_op jit(solution)/shard_map/ppermute | solution.py:269
  81.3 0.7 slice.64.slots
  82.0 0.6 collective-permute-start.13
  82.6 5.5 %collective-permute-done.8.other = f32[2,2,128,128]{3,2,1,0:T(8,128)S(1)} collective-permute-done((f32[2,2,128,128]{3,2,1,0:T(8,128)S(1)}, f32[2,2,128,128]{3,2,1,0:T(8,128)S(1)}, u32[]{:S(2)}, u32[]{:S(2)}) %collective-permute-start.8) | collective-permute-done | bytes 262176 | tf_op jit(solution)/shard_map/ppermute | solution.py:269
  88.1 0.7 copy-done.10
  88.8 2.5 %shard_map.62 = (f32[2,2,128,128]{3,2,1,0:T(8,128)}, f32[1,2,128,128]{3,2,1,0:T(8,128)}, f32[1,2,128,128]{3,2,1,0:T(8,128)}) custom-call(s32[4,2]{1,0:T(4,128)} %slice.64.slots, f32[2,2,128,128]{3,2,1,0:T(8,128)} %copy-done.3, f32[2,2,128,128]{3,2,1,0:T(8,128)} %copy-done.10, bf16[2,4,128,128]{3,2,1,0:T(8,128)(2,1)} %refs_0_.1, ...), custom_call_target="tpu_custom_call" | custom-call | flops 134217728 | bytes 1048576 | tf_op jit(solution)/shard_map/pallas_call | solution.py:159
  91.4 1.3 %collective-permute-start.15 = (f32[1,2,128,128]{3,2,1,0:T(8,128)S(1)}, f32[1,2,128,128]{3,2,1,0:T(8,128)S(1)}, u32[]{:S(2)}, u32[]{:S(2)}) collective-permute-start(f32[1,2,128,128]{3,2,1,0:T(8,128)S(1)} %collective-permute-done.14.refs_4_), channel_id=1, source_target_pairs={{0,1},{1,0},{2,3},{3,2},{4,5},{5,4},{6,7},{7,6},{8,9},{9,8},{10,11... | collective-permute-start | bytes 393224 | tf_op jit(solution)/shard_map/ppermute | solution.py:282
  92.6 0.1 collective-permute-start.17
  92.7 0.4 collective-permute-start.18
  93.1 7.2 %collective-permute-done.19.refs_4_ = f32[1,2,128,128]{3,2,1,0:T(8,128)S(1)} collective-permute-done((f32[1,2,128,128]{3,2,1,0:T(8,128)}, f32[1,2,128,128]{3,2,1,0:T(8,128)S(1)}, u32[]{:S(2)}, u32[]{:S(2)}) %collective-permute-start.19) | collective-permute-done | bytes 131104 | tf_op jit(solution)/shard_map/ppermute | solution.py:279
  100.3 1.4 %collective-permute-start.20 = (f32[1,2,128,128]{3,2,1,0:T(8,128)S(1)}, f32[1,2,128,128]{3,2,1,0:T(8,128)S(1)}, u32[]{:S(2)}, u32[]{:S(2)}) collective-permute-start(f32[1,2,128,128]{3,2,1,0:T(8,128)S(1)} %collective-permute-done.19.refs_4_), channel_id=1, source_target_pairs={{0,1},{1,0},{2,3},{3,2},{4,5},{5,4},{6,7},{7,6},{8,9},{9,8},{10,11... | collective-permute-start | bytes 393224 | tf_op jit(solution)/shard_map/ppermute | solution.py:282
  101.7 0.1 collective-permute-start.16
  101.8 0.8 concatenate.32.slots
  102.6 0.6 pad_add_fusion.5.slots
  103.1 2.9 %shard_map.64 = (f32[3,2,4,128,128]{4,3,2,1,0:T(8,128)}, f32[3,2,4,128,128]{4,3,2,1,0:T(8,128)}) custom-call(s32[16]{0:T(128)} %concatenate.32.slots, f32[6,2,128,128]{3,2,1,0:T(8,128)} %get-tuple-element.48.refs_0_, f32[6,2,128,128]{3,2,1,0:T(8,128)} %copy-done.4, f32[1,2,128,128]{3,2,1,0:T(8,128)} %copy-done.13, f32[1,2,128,128]{3,2,1,0:T(8,128)} %copy-done.14, ...), custom_call_target="tpu_custom_call" | custom-call | bytes 4194304 | tf_op jit(solution)/shard_map/pallas_call | solution.py:190
  106.2 0.6 copy-done.15
  106.8 0.1 copy-done.9
  106.9 2.2 %shard_map.65 = (f32[3,2,4,128,128]{4,3,2,1,0:T(8,128)}, f32[3,2,4,128,128]{4,3,2,1,0:T(8,128)}) custom-call(s32[8]{0:T(128)} %pad_add_fusion.5.slots, f32[2,2,128,128]{3,2,1,0:T(8,128)} %get-tuple-element.45.refs_0_, f32[2,2,128,128]{3,2,1,0:T(8,128)} %copy-done.9, f32[1,2,128,128]{3,2,1,0:T(8,128)} %copy-done.15, ...), custom_call_target="tpu_custom_call", output_to_operand_aliasing={{0}: (7, {}), {1}: (8, {})} | custom-call | bytes 2097152 | tf_op jit(solution)/shard_map/pallas_call | solution.py:190
  (76 shorter events, 0.6 us)
Async XLA Ops:
  0.6 13.4 %copy-start.22 = (s32[256,3,3]{0,2,1:T(4,128)S(1)}, s32[256,3,3]{0,2,1:T(4,128)}, u32[]{:S(2)}) copy-start(s32[256,3,3]{0,2,1:T(4,128)} %param.7) | copy-start | bytes 27652
  0.6 16.5 %copy-start.23 = (s32[256,3]{0,1:T(4,128)S(1)}, s32[256,3]{0,1:T(4,128)}, u32[]{:S(2)}) copy-start(s32[256,3]{0,1:T(4,128)} %param.6) | copy-start | bytes 9220
  3.4 25.5 %collective-permute-start.1 = (bf16[2,2,128,1024]{3,2,1,0:T(8,128)(2,1)}, bf16[2,2,128,1024]{3,2,1,0:T(8,128)(2,1)}, u32[]{:S(2)}, u32[]{:S(2)}) collective-permute-start(bf16[2,2,128,1024]{3,2,1,0:T(8,128)(2,1)} %get-tuple-element.80), channel_id=1, source_target_pairs={{0,12},{4,0},{8,4},{12,8},{16,28},{20,16},{24,20},{28,24},{32,44},... | collective-permute-start | bytes 3145736 | tf_op jit(solution)/shard_map/ppermute | solution.py:229
  6.7 28.4 %collective-permute-start.2 = (bf16[2,2,128,1024]{3,2,1,0:T(8,128)(2,1)}, bf16[2,2,128,1024]{3,2,1,0:T(8,128)(2,1)}, u32[]{:S(2)}, u32[]{:S(2)}) collective-permute-start(bf16[2,2,128,1024]{3,2,1,0:T(8,128)(2,1)} %get-tuple-element.80), channel_id=1, source_target_pairs={{0,240},{4,244},{8,248},{12,252},{16,0},{20,4},{24,8},{28,12},{32,... | collective-permute-start | bytes 3145736 | tf_op jit(solution)/shard_map/ppermute | solution.py:228
  13.3 37.9 %collective-permute-start.5 = (bf16[2,2,128,1024]{3,2,1,0:T(8,128)(2,1)S(1)}, bf16[2,2,128,1024]{3,2,1,0:T(8,128)(2,1)}, u32[]{:S(2)}, u32[]{:S(2)}) collective-permute-start(bf16[2,2,128,1024]{3,2,1,0:T(8,128)(2,1)S(1)} %get-tuple-element.79), channel_id=1, source_target_pairs={{0,12},{4,0},{8,4},{12,8},{16,28},{20,16},{24,20},{28,24},{32,44},... | collective-permute-start | bytes 3145736 | tf_op jit(solution)/shard_map/ppermute | solution.py:231
  13.9 43.7 %collective-permute-start.6 = (bf16[2,2,128,1024]{3,2,1,0:T(8,128)(2,1)S(1)}, bf16[2,2,128,1024]{3,2,1,0:T(8,128)(2,1)}, u32[]{:S(2)}, u32[]{:S(2)}) collective-permute-start(bf16[2,2,128,1024]{3,2,1,0:T(8,128)(2,1)S(1)} %get-tuple-element.79), channel_id=1, source_target_pairs={{0,240},{4,244},{8,248},{12,252},{16,0},{20,4},{24,8},{28,12},{32,... | collective-permute-start | bytes 3145736 | tf_op jit(solution)/shard_map/ppermute | solution.py:230
  22.7 1.3 %copy-start = (bf16[2,4,128,1024]{3,2,1,0:T(8,128)(2,1)}, bf16[2,4,128,1024]{3,2,1,0:T(8,128)(2,1)S(1)}, u32[]{:S(2)}) copy-start(bf16[2,4,128,1024]{3,2,1,0:T(8,128)(2,1)S(1)} %get-tuple-element.31.own) | copy-start | bytes 6291460
  24.1 19.3 %collective-permute-start = (f32[2,2,128,128]{3,2,1,0:T(8,128)}, f32[2,2,128,128]{3,2,1,0:T(8,128)S(1)}, u32[]{:S(2)}, u32[]{:S(2)}) collective-permute-start(f32[2,2,128,128]{3,2,1,0:T(8,128)} %get-tuple-element.30), channel_id=1, source_target_pairs={{0,1},{1,0},{2,3},{3,2},{4,5},{5,4},{6,7},{7,6},{8,9},{9,8},{10,11... | collective-permute-start | bytes 786440 | tf_op jit(solution)/shard_map/ppermute | solution.py:259
  35.1 8.2 %copy-start.8 = (f32[2,2,128,128]{3,2,1,0:T(8,128)S(1)}, f32[2,2,128,128]{3,2,1,0:T(8,128)}, u32[]{:S(2)}) copy-start(f32[2,2,128,128]{3,2,1,0:T(8,128)} %get-tuple-element.29) | copy-start | bytes 786436
  40.0 4.8 %collective-permute-start.3 = (f32[2,2,128,128]{3,2,1,0:T(8,128)}, f32[2,2,128,128]{3,2,1,0:T(8,128)S(1)}, u32[]{:S(2)}, u32[]{:S(2)}) collective-permute-start(f32[2,2,128,128]{3,2,1,0:T(8,128)} %get-tuple-element.33), channel_id=1, source_target_pairs={{0,1},{1,0},{2,3},{3,2},{4,5},{5,4},{6,7},{7,6},{8,9},{9,8},{10,11... | collective-permute-start | bytes 786440 | tf_op jit(solution)/shard_map/ppermute | solution.py:262
  45.8 16.6 %copy-start.2 = (f32[4,2,128,128]{3,2,1,0:T(8,128)}, f32[4,2,128,128]{3,2,1,0:T(8,128)S(1)}, u32[]{:S(2)}) copy-start(f32[4,2,128,128]{3,2,1,0:T(8,128)S(1)} %pad_maximum_fusion.mine) | copy-start | bytes 1572868
  45.8 26.1 %collective-permute-start.4 = (f32[4,2,128,128]{3,2,1,0:T(8,128)S(1)}, f32[4,2,128,128]{3,2,1,0:T(8,128)S(1)}, u32[]{:S(2)}, u32[]{:S(2)}) collective-permute-start(f32[4,2,128,128]{3,2,1,0:T(8,128)S(1)} %pad_maximum_fusion.mine), channel_id=1, source_target_pairs={{0,2},{1,3},{2,0},{3,1},{4,6},{5,7},{6,4},{7,5},{8,10},{9,11},{10,... | collective-permute-start | bytes 1572872 | tf_op jit(solution)/shard_map/ppermute | solution.py:264
  57.6 7.0 %copy-start.1 = (bf16[2,4,128,128]{3,2,1,0:T(8,128)(2,1)S(1)}, bf16[2,4,128,128]{3,2,1,0:T(8,128)(2,1)}, u32[]{:S(2)}) copy-start(bf16[2,4,128,128]{3,2,1,0:T(8,128)(2,1)} %refs_0_.1) | copy-start | bytes 786436
  57.6 12.1 %copy-start.21 = (s32[4,4]{1,0:T(4,128)S(1)}, s32[4,4]{1,0:T(4,128)}, u32[]{:S(2)}) copy-start(s32[4,4]{1,0:T(4,128)} %pad_add_fusion.2.meta) | copy-start | bytes 196
  57.6 12.2 %copy-start.20 = (s32[4,4]{1,0:T(4,128)S(1)}, s32[4,4]{1,0:T(4,128)}, u32[]{:S(2)}) copy-start(s32[4,4]{1,0:T(4,128)} %get-tuple-element.91.meta) | copy-start | bytes 196
  62.4 18.9 %copy-start.19 = (s32[4,4]{1,0:T(4,128)S(1)}, s32[4,4]{1,0:T(4,128)}, u32[]{:S(2)}) copy-start(s32[4,4]{1,0:T(4,128)} %get-tuple-element.92.meta) | copy-start | bytes 196
  62.4 8.0 %collective-permute-start.7 = (f32[2,2,128,128]{3,2,1,0:T(8,128)}, f32[2,2,128,128]{3,2,1,0:T(8,128)S(1)}, u32[]{:S(2)}, u32[]{:S(2)}) collective-permute-start(f32[2,2,128,128]{3,2,1,0:T(8,128)} %get-tuple-element.37), channel_id=1, source_target_pairs={{0,1},{1,0},{2,3},{3,2},{4,5},{5,4},{6,7},{7,6},{8,9},{9,8},{10,11... | collective-permute-start | bytes 786440 | tf_op jit(solution)/shard_map/ppermute | solution.py:268
  64.6 7.5 %collective-permute-start.10 = (bf16[2,2,128,128]{3,2,1,0:T(8,128)(2,1)S(1)}, bf16[2,2,128,128]{3,2,1,0:T(8,128)(2,1)S(1)}, u32[]{:S(2)}, u32[]{:S(2)}) collective-permute-start(bf16[2,2,128,128]{3,2,1,0:T(8,128)(2,1)S(1)} %dynamic-slice_bitcast_fusion), channel_id=1, source_target_pairs={{0,240},{4,244},{8,248},{12,252},{16,0},{20,4},{24,8},{28,12},{32,... | collective-permute-start | bytes 393224 | tf_op jit(solution)/shard_map/ppermute | solution.py:225
  69.1 4.8 %collective-permute-start.9 = (bf16[2,2,128,128]{3,2,1,0:T(8,128)(2,1)S(1)}, bf16[2,2,128,128]{3,2,1,0:T(8,128)(2,1)S(1)}, u32[]{:S(2)}, u32[]{:S(2)}) collective-permute-start(bf16[2,2,128,128]{3,2,1,0:T(8,128)(2,1)S(1)} %dynamic-slice_bitcast_fusion), channel_id=1, source_target_pairs={{0,12},{4,0},{8,4},{12,8},{16,28},{20,16},{24,20},{28,24},{32,44},... | collective-permute-start | bytes 393224 | tf_op jit(solution)/shard_map/ppermute | solution.py:224
  71.4 16.7 %copy-start.3 = (f32[2,2,128,128]{3,2,1,0:T(8,128)}, f32[2,2,128,128]{3,2,1,0:T(8,128)S(1)}, u32[]{:S(2)}) copy-start(f32[2,2,128,128]{3,2,1,0:T(8,128)S(1)} %add.260.mine) | copy-start | bytes 786436
  71.9 2.0 %copy-start.5 = (f32[4,2,128,128]{3,2,1,0:T(8,128)}, f32[4,2,128,128]{3,2,1,0:T(8,128)S(1)}, u32[]{:S(2)}) copy-start(f32[4,2,128,128]{3,2,1,0:T(8,128)S(1)} %collective-permute-done.4.other) | copy-start | bytes 1572868
  72.0 1.8 %copy-start.6 = (bf16[2,2,128,128]{3,2,1,0:T(8,128)(2,1)}, bf16[2,2,128,128]{3,2,1,0:T(8,128)(2,1)S(1)}, u32[]{:S(2)}) copy-start(bf16[2,2,128,128]{3,2,1,0:T(8,128)(2,1)S(1)} %collective-permute-done.10.refs_1_.refs_2_) | copy-start | bytes 393220
  73.9 0.7 copy-start.7
  77.6 24.1 %collective-permute-start.11 = (f32[6,2,128,128]{3,2,1,0:T(8,128)}, f32[6,2,128,128]{3,2,1,0:T(8,128)S(1)}, u32[]{:S(2)}, u32[]{:S(2)}) collective-permute-start(f32[6,2,128,128]{3,2,1,0:T(8,128)} %get-tuple-element.48.refs_0_), channel_id=1, source_target_pairs={{0,1},{1,0},{2,3},{3,2},{4,5},{5,4},{6,7},{7,6},{8,9},{9,8},{10,11... | collective-permute-start | bytes 2359304 | tf_op jit(solution)/shard_map/ppermute | solution.py:281
  78.7 9.4 %collective-permute-start.8 = (f32[2,2,128,128]{3,2,1,0:T(8,128)S(1)}, f32[2,2,128,128]{3,2,1,0:T(8,128)S(1)}, u32[]{:S(2)}, u32[]{:S(2)}) collective-permute-start(f32[2,2,128,128]{3,2,1,0:T(8,128)S(1)} %add.260.mine), channel_id=1, source_target_pairs={{0,2},{1,3},{2,0},{3,1},{4,6},{5,7},{6,4},{7,5},{8,10},{9,11},{10,... | collective-permute-start | bytes 786440 | tf_op jit(solution)/shard_map/ppermute | solution.py:269
  81.3 10.0 %collective-permute-start.14 = (f32[1,2,128,128]{3,2,1,0:T(8,128)}, f32[1,2,128,128]{3,2,1,0:T(8,128)S(1)}, u32[]{:S(2)}, u32[]{:S(2)}) collective-permute-start(f32[1,2,128,128]{3,2,1,0:T(8,128)} %get-tuple-element.44), channel_id=1, source_target_pairs={{240,0},{244,4},{248,8},{252,12},{0,16},{4,20},{8,24},{12,28},{16,... | collective-permute-start | bytes 393224 | tf_op jit(solution)/shard_map/ppermute | solution.py:279
  82.0 10.6 %collective-permute-start.12 = (f32[1,2,128,128]{3,2,1,0:T(8,128)}, f32[1,2,128,128]{3,2,1,0:T(8,128)S(1)}, u32[]{:S(2)}, u32[]{:S(2)}) collective-permute-start(f32[1,2,128,128]{3,2,1,0:T(8,128)} %get-tuple-element.43), channel_id=1, source_target_pairs={{12,0},{0,4},{4,8},{8,12},{28,16},{16,20},{20,24},{24,28},{44,32},... | collective-permute-start | bytes 393224 | tf_op jit(solution)/shard_map/ppermute | solution.py:280
  82.0 10.7 %collective-permute-start.13 = (f32[1,2,128,128]{3,2,1,0:T(8,128)}, f32[1,2,128,128]{3,2,1,0:T(8,128)S(1)}, u32[]{:S(2)}, u32[]{:S(2)}) collective-permute-start(f32[1,2,128,128]{3,2,1,0:T(8,128)} %get-tuple-element.43), channel_id=1, source_target_pairs={{12,1},{13,0},{14,3},{15,2},{0,5},{1,4},{2,7},{3,6},{4,9},{5,8},{6... | collective-permute-start | bytes 393224 | tf_op jit(solution)/shard_map/ppermute | solution.py:280
  88.1 0.7 copy-start.10
  91.3 9.0 %collective-permute-start.19 = (f32[1,2,128,128]{3,2,1,0:T(8,128)}, f32[1,2,128,128]{3,2,1,0:T(8,128)S(1)}, u32[]{:S(2)}, u32[]{:S(2)}) collective-permute-start(f32[1,2,128,128]{3,2,1,0:T(8,128)} %get-tuple-element.47), channel_id=1, source_target_pairs={{240,0},{244,4},{248,8},{252,12},{0,16},{4,20},{8,24},{12,28},{16,... | collective-permute-start | bytes 393224 | tf_op jit(solution)/shard_map/ppermute | solution.py:279
  91.3 11.8 %copy-start.11 = (f32[1,2,128,128]{3,2,1,0:T(8,128)}, f32[1,2,128,128]{3,2,1,0:T(8,128)S(1)}, u32[]{:S(2)}) copy-start(f32[1,2,128,128]{3,2,1,0:T(8,128)S(1)} %collective-permute-done.14.refs_4_) | copy-start | bytes 393220
  91.4 10.3 %collective-permute-start.15 = (f32[1,2,128,128]{3,2,1,0:T(8,128)S(1)}, f32[1,2,128,128]{3,2,1,0:T(8,128)S(1)}, u32[]{:S(2)}, u32[]{:S(2)}) collective-permute-start(f32[1,2,128,128]{3,2,1,0:T(8,128)S(1)} %collective-permute-done.14.refs_4_), channel_id=1, source_target_pairs={{0,1},{1,0},{2,3},{3,2},{4,5},{5,4},{6,7},{7,6},{8,9},{9,8},{10,11... | collective-permute-start | bytes 393224 | tf_op jit(solution)/shard_map/ppermute | solution.py:282
  92.6 10.5 %copy-start.13 = (f32[1,2,128,128]{3,2,1,0:T(8,128)}, f32[1,2,128,128]{3,2,1,0:T(8,128)S(1)}, u32[]{:S(2)}) copy-start(f32[1,2,128,128]{3,2,1,0:T(8,128)S(1)} %collective-permute-done.12.refs_2_) | copy-start | bytes 393220
  92.6 13.5 %collective-permute-start.17 = (f32[1,2,128,128]{3,2,1,0:T(8,128)}, f32[1,2,128,128]{3,2,1,0:T(8,128)S(1)}, u32[]{:S(2)}, u32[]{:S(2)}) collective-permute-start(f32[1,2,128,128]{3,2,1,0:T(8,128)} %get-tuple-element.46), channel_id=1, source_target_pairs={{12,0},{0,4},{4,8},{8,12},{28,16},{16,20},{20,24},{24,28},{44,32},... | collective-permute-start | bytes 393224 | tf_op jit(solution)/shard_map/ppermute | solution.py:280
  92.7 10.4 %copy-start.14 = (f32[1,2,128,128]{3,2,1,0:T(8,128)}, f32[1,2,128,128]{3,2,1,0:T(8,128)S(1)}, u32[]{:S(2)}) copy-start(f32[1,2,128,128]{3,2,1,0:T(8,128)S(1)} %collective-permute-done.13.refs_3_) | copy-start | bytes 393220
  92.7 13.4 %collective-permute-start.18 = (f32[1,2,128,128]{3,2,1,0:T(8,128)}, f32[1,2,128,128]{3,2,1,0:T(8,128)S(1)}, u32[]{:S(2)}, u32[]{:S(2)}) collective-permute-start(f32[1,2,128,128]{3,2,1,0:T(8,128)} %get-tuple-element.46), channel_id=1, source_target_pairs={{12,1},{13,0},{14,3},{15,2},{0,5},{1,4},{2,7},{3,6},{4,9},{5,8},{6... | collective-permute-start | bytes 393224 | tf_op jit(solution)/shard_map/ppermute | solution.py:280
  100.3 5.9 %copy-start.12 = (f32[1,2,128,128]{3,2,1,0:T(8,128)}, f32[1,2,128,128]{3,2,1,0:T(8,128)S(1)}, u32[]{:S(2)}) copy-start(f32[1,2,128,128]{3,2,1,0:T(8,128)S(1)} %collective-permute-done.19.refs_4_) | copy-start | bytes 393220
  100.3 5.8 %collective-permute-start.20 = (f32[1,2,128,128]{3,2,1,0:T(8,128)S(1)}, f32[1,2,128,128]{3,2,1,0:T(8,128)S(1)}, u32[]{:S(2)}, u32[]{:S(2)}) collective-permute-start(f32[1,2,128,128]{3,2,1,0:T(8,128)S(1)} %collective-permute-done.19.refs_4_), channel_id=1, source_target_pairs={{0,1},{1,0},{2,3},{3,2},{4,5},{5,4},{6,7},{7,6},{8,9},{9,8},{10,11... | collective-permute-start | bytes 393224 | tf_op jit(solution)/shard_map/ppermute | solution.py:282
  101.7 1.5 %copy-start.17 = (f32[1,2,128,128]{3,2,1,0:T(8,128)}, f32[1,2,128,128]{3,2,1,0:T(8,128)S(1)}, u32[]{:S(2)}) copy-start(f32[1,2,128,128]{3,2,1,0:T(8,128)S(1)} %collective-permute-done.15.refs_5_) | copy-start | bytes 393220
  101.7 1.5 %copy-start.4 = (f32[6,2,128,128]{3,2,1,0:T(8,128)}, f32[6,2,128,128]{3,2,1,0:T(8,128)S(1)}, u32[]{:S(2)}) copy-start(f32[6,2,128,128]{3,2,1,0:T(8,128)S(1)} %collective-permute-done.11.refs_1_) | copy-start | bytes 2359300
  101.7 4.5 %collective-permute-start.16 = (f32[2,2,128,128]{3,2,1,0:T(8,128)}, f32[2,2,128,128]{3,2,1,0:T(8,128)S(1)}, u32[]{:S(2)}, u32[]{:S(2)}) collective-permute-start(f32[2,2,128,128]{3,2,1,0:T(8,128)} %get-tuple-element.45.refs_0_), channel_id=1, source_target_pairs={{0,1},{1,0},{2,3},{3,2},{4,5},{5,4},{6,7},{7,6},{8,9},{9,8},{10,11... | collective-permute-start | bytes 786440 | tf_op jit(solution)/shard_map/ppermute | solution.py:281
  106.1 0.6 copy-start.15
  106.1 0.7 copy-start.16
  106.1 0.7 copy-start.18
  106.2 0.8 copy-start.9

commit v2 on v1

v2 whole, which is shorter than its diff:
```python
import math

import jax
import jax.numpy as jnp
from jax import lax
from jax.experimental import pallas as pl
from jax.experimental.pallas import tpu as pltpu
from jax.sharding import PartitionSpec as P

KRING = 4
GY = 32
GZ = 32
F32 = jnp.float32
BF16 = jnp.bfloat16
PACKED_ROWS = 16
SHIFT = 13
VMEM = pltpu.VMEM
CONTRACT_LAST = (((1,), (1,)), ((), ()))
CONTRACT_FIRST = (((0,), (0,)), ((), ()))


def grid_fractions(plane_first, plane_count, plane_total):
    point_index = jnp.arange(plane_count * GY * GZ, dtype=jnp.int32)
    plane = point_index // (GY * GZ) + plane_first
    middle = point_index // GZ % GY
    inner = point_index % GZ
    return [
        plane.astype(F32) / F32(plane_total),
        middle.astype(F32) / F32(GY),
        inner.astype(F32) / F32(GZ),
    ]


def phase_angles(shift_rows, direction, mesh_counts, fractions):
    total = jnp.zeros((shift_rows.shape[0], fractions[0].shape[0]), F32)
    for lattice in range(3):
        step = 1.0 / mesh_counts[lattice] if lattice == direction else 0.0
        wave = shift_rows[:, lattice].astype(F32) + F32(step)
        total = total + wave[:, None] * fractions[lattice][None, :]
    return F32(2.0 * math.pi) * total


def vmem(*arrays):
    return tuple(pltpu.with_memory_space_constraint(array, VMEM) for array in arrays)


def specs(*spaces):
    return [pl.BlockSpec(memory_space=space) for space in spaces]


def small(mib):
    return {
        "cost_estimate": pl.CostEstimate(flops=1, bytes_accessed=1, transcendentals=0),
        "compiler_params": pltpu.CompilerParams(vmem_limit_bytes=mib * 2**20),
    }


def load(core, orbitals, gauge, part):
    nb, points = orbitals.shape[2:]
    blocks = points // nb

    def body(core, orbitals, gauge, out, block, sems):
        copies = [
            pltpu.make_async_copy(
                orbitals.at[c, 2 * part + slot], out.at[c, slot * nb : (slot + 1) * nb], sems.at[2 * c + slot]
            )
            for c in range(2)
            for slot in range(2)
        ]
        copies.append(pltpu.make_async_copy(gauge.at[:, 2 * part + core[0]], block, sems.at[4]))
        for copy in copies:
            copy.start()
        copies[4].wait()
        for c in range(2):
            for j in range(blocks):
                rows = block[c, j * PACKED_ROWS : (j + 1) * PACKED_ROWS, :]
                out[c, 2 * nb :, j * nb : (j + 1) * nb] = rows
        for copy in copies[:4]:
            copy.wait()

    return pl.pallas_call(
        body,
        name="load",
        out_shape=VMEM((2, 2 * nb + PACKED_ROWS, points), BF16),
        in_specs=specs(pltpu.SMEM, pl.ANY, pl.ANY),
        out_specs=specs(VMEM)[0],
        scratch_shapes=[VMEM((2, nb, nb), BF16), pltpu.SemaphoreType.DMA((5,))],
        **small(2),
    )(core, *[pltpu.with_memory_space_constraint(array, pltpu.HBM) for array in (orbitals, gauge)])


def correlate(meta, base, directions, cosines, sines, own, sources):
    nb = (own[0].shape[1] - PACKED_ROWS) // 2
    points = own[0].shape[2]

    def body(meta, cosines, sines, front, rear, *refs):
        sources_in = refs[:2]
        give, keep, left, phased = refs[2:]
        for p in range(4):
            slot, k = meta[0, base + p], meta[1, base + p]
            source = sources_in[p % 2]
            lefts, shifted = left.at[p % 2], phased.at[p % 2]
            for half, ref in enumerate((front, rear)):

                @pl.when(k // 2 == half)
                def _():
                    start = pl.multiple_of((k - 2 * half) * nb, nb)
                    for c in range(2):
                        lefts[c * nb : (c + 1) * nb, :] = ref[c, pl.ds(start, nb), :]

            row = directions[p % 2] * 4 + k
            cosine = cosines[pl.ds(row, 1), :]
            sine = sines[pl.ds(row, 1), :]
            start = pl.multiple_of(slot * nb, nb)
            source_re = source[0, pl.ds(start, nb), :].astype(F32)
            source_im = source[1, pl.ds(start, nb), :].astype(F32)
            shifted[0:nb, :] = (cosine * source_re + sine * source_im).astype(BF16)
            shifted[nb:, :] = (cosine * source_im - sine * source_re).astype(BF16)
            full = lax.dot_general(lefts[...], shifted[...], CONTRACT_LAST, preferred_element_type=F32)
            out = give if p < 2 else keep
            out[p % 2, 0] = full[:nb, :nb] + full[nb:, nb:]
            out[p % 2, 1] = full[:nb, nb:] - full[nb:, :nb]

    half_out = VMEM((2, 2, nb, nb), F32)
    return pl.pallas_call(
        body,
        name="correlate",
        out_shape=(half_out, half_out),
        in_specs=specs(pltpu.SMEM, *[VMEM] * 6),
        out_specs=tuple(specs(VMEM, VMEM)),
        scratch_shapes=[VMEM((2, 2 * nb, points), BF16), VMEM((2, 2 * nb, points), BF16)],
        **small(8),
    )(meta, *vmem(cosines, sines, *own, *sources))


def split_parts(values):
    high = values.astype(BF16)
    low = (values - high.astype(F32)).astype(BF16)
    return high, low


def rotate_pair(raw_parts, left, right):
    nb = left[0].shape[0]
    raw_re, raw_im = [jnp.concatenate(split_parts(part), axis=1) for part in raw_parts]
    raw = jnp.concatenate([raw_re, raw_im], axis=0)
    wide = jnp.concatenate(right, axis=1)
    prod = jnp.dot(raw, jnp.concatenate([wide, wide], axis=0), preferred_element_type=F32)
    temp_re = prod[:nb, :nb] - prod[nb:, nb:]
    temp_im = prod[:nb, nb:] + prod[nb:, :nb]
    re_high, re_low = split_parts(temp_re)
    im_high, im_low = split_parts(temp_im)
    temp = jnp.concatenate(
        [jnp.concatenate([re_high, im_high], axis=1), jnp.concatenate([re_low, im_low], axis=1)], axis=0
    )
    tall = jnp.concatenate(left, axis=1)
    prod = lax.dot_general(
        jnp.concatenate([tall, tall], axis=0), temp, CONTRACT_FIRST, preferred_element_type=F32
    )
    return prod[:nb, :nb] + prod[nb:, nb:], prod[:nb, nb:] - prod[nb:, :nb]


def encode(chip):
    pairs, _, nb, _ = chip.shape
    largest = jnp.max(jnp.abs(chip), axis=(1, 2, 3))
    exponent = jnp.floor(jnp.log2(jnp.maximum(largest, F32(1e-30))))
    scaled = chip * jnp.exp2(F32(SHIFT) - exponent)[:, None, None, None]
    tail = jnp.broadcast_to(exponent[:, None, None], (pairs, 8, nb))
    coded = jnp.concatenate([scaled.reshape(pairs, 2 * nb, nb), tail], axis=1).astype(jnp.float16)
    return lax.optimization_barrier(coded)


def decode(coded):
    pairs, rows, nb = coded.shape
    exponent = coded[:, rows - 1, 0].astype(F32)
    values = coded[:, : 2 * nb].astype(F32) * jnp.exp2(exponent - F32(SHIFT))[:, None, None]
    return values.reshape(pairs, 2, nb, nb)


def rotate(meta, columns, raw, gauge, packed, right_of, layout):
    nb = gauge.shape[2]
    pairs = len(right_of)

    def unpack(ref, c):
        rows = ref.shape[1] - PACKED_ROWS
        blocks = [ref[c, rows:, j * nb : (j + 1) * nb] for j in range(ref.shape[2] // nb)]
        return jnp.concatenate(blocks, axis=0)

    def body(slots, raw, gauge, *refs):
        payloads, outs = refs[: len(packed)], refs[len(packed) :]
        for p in range(pairs):
            k = slots[1, columns[p]]
            if right_of[p] is None:
                right = [gauge[c, slots[3, columns[p]]] for c in range(2)]
            else:
                right = [unpack(payloads[right_of[p]], c) for c in range(2)]
            out_re, out_im = rotate_pair([raw[p, c] for c in range(2)], [gauge[c, k] for c in range(2)], right)
            for out, rows in zip(outs, layout):
                for row, (pair, adjoint) in enumerate(rows):
                    if pair == p and adjoint:
                        out[row, 0] = out_re.T
                        out[row, 1] = -out_im.T
                    elif pair == p:
                        out[row, 0] = out_re
                        out[row, 1] = out_im

    return pl.pallas_call(
        body,
        name="rotate",
        out_shape=tuple(VMEM((len(rows), 2, nb, nb), F32) for rows in layout),
        in_specs=specs(pltpu.SMEM, *[VMEM] * (2 + len(packed))),
        out_specs=tuple(specs(*[VMEM] * len(layout))),
        **small(8),
    )(meta, *vmem(raw, gauge, *packed))


def place(targets, meta, blocks, outs):
    nb = blocks[0].shape[-1]
    shape = jax.ShapeDtypeStruct((3, 2, 4, nb, nb), F32)
    previous = () if outs is None else tuple(outs)
    def body(slots, *refs):
        sems = refs[-1]
        into = refs[-3:-1]
        copies = []
        for block, rows in zip(refs, targets):
            for n, (output, direction, column) in enumerate(rows):
                target = into[output].at[direction, :, slots[3 if output else 1, column]]
                copies.append(pltpu.make_async_copy(block.at[n], target, sems.at[len(copies)]))
        for copy in copies:
            copy.start()
        for copy in copies:
            copy.wait()

    count = len(blocks)
    total = sum(len(rows) for rows in targets)
    return pl.pallas_call(
        body,
        out_shape=(shape, shape),
        name="place",
        in_specs=specs(pltpu.SMEM, *[VMEM] * count, *[pl.ANY] * len(previous)),
        out_specs=tuple(specs(pl.ANY, pl.ANY)),
        scratch_shapes=[pltpu.SemaphoreType.DMA((total,))],
        input_output_aliases={1 + count: 0, 2 + count: 1} if previous else {},
        **small(2),
    )(meta, *vmem(*blocks), *previous)


def shards(orbitals, gauge, neighbour, wrap_shift):
    kloc = orbitals.shape[1]
    grid_points = orbitals.shape[3]
    ka_count = lax.axis_size("ka")
    ga_count = lax.axis_size("ga")
    device = lax.axis_index("ka")
    grid_part = lax.axis_index("ga")
    core = grid_part % 2
    plane_count = grid_points // (GY * GZ)
    counts = (kloc, KRING, ka_count // KRING)

    ring_back = [(d, d // KRING * KRING + (d - 1) % KRING) for d in range(ka_count)]
    outer_back = [(d, (d - KRING) % ka_count) for d in range(ka_count)]
    ring_ahead = [(t, s) for s, t in ring_back]
    outer_ahead = [(t, s) for s, t in outer_back]
    sibling = [(g, g ^ 1) for g in range(ga_count)]
    across = [(g, g ^ 2) for g in range(ga_count)]

    core_index = core.reshape(1).astype(jnp.int32)
    front = load(core_index, orbitals, gauge, 0)
    beyond_front = lax.ppermute(front, "ka", outer_back)
    beside_front = lax.ppermute(front, "ka", ring_back)
    rear = load(core_index, orbitals, gauge, 1)
    beyond_rear = lax.ppermute(rear, "ka", outer_back)
    beside_rear = lax.ppermute(rear, "ka", ring_back)
    own = (front, rear)

    fractions = grid_fractions(grid_part * plane_count, plane_count, plane_count * ga_count)
    my_table = lax.dynamic_slice_in_dim(neighbour, device * kloc, kloc, 0) % kloc
    my_shift = lax.dynamic_slice_in_dim(wrap_shift, device * kloc, kloc, 0)
    slots = jnp.arange(kloc, dtype=jnp.int32)
    local = jnp.stack([1 - core, 1 - core, core, core]).astype(jnp.int32)
    is_second = slots % 2

    def k_slots(direction, wanted):
        match = my_table[:, direction][:, None] == wanted[None, :]
        return jnp.sum(jnp.where(match, slots[:, None], 0), axis=0)

    order = local + 2 * is_second
    first_k = jnp.stack([k_slots(0, order), k_slots(1, local), k_slots(1, local + 2)])
    second_k = jnp.stack([k_slots(0, order), k_slots(2, local), k_slots(2, local + 2)])
    ks = jnp.where(is_second == 0, first_k, second_k).reshape(-1)
    locals_ = jnp.tile(local, 3)
    meta = jnp.stack([locals_, ks, locals_, jnp.concatenate([order, local, local + 2])])

    angles = jnp.concatenate([phase_angles(my_shift[:, b, :], b, counts, fractions) for b in range(3)])
    cosines, sines = jnp.cos(angles), jnp.sin(angles)

    give, keep = correlate(meta, 0, (0, 0), cosines, sines, own, own)
    got = lax.ppermute(give, "ga", sibling)
    give_front, keep_front = correlate(meta, 4, (1, 2), cosines, sines, own, (beside_front, beyond_front))
    got_front = lax.ppermute(give_front, "ga", sibling)
    coded = encode(jnp.concatenate([keep + got, keep_front + got_front], axis=0))
    coded, beside_rear, beyond_rear = lax.optimization_barrier((coded, beside_rear, beyond_rear))
    other = lax.ppermute(coded, "ga", across)
    give, keep = correlate(meta, 8, (1, 2), cosines, sines, own, (beside_rear, beyond_rear))
    coded_rear = encode(keep + lax.ppermute(give, "ga", sibling))
    other_rear = lax.ppermute(coded_rear, "ga", across)

    other, coded_rear = lax.optimization_barrier((other, coded_rear))
    first, adj_x, adj_y = rotate(
        meta, (2, 3, 6, 7), decode(coded) + decode(other), gauge, (beside_front, beyond_front), (None, None, 0, 1),
        [[(0, 0), (1, 0), (2, 0), (3, 0), (0, 1), (1, 1)], [(2, 1)], [(3, 1)]],
    )
    last, adj_x_rear, adj_y_rear = rotate(
        meta, (10, 11), decode(coded_rear) + decode(other_rear), gauge, (beside_rear, beyond_rear), (0, 1),
        [[(0, 0), (1, 0)], [(0, 1)], [(1, 1)]],
    )
    adj_y = lax.ppermute(jnp.concatenate([adj_y, adj_y_rear], axis=0), "ka", outer_ahead)
    adj_x = lax.ppermute(jnp.concatenate([adj_x, adj_x_rear], axis=0), "ka", ring_ahead)
    fwd = jnp.concatenate([first, last], axis=0)
    fwd_sib = lax.ppermute(fwd, "ga", sibling)
    adj = jnp.concatenate([adj_x, adj_y], axis=0)
    adj_sib = lax.ppermute(adj, "ga", sibling)
    targets = [
        [(0, 0, i), (0, 0, i + 1), (0, 1, i + 4), (0, 2, i + 5), (1, 0, i), (1, 0, i + 1), (0, 1, i + 8), (0, 2, i + 9)]
        for i in (2, 0)
    ]
    outs = place(targets, meta, (fwd, fwd_sib), None)
    targets = [[(1, 1, i + 4), (1, 1, i + 8), (1, 2, i + 5), (1, 2, i + 9)] for i in (2, 0)]
    return tuple(place(targets, meta, (adj, adj_sib), outs))


def solution(mesh):
    in_specs = (P(None, "ka", None, "ga"), P(None, "ka", None, None), P(), P())
    out_specs = (P(None, None, "ka", None, None), P(None, None, "ka", None, None))
    return jax.shard_map(shards, mesh=mesh, in_specs=in_specs, out_specs=out_specs, check_vma=False)
```

time: 110 us -> 96.4 us (0.88)
  waiting for transfers between devices: 32.6 us -> 46.6 us
  local copies, waits for them, and re-layouts: 9.52 us -> 0.89 us
  starting transfers between devices: 33.3 us -> 25.3 us
  other arithmetic: 8.22 us -> 2.56 us
  Pallas kernels: 24.4 us -> 19.6 us
    ppermute x15 -> x7, starting transfers between devices: 17.5 us -> 9.2 us  [the longest x1 2.64 us: shards(): other = lax.ppermute(coded, 'ga', across)]
    ppermute x1, waiting for transfers between devices: 6.31 us -> 13.4 us  [shards(): beyond_rear = lax.ppermute(rear, 'ka', outer_back)]
    ppermute x1, waiting for transfers between devices: 6.27 us -> 12.5 us  [shards(): beyond_front = lax.ppermute(front, 'ka', outer_back)]
    pallas_call x7 -> x9, Pallas kernels: 24.4 us -> 19.6 us  [the longest x3 9.43 us: correlate(): pl.pallas_call(body, name='correlate', out_shape=(half_out, half_out), in...]
    slice x4 -> x0, local copies, waits for them, and re-layouts: 3.58 us -> none  [the longest x1 2.77 us: shards(): rear = orbitals[:, 2:]]
    unnamed x48 -> x8, local copies, waits for them, and re-layouts: 3.51 us -> 0.09 us
    another operation x4 -> x3, other arithmetic: 2.52 us -> 0.25 us  [the longest x2 1.32 us: shards(): twiddles = [jnp.stack([jnp.cos(a), jnp.sin(a)], axis=1) for a in angles]]
    add x7 -> x6, other arithmetic: 2.15 us -> 0.41 us  [the longest x1 0.15 us: shards(): decode(coded) + decode(other)]
  transfers between devices with their start and end apart: 21 -> 13, of which waited for: 10 -> 9; matrix products, arithmetic and copies ran while one was open for 10% -> 3% of each run, Pallas kernels for 18% -> 11%
where the time goes in v2:
time: 96.4 us; the launch traced here: 96 us
  waiting for transfers between devices  46.6 us (48%)
  starting transfers between devices  25.3 us (26%)
  Pallas kernels  19.6 us (20%)
  other arithmetic  2.56 us (3%)
  between operations  1.03 us (1%)
    ppermute x1, waiting for transfers between devices, shards(): beyond_rear = lax.ppermute(rear, 'ka', outer_back)  13.4 us
    ppermute x1, waiting for transfers between devices, shards(): beyond_front = lax.ppermute(front, 'ka', outer_back)  12.5 us
    pallas_call x3, Pallas kernels, correlate(): pl.pallas_call(body, name='correlate', out_shape=(half_out, half_out), in...  9.43 us
    ppermute x1, waiting for transfers between devices, shards(): lax.ppermute(jnp.concatenate([adj_x, adj_x_rear], axis=0), 'ka', ring_ahead)  9.07 us
    ppermute x1, starting transfers between devices, shards(): beyond_front = lax.ppermute(front, 'ka', outer_back)  7.49 us
    ppermute x1, waiting for transfers between devices, shards(): other = lax.ppermute(coded, 'ga', across)  5.12 us
    pallas_call x2, Pallas kernels, rotate(): pl.pallas_call(body, name='rotate', out_shape=tuple((VMEM((len(rows), 2,...  4.11 us
    pallas_call x2, Pallas kernels, place(): pl.pallas_call(body, out_shape=(shape, shape), name='place', in_specs=spe...  3.6 us
  transfers between devices with their start and end apart: 13, of which 9 were waited for; matrix products, arithmetic and copies ran while one was open for 3% of the time, Pallas kernels for 11%

profile of v2, /device:TPU:1, one launch (start us, length us, event | category | flops | bytes accessed | tf_op | source)
XLA Modules:
  0.0 96.0 jit_solution(6354632806892208419)
XLA Ops:
  0.6 1.2 %load.2.front.refs_0_ = bf16[2,272,1024]{2,1,0:T(8,128)(2,1)S(1)} custom-call(s32[1]{0:T(128)} %bitcast.1.core, bf16[2,4,128,1024]{3,2,1,0:T(8,128)(2,1)} %orbitals.3, bf16[2,4,128,128]{3,2,1,0:T(8,128)(2,1)} %gauge.7), custom_call_target="tpu_custom_call" | custom-call | flops 1 | bytes 1 | tf_op jit(solution)/shard_map/load/pallas_call | solution.py:81
  1.9 0.0 copy-start.2
  1.9 0.0 copy-start.1
  1.9 7.5 %collective-permute-start.2 = (bf16[2,272,1024]{2,1,0:T(8,128)(2,1)S(1)}, bf16[2,272,1024]{2,1,0:T(8,128)(2,1)S(1)}, u32[]{:S(2)}, u32[]{:S(2)}) collective-permute-start(bf16[2,272,1024]{2,1,0:T(8,128)(2,1)S(1)} %load.2.front.refs_0_), channel_id=1, source_target_pairs={{0,240},{4,244},{8,248},{12,252},{16,0},{20,4},{24,8},{28,12},{32,... | collective-permute-start | bytes 3342344 | tf_op jit(solution)/shard_map/ppermute | solution.py:267
  9.4 2.5 %collective-permute-start.1 = (bf16[2,272,1024]{2,1,0:T(8,128)(2,1)S(1)}, bf16[2,272,1024]{2,1,0:T(8,128)(2,1)}, u32[]{:S(2)}, u32[]{:S(2)}) collective-permute-start(bf16[2,272,1024]{2,1,0:T(8,128)(2,1)S(1)} %load.2.front.refs_0_), channel_id=1, source_target_pairs={{0,12},{4,0},{8,4},{12,8},{16,28},{20,16},{24,20},{28,24},{32,44},... | collective-permute-start | bytes 3342344 | tf_op jit(solution)/shard_map/ppermute | solution.py:268
  11.9 1.2 %load.3.rear.refs_1_ = bf16[2,272,1024]{2,1,0:T(8,128)(2,1)S(1)} custom-call(s32[1]{0:T(128)} %bitcast.1.core, bf16[2,4,128,1024]{3,2,1,0:T(8,128)(2,1)} %orbitals.3, bf16[2,4,128,128]{3,2,1,0:T(8,128)(2,1)} %gauge.7), custom_call_target="tpu_custom_call" | custom-call | flops 1 | bytes 1 | tf_op jit(solution)/shard_map/load/pallas_call | solution.py:81
  13.1 0.2 collective-permute-start.5
  13.4 0.5 collective-permute-start.4
  13.9 0.1 broadcast_add_fusion
  14.0 0.1 add_select_fusion.4
  14.1 0.1 constant_dynamic-slice_fusion.1
  14.2 0.1 copy.30
  14.3 0.2 add_reduce_fusion.2
  14.5 0.1 copy.31
  14.6 0.1 copy.32
  14.7 0.3 convert_reduce_fusion.1
  14.9 0.1 select_reduce_fusion.1
  15.0 0.1 add_multiply_fusion.2
  15.1 0.1 concatenate.45
  15.2 0.1 stack_tile.4
  15.3 0.1 select_n.116
  15.4 0.3 fusion.2
  15.7 2.6 %correlate.3 = (f32[2,2,128,128]{3,2,1,0:T(8,128)S(1)}, f32[2,2,128,128]{3,2,1,0:T(8,128)S(1)}) custom-call(s32[4,12]{1,0:T(4,128)S(1)} %pad_add_fusion.2.meta.slots, f32[12,1024]{1,0:T(8,128)S(1)} %get-tuple-element.58.cosines, f32[12,1024]{1,0:T(8,128)S(1)} %get-tuple-element.57.sines, bf16[2,272,1024]{2,1,0:T(8,128)(2,1)S(1)} %load.2.front.refs_0_, ...), custom_call_target="tpu_custom_call" | custom-call | flops 1 | bytes 1 | tf_op jit(solution)/shard_map/correlate/pallas_call | solution.py:125
  18.2 1.9 %collective-permute-start = (f32[2,2,128,128]{3,2,1,0:T(8,128)S(1)}, f32[2,2,128,128]{3,2,1,0:T(8,128)S(1)}, u32[]{:S(2)}, u32[]{:S(2)}) collective-permute-start(f32[2,2,128,128]{3,2,1,0:T(8,128)S(1)} %get-tuple-element.22), channel_id=1, source_target_pairs={{0,1},{1,0},{2,3},{3,2},{4,5},{5,4},{6,7},{7,6},{8,9},{9,8},{10,11... | collective-permute-start | bytes 786440 | tf_op jit(solution)/shard_map/ppermute | solution.py:296
  20.1 12.5 %collective-permute-done.2.refs_1_ = bf16[2,272,1024]{2,1,0:T(8,128)(2,1)S(1)} collective-permute-done((bf16[2,272,1024]{2,1,0:T(8,128)(2,1)S(1)}, bf16[2,272,1024]{2,1,0:T(8,128)(2,1)S(1)}, u32[]{:S(2)}, u32[]{:S(2)}) %collective-permute-start.2) | collective-permute-done | bytes 1114144 | tf_op jit(solution)/shard_map/ppermute | solution.py:267
  32.6 2.2 %collective-permute-done.1.refs_0_ = bf16[2,272,1024]{2,1,0:T(8,128)(2,1)} collective-permute-done((bf16[2,272,1024]{2,1,0:T(8,128)(2,1)S(1)}, bf16[2,272,1024]{2,1,0:T(8,128)(2,1)}, u32[]{:S(2)}, u32[]{:S(2)}) %collective-permute-start.1) | collective-permute-done | bytes 1114144 | tf_op jit(solution)/shard_map/ppermute | solution.py:268
  34.8 3.3 %correlate.4 = (f32[2,2,128,128]{3,2,1,0:T(8,128)S(1)}, f32[2,2,128,128]{3,2,1,0:T(8,128)S(1)}) custom-call(s32[4,12]{1,0:T(4,128)S(1)} %pad_add_fusion.2.meta.slots, f32[12,1024]{1,0:T(8,128)S(1)} %get-tuple-element.58.cosines, f32[12,1024]{1,0:T(8,128)S(1)} %get-tuple-element.57.sines, bf16[2,272,1024]{2,1,0:T(8,128)(2,1)S(1)} %load.2.front.refs_0_, ...), custom_call_target="tpu_custom_call" | custom-call | flops 1 | bytes 1 | tf_op jit(solution)/shard_map/correlate/pallas_call | solution.py:125
  38.1 3.4 %collective-permute-start.3 = (f32[2,2,128,128]{3,2,1,0:T(8,128)S(1)}, f32[2,2,128,128]{3,2,1,0:T(8,128)S(1)}, u32[]{:S(2)}, u32[]{:S(2)}) collective-permute-start(f32[2,2,128,128]{3,2,1,0:T(8,128)S(1)} %get-tuple-element.24), channel_id=1, source_target_pairs={{0,1},{1,0},{2,3},{3,2},{4,5},{5,4},{6,7},{7,6},{8,9},{9,8},{10,11... | collective-permute-start | bytes 786440 | tf_op jit(solution)/shard_map/ppermute | solution.py:298
  41.5 0.0 collective-permute-done
  41.5 1.1 %collective-permute-done.3 = f32[2,2,128,128]{3,2,1,0:T(8,128)S(1)} collective-permute-done((f32[2,2,128,128]{3,2,1,0:T(8,128)S(1)}, f32[2,2,128,128]{3,2,1,0:T(8,128)S(1)}, u32[]{:S(2)}, u32[]{:S(2)}) %collective-permute-start.3) | collective-permute-done | bytes 262176 | tf_op jit(solution)/shard_map/ppermute | solution.py:298
  42.7 0.1 fusion.1
  42.8 0.1 fusion
  42.9 0.1 broadcast_in_dim.99
  43.0 0.1 pad_maximum_fusion
  43.1 13.4 %collective-permute-done.5.refs_1_ = bf16[2,272,1024]{2,1,0:T(8,128)(2,1)} collective-permute-done((bf16[2,272,1024]{2,1,0:T(8,128)(2,1)S(1)}, bf16[2,272,1024]{2,1,0:T(8,128)(2,1)}, u32[]{:S(2)}, u32[]{:S(2)}) %collective-permute-start.5) | collective-permute-done | bytes 1114144 | tf_op jit(solution)/shard_map/ppermute | solution.py:270
  56.5 2.2 %collective-permute-done.4.refs_0_ = bf16[2,272,1024]{2,1,0:T(8,128)(2,1)} collective-permute-done((bf16[2,272,1024]{2,1,0:T(8,128)(2,1)S(1)}, bf16[2,272,1024]{2,1,0:T(8,128)(2,1)}, u32[]{:S(2)}, u32[]{:S(2)}) %collective-permute-start.4) | collective-permute-done | bytes 1114144 | tf_op jit(solution)/shard_map/ppermute | solution.py:271
  58.7 3.6 %correlate.5 = (f32[2,2,128,128]{3,2,1,0:T(8,128)S(1)}, f32[2,2,128,128]{3,2,1,0:T(8,128)S(1)}) custom-call(s32[4,12]{1,0:T(4,128)S(1)} %pad_add_fusion.2.meta.slots, f32[12,1024]{1,0:T(8,128)S(1)} %get-tuple-element.58.cosines, f32[12,1024]{1,0:T(8,128)S(1)} %get-tuple-element.57.sines, bf16[2,272,1024]{2,1,0:T(8,128)(2,1)S(1)} %load.2.front.refs_0_, ...), custom_call_target="tpu_custom_call" | custom-call | flops 1 | bytes 1 | tf_op jit(solution)/shard_map/correlate/pallas_call | solution.py:125
  62.3 1.9 %collective-permute-start.7 = (f32[2,2,128,128]{3,2,1,0:T(8,128)S(1)}, f32[2,2,128,128]{3,2,1,0:T(8,128)S(1)}, u32[]{:S(2)}, u32[]{:S(2)}) collective-permute-start(f32[2,2,128,128]{3,2,1,0:T(8,128)S(1)} %get-tuple-element.29), channel_id=1, source_target_pairs={{0,1},{1,0},{2,3},{3,2},{4,5},{5,4},{6,7},{7,6},{8,9},{9,8},{10,11... | collective-permute-start | bytes 786440 | tf_op jit(solution)/shard_map/ppermute | solution.py:303
  64.2 2.6 %collective-permute-start.6 = (f16[4,264,128]{2,1,0:T(8,128)(2,1)S(1)}, f16[4,264,128]{2,1,0:T(8,128)(2,1)S(1)}, u32[]{:S(2)}, u32[]{:S(2)}) collective-permute-start(f16[4,264,128]{2,1,0:T(8,128)(2,1)S(1)} %pad_maximum_fusion), channel_id=1, source_target_pairs={{0,2},{1,3},{2,0},{3,1},{4,6},{5,7},{6,4},{7,5},{8,10},{9,11},{10,... | collective-permute-start | bytes 811016 | tf_op jit(solution)/shard_map/ppermute | solution.py:301
  66.9 0.1 exponential_reduce_fusion.1
  67.0 0.0 collective-permute-done.7
  67.0 0.1 abs_reduce_fusion
  67.1 0.1 multiply_convert_fusion
  67.2 0.1 broadcast_in_dim.100
  67.4 1.3 %collective-permute-start.8 = (f16[2,264,128]{2,1,0:T(8,128)(2,1)S(1)}, f16[2,264,128]{2,1,0:T(8,128)(2,1)S(1)}, u32[]{:S(2)}, u32[]{:S(2)}) collective-permute-start(f16[2,264,128]{2,1,0:T(8,128)(2,1)S(1)} %pad_maximum_fusion.3), channel_id=1, source_target_pairs={{0,2},{1,3},{2,0},{3,1},{4,6},{5,7},{6,4},{7,5},{8,10},{9,11},{10,... | collective-permute-start | bytes 405512 | tf_op jit(solution)/shard_map/ppermute | solution.py:304
  68.6 5.1 %collective-permute-done.6 = f16[4,264,128]{2,1,0:T(8,128)(2,1)S(1)} collective-permute-done((f16[4,264,128]{2,1,0:T(8,128)(2,1)S(1)}, f16[4,264,128]{2,1,0:T(8,128)(2,1)S(1)}, u32[]{:S(2)}, u32[]{:S(2)}) %collective-permute-start.6) | collective-permute-done | bytes 270368 | tf_op jit(solution)/shard_map/ppermute | solution.py:301
  73.8 0.1 exponential_reduce_fusion
  73.9 0.2 multiply_add_fusion
  74.0 0.1 exponential_reduce_fusion.2
  74.2 2.0 %rotate.2 = (f32[6,2,128,128]{3,2,1,0:T(8,128)S(1)}, f32[1,2,128,128]{3,2,1,0:T(8,128)S(1)}, f32[1,2,128,128]{3,2,1,0:T(8,128)S(1)}) custom-call(s32[4,12]{1,0:T(4,128)S(1)} %pad_add_fusion.2.meta.slots, f32[4,2,128,128]{3,2,1,0:T(8,128)S(1)} %bitcast.22, bf16[2,4,128,128]{3,2,1,0:T(8,128)(2,1)S(1)} %copy-done, ...), custom_call_target="tpu_custom_call" | custom-call | flops 1 | bytes 1 | tf_op jit(solution)/shard_map/rotate/pallas_call | solution.py:206
  76.1 0.1 constant_dynamic-update-slice_fusion.3
  76.2 0.5 collective-permute-done.8
  76.7 0.1 fusion.26
  76.8 0.1 multiply_add_fusion.1
  76.9 2.2 %rotate.3 = (f32[2,2,128,128]{3,2,1,0:T(8,128)S(1)}, f32[1,2,128,128]{3,2,1,0:T(8,128)S(1)}, f32[1,2,128,128]{3,2,1,0:T(8,128)S(1)}) custom-call(s32[4,12]{1,0:T(4,128)S(1)} %pad_add_fusion.2.meta.slots, f32[2,2,128,128]{3,2,1,0:T(8,128)S(1)} %bitcast.23, bf16[2,4,128,128]{3,2,1,0:T(8,128)(2,1)S(1)} %copy-done, ...), custom_call_target="tpu_custom_call" | custom-call | flops 1 | bytes 1 | tf_op jit(solution)/shard_map/rotate/pallas_call | solution.py:206
  79.1 1.0 %collective-permute-start.12 = (f32[8,2,128,128]{3,2,1,0:T(8,128)S(1)}, f32[8,2,128,128]{3,2,1,0:T(8,128)S(1)}, u32[]{:S(2)}, u32[]{:S(2)}) collective-permute-start(f32[8,2,128,128]{3,2,1,0:T(8,128)S(1)} %constant_dynamic-update-slice_fusion.2.refs_0_), channel_id=1, source_target_pairs={{0,1},{1,0},{2,3},{3,2},{4,5},{5,4},{6,7},{7,6},{8,9},{9,8},{10,11... | collective-permute-start | bytes 3145736 | tf_op jit(solution)/shard_map/ppermute | solution.py:318
  80.1 1.1 %collective-permute-start.9 = (f32[2,2,128,128]{3,2,1,0:T(8,128)S(1)}, f32[2,2,128,128]{3,2,1,0:T(8,128)S(1)}, u32[]{:S(2)}, u32[]{:S(2)}) collective-permute-start(f32[2,2,128,128]{3,2,1,0:T(8,128)S(1)} %pad_maximum_fusion.1), channel_id=1, source_target_pairs={{12,0},{0,4},{4,8},{8,12},{28,16},{16,20},{20,24},{24,28},{44,32},... | collective-permute-start | bytes 786440 | tf_op jit(solution)/shard_map/ppermute | solution.py:316
  81.2 0.1 collective-permute-start.10
  81.3 9.1 %collective-permute-done.9 = f32[2,2,128,128]{3,2,1,0:T(8,128)S(1)} collective-permute-done((f32[2,2,128,128]{3,2,1,0:T(8,128)S(1)}, f32[2,2,128,128]{3,2,1,0:T(8,128)S(1)}, u32[]{:S(2)}, u32[]{:S(2)}) %collective-permute-start.9) | collective-permute-done | bytes 262176 | tf_op jit(solution)/shard_map/ppermute | solution.py:316
  90.4 0.6 collective-permute-done.10
  91.0 1.2 %collective-permute-start.11 = (f32[4,2,128,128]{3,2,1,0:T(8,128)S(1)}, f32[4,2,128,128]{3,2,1,0:T(8,128)S(1)}, u32[]{:S(2)}, u32[]{:S(2)}) collective-permute-start(f32[4,2,128,128]{3,2,1,0:T(8,128)S(1)} %constant_dynamic-update-slice_fusion.refs_0_), channel_id=1, source_target_pairs={{0,1},{1,0},{2,3},{3,2},{4,5},{5,4},{6,7},{7,6},{8,9},{9,8},{10,11... | collective-permute-start | bytes 1572872 | tf_op jit(solution)/shard_map/ppermute | solution.py:320
  92.2 0.0 collective-permute-done.12.refs_1_
  92.2 2.0 %place.2 = (f32[3,2,4,128,128]{4,3,2,1,0:T(8,128)}, f32[3,2,4,128,128]{4,3,2,1,0:T(8,128)}) custom-call(s32[4,12]{1,0:T(4,128)S(1)} %pad_add_fusion.2.meta.slots, f32[8,2,128,128]{3,2,1,0:T(8,128)S(1)} %constant_dynamic-update-slice_fusion.2.refs_0_, f32[8,2,128,128]{3,2,1,0:T(8,128)S(1)} %collective-permute-done.12.refs_1_), custom_call_target="tpu_custom_call" | custom-call | flops 1 | bytes 1 | tf_op jit(solution)/shard_map/place/pallas_call | solution.py:235
  94.2 1.6 %place.3 = (f32[3,2,4,128,128]{4,3,2,1,0:T(8,128)}, f32[3,2,4,128,128]{4,3,2,1,0:T(8,128)}) custom-call(s32[4,12]{1,0:T(4,128)S(1)} %pad_add_fusion.2.meta.slots, f32[4,2,128,128]{3,2,1,0:T(8,128)S(1)} %constant_dynamic-update-slice_fusion.refs_0_, ...), custom_call_target="tpu_custom_call", output_to_operand_aliasing={{0}: (3, {}), {1}: (4, {})} | custom-call | flops 1 | bytes 1 | tf_op jit(solution)/shard_map/place/pallas_call | solution.py:235
  (23 shorter events, 0.3 us)
Async XLA Ops:
  1.9 12.1 %copy-start.2 = (s32[256,3]{0,1:T(4,128)S(1)}, s32[256,3]{0,1:T(4,128)}, u32[]{:S(2)}) copy-start(s32[256,3]{0,1:T(4,128)} %param.6) | copy-start | bytes 9220
  1.9 12.2 %copy-start.1 = (s32[256,3,3]{0,2,1:T(4,128)S(1)}, s32[256,3,3]{0,2,1:T(4,128)}, u32[]{:S(2)}) copy-start(s32[256,3,3]{0,2,1:T(4,128)} %param.7) | copy-start | bytes 27652
  1.9 30.7 %collective-permute-start.2 = (bf16[2,272,1024]{2,1,0:T(8,128)(2,1)S(1)}, bf16[2,272,1024]{2,1,0:T(8,128)(2,1)S(1)}, u32[]{:S(2)}, u32[]{:S(2)}) collective-permute-start(bf16[2,272,1024]{2,1,0:T(8,128)(2,1)S(1)} %load.2.front.refs_0_), channel_id=1, source_target_pairs={{0,240},{4,244},{8,248},{12,252},{16,0},{20,4},{24,8},{28,12},{32,... | collective-permute-start | bytes 3342344 | tf_op jit(solution)/shard_map/ppermute | solution.py:267
  9.4 25.4 %collective-permute-start.1 = (bf16[2,272,1024]{2,1,0:T(8,128)(2,1)S(1)}, bf16[2,272,1024]{2,1,0:T(8,128)(2,1)}, u32[]{:S(2)}, u32[]{:S(2)}) collective-permute-start(bf16[2,272,1024]{2,1,0:T(8,128)(2,1)S(1)} %load.2.front.refs_0_), channel_id=1, source_target_pairs={{0,12},{4,0},{8,4},{12,8},{16,28},{20,16},{24,20},{28,24},{32,44},... | collective-permute-start | bytes 3342344 | tf_op jit(solution)/shard_map/ppermute | solution.py:268
  13.1 43.4 %collective-permute-start.5 = (bf16[2,272,1024]{2,1,0:T(8,128)(2,1)S(1)}, bf16[2,272,1024]{2,1,0:T(8,128)(2,1)}, u32[]{:S(2)}, u32[]{:S(2)}) collective-permute-start(bf16[2,272,1024]{2,1,0:T(8,128)(2,1)S(1)} %load.3.rear.refs_1_), channel_id=1, source_target_pairs={{0,240},{4,244},{8,248},{12,252},{16,0},{20,4},{24,8},{28,12},{32,... | collective-permute-start | bytes 3342344 | tf_op jit(solution)/shard_map/ppermute | solution.py:270
  13.4 45.3 %collective-permute-start.4 = (bf16[2,272,1024]{2,1,0:T(8,128)(2,1)S(1)}, bf16[2,272,1024]{2,1,0:T(8,128)(2,1)}, u32[]{:S(2)}, u32[]{:S(2)}) collective-permute-start(bf16[2,272,1024]{2,1,0:T(8,128)(2,1)S(1)} %load.3.rear.refs_1_), channel_id=1, source_target_pairs={{0,12},{4,0},{8,4},{12,8},{16,28},{20,16},{24,20},{28,24},{32,44},... | collective-permute-start | bytes 3342344 | tf_op jit(solution)/shard_map/ppermute | solution.py:271
  18.2 23.2 %collective-permute-start = (f32[2,2,128,128]{3,2,1,0:T(8,128)S(1)}, f32[2,2,128,128]{3,2,1,0:T(8,128)S(1)}, u32[]{:S(2)}, u32[]{:S(2)}) collective-permute-start(f32[2,2,128,128]{3,2,1,0:T(8,128)S(1)} %get-tuple-element.22), channel_id=1, source_target_pairs={{0,1},{1,0},{2,3},{3,2},{4,5},{5,4},{6,7},{7,6},{8,9},{9,8},{10,11... | collective-permute-start | bytes 786440 | tf_op jit(solution)/shard_map/ppermute | solution.py:296
  38.1 4.6 %collective-permute-start.3 = (f32[2,2,128,128]{3,2,1,0:T(8,128)S(1)}, f32[2,2,128,128]{3,2,1,0:T(8,128)S(1)}, u32[]{:S(2)}, u32[]{:S(2)}) collective-permute-start(f32[2,2,128,128]{3,2,1,0:T(8,128)S(1)} %get-tuple-element.24), channel_id=1, source_target_pairs={{0,1},{1,0},{2,3},{3,2},{4,5},{5,4},{6,7},{7,6},{8,9},{9,8},{10,11... | collective-permute-start | bytes 786440 | tf_op jit(solution)/shard_map/ppermute | solution.py:298
  62.3 4.7 %collective-permute-start.7 = (f32[2,2,128,128]{3,2,1,0:T(8,128)S(1)}, f32[2,2,128,128]{3,2,1,0:T(8,128)S(1)}, u32[]{:S(2)}, u32[]{:S(2)}) collective-permute-start(f32[2,2,128,128]{3,2,1,0:T(8,128)S(1)} %get-tuple-element.29), channel_id=1, source_target_pairs={{0,1},{1,0},{2,3},{3,2},{4,5},{5,4},{6,7},{7,6},{8,9},{9,8},{10,11... | collective-permute-start | bytes 786440 | tf_op jit(solution)/shard_map/ppermute | solution.py:303
  64.2 9.5 %collective-permute-start.6 = (f16[4,264,128]{2,1,0:T(8,128)(2,1)S(1)}, f16[4,264,128]{2,1,0:T(8,128)(2,1)S(1)}, u32[]{:S(2)}, u32[]{:S(2)}) collective-permute-start(f16[4,264,128]{2,1,0:T(8,128)(2,1)S(1)} %pad_maximum_fusion), channel_id=1, source_target_pairs={{0,2},{1,3},{2,0},{3,1},{4,6},{5,7},{6,4},{7,5},{8,10},{9,11},{10,... | collective-permute-start | bytes 811016 | tf_op jit(solution)/shard_map/ppermute | solution.py:301
  67.0 7.2 %copy-start = (bf16[2,4,128,128]{3,2,1,0:T(8,128)(2,1)S(1)}, bf16[2,4,128,128]{3,2,1,0:T(8,128)(2,1)}, u32[]{:S(2)}) copy-start(bf16[2,4,128,128]{3,2,1,0:T(8,128)(2,1)} %gauge.7) | copy-start | bytes 786436
  67.4 9.3 %collective-permute-start.8 = (f16[2,264,128]{2,1,0:T(8,128)(2,1)S(1)}, f16[2,264,128]{2,1,0:T(8,128)(2,1)S(1)}, u32[]{:S(2)}, u32[]{:S(2)}) collective-permute-start(f16[2,264,128]{2,1,0:T(8,128)(2,1)S(1)} %pad_maximum_fusion.3), channel_id=1, source_target_pairs={{0,2},{1,3},{2,0},{3,1},{4,6},{5,7},{6,4},{7,5},{8,10},{9,11},{10,... | collective-permute-start | bytes 405512 | tf_op jit(solution)/shard_map/ppermute | solution.py:304
  79.1 13.1 %collective-permute-start.12 = (f32[8,2,128,128]{3,2,1,0:T(8,128)S(1)}, f32[8,2,128,128]{3,2,1,0:T(8,128)S(1)}, u32[]{:S(2)}, u32[]{:S(2)}) collective-permute-start(f32[8,2,128,128]{3,2,1,0:T(8,128)S(1)} %constant_dynamic-update-slice_fusion.2.refs_0_), channel_id=1, source_target_pairs={{0,1},{1,0},{2,3},{3,2},{4,5},{5,4},{6,7},{7,6},{8,9},{9,8},{10,11... | collective-permute-start | bytes 3145736 | tf_op jit(solution)/shard_map/ppermute | solution.py:318
  80.1 10.3 %collective-permute-start.9 = (f32[2,2,128,128]{3,2,1,0:T(8,128)S(1)}, f32[2,2,128,128]{3,2,1,0:T(8,128)S(1)}, u32[]{:S(2)}, u32[]{:S(2)}) collective-permute-start(f32[2,2,128,128]{3,2,1,0:T(8,128)S(1)} %pad_maximum_fusion.1), channel_id=1, source_target_pairs={{12,0},{0,4},{4,8},{8,12},{28,16},{16,20},{20,24},{24,28},{44,32},... | collective-permute-start | bytes 786440 | tf_op jit(solution)/shard_map/ppermute | solution.py:316
  81.2 9.8 %collective-permute-start.10 = (f32[2,2,128,128]{3,2,1,0:T(8,128)S(1)}, f32[2,2,128,128]{3,2,1,0:T(8,128)S(1)}, u32[]{:S(2)}, u32[]{:S(2)}) collective-permute-start(f32[2,2,128,128]{3,2,1,0:T(8,128)S(1)} %pad_maximum_fusion.2), channel_id=1, source_target_pairs={{240,0},{244,4},{248,8},{252,12},{0,16},{4,20},{8,24},{12,28},{16,... | collective-permute-start | bytes 786440 | tf_op jit(solution)/shard_map/ppermute | solution.py:315
  91.0 3.2 %collective-permute-start.11 = (f32[4,2,128,128]{3,2,1,0:T(8,128)S(1)}, f32[4,2,128,128]{3,2,1,0:T(8,128)S(1)}, u32[]{:S(2)}, u32[]{:S(2)}) collective-permute-start(f32[4,2,128,128]{3,2,1,0:T(8,128)S(1)} %constant_dynamic-update-slice_fusion.refs_0_), channel_id=1, source_target_pairs={{0,1},{1,0},{2,3},{3,2},{4,5},{5,4},{6,7},{7,6},{8,9},{9,8},{10,11... | collective-permute-start | bytes 1572872 | tf_op jit(solution)/shard_map/ppermute | solution.py:320

commit v3 on v2

--- a/solution.py
+++ b/solution.py
@@ -93,13 +93,16 @@
     nb = (own[0].shape[1] - PACKED_ROWS) // 2
     points = own[0].shape[2]
 
-    def body(meta, cosines, sines, front, rear, *refs):
-        sources_in = refs[:2]
-        give, keep, left, phased = refs[2:]
-        for p in range(4):
-            slot, k = meta[0, base + p], meta[1, base + p]
-            source = sources_in[p % 2]
-            lefts, shifted = left.at[p % 2], phased.at[p % 2]
+    def body(meta, cosines, sines, front, rear, first, second, out, arrived, left, phased, sems):
+        copies = []
+        for p, source in enumerate((first, second)):
+            rows = pl.ds(pl.multiple_of(meta[0, base + p] * nb, nb), nb)
+            copies += [pltpu.make_async_copy(source.at[c, rows], arrived.at[p, c], sems.at[p, c]) for c in range(2)]
+        for copy in copies:
+            copy.start()
+        for p in range(2):
+            k = meta[1, base + p]
+            lefts, shifted = left.at[p], phased.at[p]
             for half, ref in enumerate((front, rear)):
 
                 @pl.when(k // 2 == half)
@@ -108,29 +111,33 @@
                     for c in range(2):
                         lefts[c * nb : (c + 1) * nb, :] = ref[c, pl.ds(start, nb), :]
 
-            row = directions[p % 2] * 4 + k
+            row = directions[p] * 4 + k
             cosine = cosines[pl.ds(row, 1), :]
             sine = sines[pl.ds(row, 1), :]
-            start = pl.multiple_of(slot * nb, nb)
-            source_re = source[0, pl.ds(start, nb), :].astype(F32)
-            source_im = source[1, pl.ds(start, nb), :].astype(F32)
+            for c in range(2):
+                copies[2 * p + c].wait()
+            source_re = arrived[p, 0].astype(F32)
+            source_im = arrived[p, 1].astype(F32)
             shifted[0:nb, :] = (cosine * source_re + sine * source_im).astype(BF16)
             shifted[nb:, :] = (cosine * source_im - sine * source_re).astype(BF16)
             full = lax.dot_general(lefts[...], shifted[...], CONTRACT_LAST, preferred_element_type=F32)
-            out = give if p < 2 else keep
-            out[p % 2, 0] = full[:nb, :nb] + full[nb:, nb:]
-            out[p % 2, 1] = full[:nb, nb:] - full[nb:, :nb]
-
-    half_out = VMEM((2, 2, nb, nb), F32)
+            out[p, 0] = full[:nb, :nb] + full[nb:, nb:]
+            out[p, 1] = full[:nb, nb:] - full[nb:, :nb]
+
     return pl.pallas_call(
         body,
         name="correlate",
-        out_shape=(half_out, half_out),
-        in_specs=specs(pltpu.SMEM, *[VMEM] * 6),
-        out_specs=tuple(specs(VMEM, VMEM)),
-        scratch_shapes=[VMEM((2, 2 * nb, points), BF16), VMEM((2, 2 * nb, points), BF16)],
+        out_shape=VMEM((2, 2, nb, nb), F32),
+        in_specs=specs(pltpu.SMEM, *[VMEM] * 4, pl.ANY, pl.ANY),
+        out_specs=specs(VMEM)[0],
+        scratch_shapes=[
+            VMEM((2, 2, nb, points), BF16),
+            VMEM((2, 2 * nb, points), BF16),
+            VMEM((2, 2 * nb, points), BF16),
+            pltpu.SemaphoreType.DMA((2, 2)),
+        ],
         **small(8),
-    )(meta, *vmem(cosines, sines, *own, *sources))
+    )(meta, *vmem(cosines, sines, *own), *sources)
 
 
 def split_parts(values):
@@ -292,18 +299,21 @@
     angles = jnp.concatenate([phase_angles(my_shift[:, b, :], b, counts, fractions) for b in range(3)])
     cosines, sines = jnp.cos(angles), jnp.sin(angles)
 
-    give, keep = correlate(meta, 0, (0, 0), cosines, sines, own, own)
-    got = lax.ppermute(give, "ga", sibling)
-    give_front, keep_front = correlate(meta, 4, (1, 2), cosines, sines, own, (beside_front, beyond_front))
-    got_front = lax.ppermute(give_front, "ga", sibling)
+    def halves(base, directions, sources):
+        give = correlate(meta, base, directions, cosines, sines, own, sources)
+        got = lax.ppermute(give, "ga", sibling)
+        return got, correlate(meta, base + 2, directions, cosines, sines, own, sources)
+
+    got, keep = halves(0, (0, 0), own)
+    got_front, keep_front = halves(4, (1, 2), (beside_front, beyond_front))
     coded = encode(jnp.concatenate([keep + got, keep_front + got_front], axis=0))
+    other = lax.ppermute(coded, "ga", across)
     coded, beside_rear, beyond_rear = lax.optimization_barrier((coded, beside_rear, beyond_rear))
-    other = lax.ppermute(coded, "ga", across)
-    give, keep = correlate(meta, 8, (1, 2), cosines, sines, own, (beside_rear, beyond_rear))
-    coded_rear = encode(keep + lax.ppermute(give, "ga", sibling))
+    got, keep = halves(8, (1, 2), (beside_rear, beyond_rear))
+    other, got = lax.optimization_barrier((other, got))
+    coded_rear = encode(keep + got)
     other_rear = lax.ppermute(coded_rear, "ga", across)
 
-    other, coded_rear = lax.optimization_barrier((other, coded_rear))
     first, adj_x, adj_y = rotate(
         meta, (2, 3, 6, 7), decode(coded) + decode(other), gauge, (beside_front, beyond_front), (None, None, 0, 1),
         [[(0, 0), (1, 0), (2, 0), (3, 0), (0, 1), (1, 1)], [(2, 1)], [(3, 1)]],
@@ -312,17 +322,19 @@
         meta, (10, 11), decode(coded_rear) + decode(other_rear), gauge, (beside_rear, beyond_rear), (0, 1),
         [[(0, 0), (1, 0)], [(0, 1)], [(1, 1)]],
     )
-    adj_y = lax.ppermute(jnp.concatenate([adj_y, adj_y_rear], axis=0), "ka", outer_ahead)
-    adj_x = lax.ppermute(jnp.concatenate([adj_x, adj_x_rear], axis=0), "ka", ring_ahead)
+    adj_y = lax.ppermute(encode(jnp.concatenate([adj_y, adj_y_rear], axis=0)), "ka", outer_ahead)
+    adj_x = lax.ppermute(encode(jnp.concatenate([adj_x, adj_x_rear], axis=0)), "ka", ring_ahead)
     fwd = jnp.concatenate([first, last], axis=0)
     fwd_sib = lax.ppermute(fwd, "ga", sibling)
-    adj = jnp.concatenate([adj_x, adj_y], axis=0)
+    adj = lax.optimization_barrier(jnp.concatenate([adj_x, adj_y], axis=0))
     adj_sib = lax.ppermute(adj, "ga", sibling)
     targets = [
         [(0, 0, i), (0, 0, i + 1), (0, 1, i + 4), (0, 2, i + 5), (1, 0, i), (1, 0, i + 1), (0, 1, i + 8), (0, 2, i + 9)]
         for i in (2, 0)
     ]
     outs = place(targets, meta, (fwd, fwd_sib), None)
+    adj_sib, *outs = lax.optimization_barrier((adj_sib, *outs))
+    adj, adj_sib = decode(adj), decode(adj_sib)
     targets = [[(1, 1, i + 4), (1, 1, i + 8), (1, 2, i + 5), (1, 2, i + 9)] for i in (2, 0)]
     return tuple(place(targets, meta, (adj, adj_sib), outs))
 

time: 96.4 us -> 90.5 us (0.939)
  waiting for transfers between devices: 46.6 us -> 34.8 us
  Pallas kernels: 19.6 us -> 23 us
  other arithmetic: 2.56 us -> 3.6 us
    ppermute x1, waiting for transfers between devices: 13.4 us -> 6.31 us  [shards(): beyond_rear = lax.ppermute(rear, 'ka', outer_back)]
    ppermute x1, waiting for transfers between devices: 2.16 us -> 9.26 us  [shards(): beside_front = lax.ppermute(front, 'ka', ring_back)]
    ppermute x1, waiting for transfers between devices: 12.5 us -> 6.27 us  [shards(): beyond_front = lax.ppermute(front, 'ka', outer_back)]
    ppermute x1, waiting for transfers between devices: 5.12 us -> 0.01 us  [shards(): other = lax.ppermute(coded, 'ga', across)]
    ppermute x5, waiting for transfers between devices: 10.8 us -> 6.41 us  [the longest x1 6.27 us: shards(): lax.ppermute(encode(jnp.concatenate([adj_y, adj_y_rear], axis=0)), 'ka',...]
    pallas_call x3 -> x6, Pallas kernels: 9.43 us -> 12.8 us  [correlate(): pl.pallas_call(body, name='correlate', out_shape=VMEM((2, 2, nb, nb), F32...]
    ppermute x1, waiting for transfers between devices: 2.16 us -> 4.95 us  [shards(): beside_rear = lax.ppermute(rear, 'ka', ring_back)]
    ppermute x1, starting transfers between devices: 1.28 us -> 2.89 us  [shards(): other_rear = lax.ppermute(coded_rear, 'ga', across)]
  transfers between devices with their start and end apart: 13 -> 13, of which waited for: 9 -> 7; matrix products, arithmetic and copies ran while one was open for 3% -> 4% of each run, Pallas kernels for 11% -> 20%
where the time goes in v3:
time: 90.5 us; the launch traced here: 89.6 us
  waiting for transfers between devices  34.8 us (38%)
  starting transfers between devices  26 us (29%)
  Pallas kernels  23 us (25%)
  other arithmetic  3.6 us (4%)
  between operations  1.14 us (1%)
  local copies, waits for them, and re-layouts  1 us (1%)
    pallas_call x6, Pallas kernels, correlate(): pl.pallas_call(body, name='correlate', out_shape=VMEM((2, 2, nb, nb), F32...  12.8 us
    ppermute x1, waiting for transfers between devices, shards(): beside_front = lax.ppermute(front, 'ka', ring_back)  9.26 us
    ppermute x3, starting transfers between devices, halves(): got = lax.ppermute(give, 'ga', sibling)  7.25 us
    ppermute x1, starting transfers between devices, shards(): beyond_front = lax.ppermute(front, 'ka', outer_back)  6.59 us
    ppermute x1, waiting for transfers between devices, shards(): beyond_rear = lax.ppermute(rear, 'ka', outer_back)  6.31 us
    ppermute x1, waiting for transfers between devices, shards(): lax.ppermute(encode(jnp.concatenate([adj_y, adj_y_rear], axis=0)), 'ka',...  6.27 us
    ppermute x1, waiting for transfers between devices, shards(): beyond_front = lax.ppermute(front, 'ka', outer_back)  6.27 us
    ppermute x1, waiting for transfers between devices, shards(): beside_rear = lax.ppermute(rear, 'ka', ring_back)  4.95 us
  transfers between devices with their start and end apart: 13, of which 7 were waited for; matrix products, arithmetic and copies ran while one was open for 4% of the time, Pallas kernels for 20%

profile of v3, /device:TPU:1, one launch (start us, length us, event | category | flops | bytes accessed | tf_op | source)
XLA Modules:
  0.0 89.6 jit_solution(15799612788563555080)
XLA Ops:
  0.6 1.2 %load.2.front.first = bf16[2,272,1024]{2,1,0:T(8,128)(2,1)S(1)} custom-call(s32[1]{0:T(128)} %bitcast.1.core, bf16[2,4,128,1024]{3,2,1,0:T(8,128)(2,1)} %orbitals.3, bf16[2,4,128,128]{3,2,1,0:T(8,128)(2,1)} %gauge.7), custom_call_target="tpu_custom_call" | custom-call | flops 1 | bytes 1 | tf_op jit(solution)/shard_map/load/pallas_call | solution.py:81
  1.9 3.4 %collective-permute-start.1 = (bf16[2,272,1024]{2,1,0:T(8,128)(2,1)S(1)}, bf16[2,272,1024]{2,1,0:T(8,128)(2,1)S(1)}, u32[]{:S(2)}, u32[]{:S(2)}) collective-permute-start(bf16[2,272,1024]{2,1,0:T(8,128)(2,1)S(1)} %load.2.front.first), channel_id=1, source_target_pairs={{0,12},{4,0},{8,4},{12,8},{16,28},{20,16},{24,20},{28,24},{32,44},... | collective-permute-start | bytes 3342344 | tf_op jit(solution)/shard_map/ppermute | solution.py:275
  5.3 6.6 %collective-permute-start.2 = (bf16[2,272,1024]{2,1,0:T(8,128)(2,1)S(1)}, bf16[2,272,1024]{2,1,0:T(8,128)(2,1)}, u32[]{:S(2)}, u32[]{:S(2)}) collective-permute-start(bf16[2,272,1024]{2,1,0:T(8,128)(2,1)S(1)} %load.2.front.first), channel_id=1, source_target_pairs={{0,240},{4,244},{8,248},{12,252},{16,0},{20,4},{24,8},{28,12},{32,... | collective-permute-start | bytes 3342344 | tf_op jit(solution)/shard_map/ppermute | solution.py:274
  11.9 1.2 %load.3.rear.second = bf16[2,272,1024]{2,1,0:T(8,128)(2,1)S(1)} custom-call(s32[1]{0:T(128)} %bitcast.1.core, bf16[2,4,128,1024]{3,2,1,0:T(8,128)(2,1)} %orbitals.3, bf16[2,4,128,128]{3,2,1,0:T(8,128)(2,1)} %gauge.7), custom_call_target="tpu_custom_call" | custom-call | flops 1 | bytes 1 | tf_op jit(solution)/shard_map/load/pallas_call | solution.py:81
  13.1 0.6 collective-permute-start.4
  13.7 0.2 collective-permute-start.5
  13.9 0.1 broadcast_add_fusion
  14.0 0.1 add_select_fusion.4
  14.2 0.1 copy.42
  14.3 0.2 add_reduce_fusion.2
  14.5 0.1 copy.44
  14.6 0.1 copy.43
  14.6 0.3 convert_reduce_fusion.1
  14.9 0.1 select_reduce_fusion.1
  15.0 0.1 add_multiply_fusion.2
  15.1 0.1 concatenate.67
  15.2 0.1 stack_tile.4
  15.3 0.1 select_n.116
  15.4 0.3 fusion.6
  15.7 1.7 %correlate.7 = f32[2,2,128,128]{3,2,1,0:T(8,128)S(1)} custom-call(s32[4,12]{1,0:T(4,128)S(1)} %pad_add_fusion.2.meta.slots, f32[12,1024]{1,0:T(8,128)S(1)} %get-tuple-element.52.cosines, f32[12,1024]{1,0:T(8,128)S(1)} %get-tuple-element.51.sines, bf16[2,272,1024]{2,1,0:T(8,128)(2,1)S(1)} %load.2.front.first, bf16[2,272,1024]{2,1,0:T(8,128)(2,1)S(1)} %load.3.rear.second, ...), custom_call_target="tpu_custom_call" | custom-call | flops 1 | bytes 1 | tf_op jit(solution)/shard_map/correlate/pallas_call | solution.py:127
  17.4 1.9 %collective-permute-start = (f32[2,2,128,128]{3,2,1,0:T(8,128)S(1)}, f32[2,2,128,128]{3,2,1,0:T(8,128)S(1)}, u32[]{:S(2)}, u32[]{:S(2)}) collective-permute-start(f32[2,2,128,128]{3,2,1,0:T(8,128)S(1)} %correlate.7), channel_id=1, source_target_pairs={{0,1},{1,0},{2,3},{3,2},{4,5},{5,4},{6,7},{7,6},{8,9},{9,8},{10,11... | collective-permute-start | bytes 786440 | tf_op jit(solution)/shard_map/ppermute | solution.py:304
  19.3 9.3 %collective-permute-done.1.first.refs_0_ = bf16[2,272,1024]{2,1,0:T(8,128)(2,1)S(1)} collective-permute-done((bf16[2,272,1024]{2,1,0:T(8,128)(2,1)S(1)}, bf16[2,272,1024]{2,1,0:T(8,128)(2,1)S(1)}, u32[]{:S(2)}, u32[]{:S(2)}) %collective-permute-start.1) | collective-permute-done | bytes 1114144 | tf_op jit(solution)/shard_map/ppermute | solution.py:275
  28.5 6.3 %collective-permute-done.2.second.refs_1_ = bf16[2,272,1024]{2,1,0:T(8,128)(2,1)} collective-permute-done((bf16[2,272,1024]{2,1,0:T(8,128)(2,1)S(1)}, bf16[2,272,1024]{2,1,0:T(8,128)(2,1)}, u32[]{:S(2)}, u32[]{:S(2)}) %collective-permute-start.2) | collective-permute-done | bytes 1114144 | tf_op jit(solution)/shard_map/ppermute | solution.py:274
  34.8 2.1 %correlate.9 = f32[2,2,128,128]{3,2,1,0:T(8,128)S(1)} custom-call(s32[4,12]{1,0:T(4,128)S(1)} %pad_add_fusion.2.meta.slots, f32[12,1024]{1,0:T(8,128)S(1)} %get-tuple-element.52.cosines, f32[12,1024]{1,0:T(8,128)S(1)} %get-tuple-element.51.sines, bf16[2,272,1024]{2,1,0:T(8,128)(2,1)S(1)} %load.2.front.first, bf16[2,272,1024]{2,1,0:T(8,128)(2,1)S(1)} %load.3.rear.second, ...), custom_call_target="tpu_custom_call" | custom-call | flops 1 | bytes 1 | tf_op jit(solution)/shard_map/correlate/pallas_call | solution.py:127
  36.9 3.4 %collective-permute-start.3 = (f32[2,2,128,128]{3,2,1,0:T(8,128)S(1)}, f32[2,2,128,128]{3,2,1,0:T(8,128)S(1)}, u32[]{:S(2)}, u32[]{:S(2)}) collective-permute-start(f32[2,2,128,128]{3,2,1,0:T(8,128)S(1)} %correlate.9), channel_id=1, source_target_pairs={{0,1},{1,0},{2,3},{3,2},{4,5},{5,4},{6,7},{7,6},{8,9},{9,8},{10,11... | collective-permute-start | bytes 786440 | tf_op jit(solution)/shard_map/ppermute | solution.py:304
  40.4 1.7 %correlate.6 = f32[2,2,128,128]{3,2,1,0:T(8,128)S(1)} custom-call(s32[4,12]{1,0:T(4,128)S(1)} %pad_add_fusion.2.meta.slots, f32[12,1024]{1,0:T(8,128)S(1)} %get-tuple-element.52.cosines, f32[12,1024]{1,0:T(8,128)S(1)} %get-tuple-element.51.sines, bf16[2,272,1024]{2,1,0:T(8,128)(2,1)S(1)} %load.2.front.first, bf16[2,272,1024]{2,1,0:T(8,128)(2,1)S(1)} %load.3.rear.second, ...), custom_call_target="tpu_custom_call" | custom-call | flops 1 | bytes 1 | tf_op jit(solution)/shard_map/correlate/pallas_call | solution.py:127
  42.1 2.1 %correlate.8 = f32[2,2,128,128]{3,2,1,0:T(8,128)S(1)} custom-call(s32[4,12]{1,0:T(4,128)S(1)} %pad_add_fusion.2.meta.slots, f32[12,1024]{1,0:T(8,128)S(1)} %get-tuple-element.52.cosines, f32[12,1024]{1,0:T(8,128)S(1)} %get-tuple-element.51.sines, bf16[2,272,1024]{2,1,0:T(8,128)(2,1)S(1)} %load.2.front.first, bf16[2,272,1024]{2,1,0:T(8,128)(2,1)S(1)} %load.3.rear.second, ...), custom_call_target="tpu_custom_call" | custom-call | flops 1 | bytes 1 | tf_op jit(solution)/shard_map/correlate/pallas_call | solution.py:127
  44.3 0.1 fusion.1
  44.4 0.1 fusion
  44.7 0.1 pad_maximum_fusion
  44.7 2.7 %collective-permute-start.6 = (f16[4,264,128]{2,1,0:T(8,128)(2,1)S(1)}, f16[4,264,128]{2,1,0:T(8,128)(2,1)S(1)}, u32[]{:S(2)}, u32[]{:S(2)}) collective-permute-start(f16[4,264,128]{2,1,0:T(8,128)(2,1)S(1)} %pad_maximum_fusion), channel_id=1, source_target_pairs={{0,2},{1,3},{2,0},{3,1},{4,6},{5,7},{6,4},{7,5},{8,10},{9,11},{10,... | collective-permute-start | bytes 811016 | tf_op jit(solution)/shard_map/ppermute | solution.py:310
  47.4 5.0 %collective-permute-done.4.first.refs_0_ = bf16[2,272,1024]{2,1,0:T(8,128)(2,1)} collective-permute-done((bf16[2,272,1024]{2,1,0:T(8,128)(2,1)S(1)}, bf16[2,272,1024]{2,1,0:T(8,128)(2,1)}, u32[]{:S(2)}, u32[]{:S(2)}) %collective-permute-start.4) | collective-permute-done | bytes 1114144 | tf_op jit(solution)/shard_map/ppermute | solution.py:278
  52.4 6.3 %collective-permute-done.5.second.refs_1_ = bf16[2,272,1024]{2,1,0:T(8,128)(2,1)} collective-permute-done((bf16[2,272,1024]{2,1,0:T(8,128)(2,1)S(1)}, bf16[2,272,1024]{2,1,0:T(8,128)(2,1)}, u32[]{:S(2)}, u32[]{:S(2)}) %collective-permute-start.5) | collective-permute-done | bytes 1114144 | tf_op jit(solution)/shard_map/ppermute | solution.py:277
  58.7 2.6 %correlate.10 = f32[2,2,128,128]{3,2,1,0:T(8,128)S(1)} custom-call(s32[4,12]{1,0:T(4,128)S(1)} %pad_add_fusion.2.meta.slots, f32[12,1024]{1,0:T(8,128)S(1)} %get-tuple-element.52.cosines, f32[12,1024]{1,0:T(8,128)S(1)} %get-tuple-element.51.sines, bf16[2,272,1024]{2,1,0:T(8,128)(2,1)S(1)} %load.2.front.first, bf16[2,272,1024]{2,1,0:T(8,128)(2,1)S(1)} %load.3.rear.second, ...), custom_call_target="tpu_custom_call" | custom-call | flops 1 | bytes 1 | tf_op jit(solution)/shard_map/correlate/pallas_call | solution.py:127
  61.3 1.9 %collective-permute-start.7 = (f32[2,2,128,128]{3,2,1,0:T(8,128)S(1)}, f32[2,2,128,128]{3,2,1,0:T(8,128)S(1)}, u32[]{:S(2)}, u32[]{:S(2)}) collective-permute-start(f32[2,2,128,128]{3,2,1,0:T(8,128)S(1)} %correlate.10), channel_id=1, source_target_pairs={{0,1},{1,0},{2,3},{3,2},{4,5},{5,4},{6,7},{7,6},{8,9},{9,8},{10,11... | collective-permute-start | bytes 786440 | tf_op jit(solution)/shard_map/ppermute | solution.py:304
  63.2 2.6 %correlate.11 = f32[2,2,128,128]{3,2,1,0:T(8,128)S(1)} custom-call(s32[4,12]{1,0:T(4,128)S(1)} %pad_add_fusion.2.meta.slots, f32[12,1024]{1,0:T(8,128)S(1)} %get-tuple-element.52.cosines, f32[12,1024]{1,0:T(8,128)S(1)} %get-tuple-element.51.sines, bf16[2,272,1024]{2,1,0:T(8,128)(2,1)S(1)} %load.2.front.first, bf16[2,272,1024]{2,1,0:T(8,128)(2,1)S(1)} %load.3.rear.second, ...), custom_call_target="tpu_custom_call" | custom-call | flops 1 | bytes 1 | tf_op jit(solution)/shard_map/correlate/pallas_call | solution.py:127
  65.8 0.1 exponential_reduce_fusion.2
  66.0 0.1 abs_reduce_fusion
  66.1 0.1 multiply_convert_fusion
  66.4 2.9 %collective-permute-start.8 = (f16[2,264,128]{2,1,0:T(8,128)(2,1)S(1)}, f16[2,264,128]{2,1,0:T(8,128)(2,1)S(1)}, u32[]{:S(2)}, u32[]{:S(2)}) collective-permute-start(f16[2,264,128]{2,1,0:T(8,128)(2,1)S(1)} %pad_maximum_fusion.2), channel_id=1, source_target_pairs={{0,2},{1,3},{2,0},{3,1},{4,6},{5,7},{6,4},{7,5},{8,10},{9,11},{10,... | collective-permute-start | bytes 405512 | tf_op jit(solution)/shard_map/ppermute | solution.py:315
  69.2 0.1 exponential_reduce_fusion.1
  69.4 0.2 multiply_add_fusion
  69.5 0.1 fusion.37
  69.6 2.0 %rotate.2 = (f32[6,2,128,128]{3,2,1,0:T(8,128)S(1)}, f32[1,2,128,128]{3,2,1,0:T(8,128)S(1)}, f32[1,2,128,128]{3,2,1,0:T(8,128)S(1)}) custom-call(s32[4,12]{1,0:T(4,128)S(1)} %pad_add_fusion.2.meta.slots, f32[4,2,128,128]{3,2,1,0:T(8,128)S(1)} %bitcast.28, bf16[2,4,128,128]{3,2,1,0:T(8,128)(2,1)S(1)} %copy-done, ...), custom_call_target="tpu_custom_call" | custom-call | flops 1 | bytes 1 | tf_op jit(solution)/shard_map/rotate/pallas_call | solution.py:213
  71.7 1.6 %collective-permute-done.8 = f16[2,264,128]{2,1,0:T(8,128)(2,1)S(1)} collective-permute-done((f16[2,264,128]{2,1,0:T(8,128)(2,1)S(1)}, f16[2,264,128]{2,1,0:T(8,128)(2,1)S(1)}, u32[]{:S(2)}, u32[]{:S(2)}) %collective-permute-start.8) | collective-permute-done | bytes 135200 | tf_op jit(solution)/shard_map/ppermute | solution.py:315
  73.3 0.1 fusion.38
  73.4 0.1 multiply_add_fusion.1
  73.5 2.2 %rotate.3 = (f32[2,2,128,128]{3,2,1,0:T(8,128)S(1)}, f32[1,2,128,128]{3,2,1,0:T(8,128)S(1)}, f32[1,2,128,128]{3,2,1,0:T(8,128)S(1)}) custom-call(s32[4,12]{1,0:T(4,128)S(1)} %pad_add_fusion.2.meta.slots, f32[2,2,128,128]{3,2,1,0:T(8,128)S(1)} %bitcast.31, bf16[2,4,128,128]{3,2,1,0:T(8,128)(2,1)S(1)} %copy-done, ...), custom_call_target="tpu_custom_call" | custom-call | flops 1 | bytes 1 | tf_op jit(solution)/shard_map/rotate/pallas_call | solution.py:213
  75.7 0.1 fusion.5
  75.8 0.1 fusion.4
  76.1 0.1 collective-permute-start.10
  76.2 0.9 %collective-permute-start.12 = (f32[8,2,128,128]{3,2,1,0:T(8,128)S(1)}, f32[8,2,128,128]{3,2,1,0:T(8,128)S(1)}, u32[]{:S(2)}, u32[]{:S(2)}) collective-permute-start(f32[8,2,128,128]{3,2,1,0:T(8,128)S(1)} %constant_dynamic-update-slice_fusion.refs_0_), channel_id=1, source_target_pairs={{0,1},{1,0},{2,3},{3,2},{4,5},{5,4},{6,7},{7,6},{8,9},{9,8},{10,11... | collective-permute-start | bytes 3145736 | tf_op jit(solution)/shard_map/ppermute | solution.py:328
  77.1 0.1 fusion.3
  77.2 0.1 fusion.2
  77.4 0.1 collective-permute-start.9
  77.5 6.3 %collective-permute-done.10 = f16[2,264,128]{2,1,0:T(8,128)(2,1)S(1)} collective-permute-done((f16[2,264,128]{2,1,0:T(8,128)(2,1)S(1)}, f16[2,264,128]{2,1,0:T(8,128)(2,1)S(1)}, u32[]{:S(2)}, u32[]{:S(2)}) %collective-permute-start.10) | collective-permute-done | bytes 135200 | tf_op jit(solution)/shard_map/ppermute | solution.py:325
  83.8 0.1 collective-permute-done.9
  84.0 1.3 %collective-permute-start.11 = (f16[4,264,128]{2,1,0:T(8,128)(2,1)S(1)}, f16[4,264,128]{2,1,0:T(8,128)(2,1)S(1)}, u32[]{:S(2)}, u32[]{:S(2)}) collective-permute-start(f16[4,264,128]{2,1,0:T(8,128)(2,1)S(1)} %pad_maximum_fusion.1), channel_id=1, source_target_pairs={{0,1},{1,0},{2,3},{3,2},{4,5},{5,4},{6,7},{7,6},{8,9},{9,8},{10,11... | collective-permute-start | bytes 811016 | tf_op jit(solution)/shard_map/ppermute | solution.py:330
  85.3 0.1 fusion.30
  85.5 0.1 convert_multiply_fusion.1
  85.6 2.0 %place.2 = (f32[3,2,4,128,128]{4,3,2,1,0:T(8,128)}, f32[3,2,4,128,128]{4,3,2,1,0:T(8,128)}) custom-call(s32[4,12]{1,0:T(4,128)S(1)} %pad_add_fusion.2.meta.slots, f32[8,2,128,128]{3,2,1,0:T(8,128)S(1)} %constant_dynamic-update-slice_fusion.refs_0_, f32[8,2,128,128]{3,2,1,0:T(8,128)S(1)} %collective-permute-done.12.refs_1_), custom_call_target="tpu_custom_call" | custom-call | flops 1 | bytes 1 | tf_op jit(solution)/shard_map/place/pallas_call | solution.py:242
  87.6 0.1 exponential_reduce_fusion
  87.7 0.1 convert_multiply_fusion
  87.8 1.6 %place.3 = (f32[3,2,4,128,128]{4,3,2,1,0:T(8,128)}, f32[3,2,4,128,128]{4,3,2,1,0:T(8,128)}) custom-call(s32[4,12]{1,0:T(4,128)S(1)} %pad_add_fusion.2.meta.slots, f32[4,2,128,128]{3,2,1,0:T(8,128)S(1)} %bitcast.29, f32[4,2,128,128]{3,2,1,0:T(8,128)S(1)} %bitcast.30, ...), custom_call_target="tpu_custom_call", output_to_operand_aliasing={{0}: (3, {}), {1}: (4, {})} | custom-call | flops 1 | bytes 1 | tf_op jit(solution)/shard_map/place/pallas_call | solution.py:242
  (37 shorter events, 0.9 us)
Async XLA Ops:
  1.9 12.1 %copy-start.2 = (s32[256,3]{0,1:T(4,128)S(1)}, s32[256,3]{0,1:T(4,128)}, u32[]{:S(2)}) copy-start(s32[256,3]{0,1:T(4,128)} %param.6) | copy-start | bytes 9220
  1.9 12.2 %copy-start.1 = (s32[256,3,3]{0,2,1:T(4,128)S(1)}, s32[256,3,3]{0,2,1:T(4,128)}, u32[]{:S(2)}) copy-start(s32[256,3,3]{0,2,1:T(4,128)} %param.7) | copy-start | bytes 27652
  1.9 26.6 %collective-permute-start.1 = (bf16[2,272,1024]{2,1,0:T(8,128)(2,1)S(1)}, bf16[2,272,1024]{2,1,0:T(8,128)(2,1)S(1)}, u32[]{:S(2)}, u32[]{:S(2)}) collective-permute-start(bf16[2,272,1024]{2,1,0:T(8,128)(2,1)S(1)} %load.2.front.first), channel_id=1, source_target_pairs={{0,12},{4,0},{8,4},{12,8},{16,28},{20,16},{24,20},{28,24},{32,44},... | collective-permute-start | bytes 3342344 | tf_op jit(solution)/shard_map/ppermute | solution.py:275
  5.3 29.5 %collective-permute-start.2 = (bf16[2,272,1024]{2,1,0:T(8,128)(2,1)S(1)}, bf16[2,272,1024]{2,1,0:T(8,128)(2,1)}, u32[]{:S(2)}, u32[]{:S(2)}) collective-permute-start(bf16[2,272,1024]{2,1,0:T(8,128)(2,1)S(1)} %load.2.front.first), channel_id=1, source_target_pairs={{0,240},{4,244},{8,248},{12,252},{16,0},{20,4},{24,8},{28,12},{32,... | collective-permute-start | bytes 3342344 | tf_op jit(solution)/shard_map/ppermute | solution.py:274
  13.1 39.3 %collective-permute-start.4 = (bf16[2,272,1024]{2,1,0:T(8,128)(2,1)S(1)}, bf16[2,272,1024]{2,1,0:T(8,128)(2,1)}, u32[]{:S(2)}, u32[]{:S(2)}) collective-permute-start(bf16[2,272,1024]{2,1,0:T(8,128)(2,1)S(1)} %load.3.rear.second), channel_id=1, source_target_pairs={{0,12},{4,0},{8,4},{12,8},{16,28},{20,16},{24,20},{28,24},{32,44},... | collective-permute-start | bytes 3342344 | tf_op jit(solution)/shard_map/ppermute | solution.py:278
  13.7 45.0 %collective-permute-start.5 = (bf16[2,272,1024]{2,1,0:T(8,128)(2,1)S(1)}, bf16[2,272,1024]{2,1,0:T(8,128)(2,1)}, u32[]{:S(2)}, u32[]{:S(2)}) collective-permute-start(bf16[2,272,1024]{2,1,0:T(8,128)(2,1)S(1)} %load.3.rear.second), channel_id=1, source_target_pairs={{0,240},{4,244},{8,248},{12,252},{16,0},{20,4},{24,8},{28,12},{32,... | collective-permute-start | bytes 3342344 | tf_op jit(solution)/shard_map/ppermute | solution.py:277
  17.4 24.7 %collective-permute-start = (f32[2,2,128,128]{3,2,1,0:T(8,128)S(1)}, f32[2,2,128,128]{3,2,1,0:T(8,128)S(1)}, u32[]{:S(2)}, u32[]{:S(2)}) collective-permute-start(f32[2,2,128,128]{3,2,1,0:T(8,128)S(1)} %correlate.7), channel_id=1, source_target_pairs={{0,1},{1,0},{2,3},{3,2},{4,5},{5,4},{6,7},{7,6},{8,9},{9,8},{10,11... | collective-permute-start | bytes 786440 | tf_op jit(solution)/shard_map/ppermute | solution.py:304
  36.9 7.3 %collective-permute-start.3 = (f32[2,2,128,128]{3,2,1,0:T(8,128)S(1)}, f32[2,2,128,128]{3,2,1,0:T(8,128)S(1)}, u32[]{:S(2)}, u32[]{:S(2)}) collective-permute-start(f32[2,2,128,128]{3,2,1,0:T(8,128)S(1)} %correlate.9), channel_id=1, source_target_pairs={{0,1},{1,0},{2,3},{3,2},{4,5},{5,4},{6,7},{7,6},{8,9},{9,8},{10,11... | collective-permute-start | bytes 786440 | tf_op jit(solution)/shard_map/ppermute | solution.py:304
  44.7 21.2 %collective-permute-start.6 = (f16[4,264,128]{2,1,0:T(8,128)(2,1)S(1)}, f16[4,264,128]{2,1,0:T(8,128)(2,1)S(1)}, u32[]{:S(2)}, u32[]{:S(2)}) collective-permute-start(f16[4,264,128]{2,1,0:T(8,128)(2,1)S(1)} %pad_maximum_fusion), channel_id=1, source_target_pairs={{0,2},{1,3},{2,0},{3,1},{4,6},{5,7},{6,4},{7,5},{8,10},{9,11},{10,... | collective-permute-start | bytes 811016 | tf_op jit(solution)/shard_map/ppermute | solution.py:310
  61.3 4.6 %collective-permute-start.7 = (f32[2,2,128,128]{3,2,1,0:T(8,128)S(1)}, f32[2,2,128,128]{3,2,1,0:T(8,128)S(1)}, u32[]{:S(2)}, u32[]{:S(2)}) collective-permute-start(f32[2,2,128,128]{3,2,1,0:T(8,128)S(1)} %correlate.10), channel_id=1, source_target_pairs={{0,1},{1,0},{2,3},{3,2},{4,5},{5,4},{6,7},{7,6},{8,9},{9,8},{10,11... | collective-permute-start | bytes 786440 | tf_op jit(solution)/shard_map/ppermute | solution.py:304
  66.0 3.7 %copy-start = (bf16[2,4,128,128]{3,2,1,0:T(8,128)(2,1)S(1)}, bf16[2,4,128,128]{3,2,1,0:T(8,128)(2,1)}, u32[]{:S(2)}) copy-start(bf16[2,4,128,128]{3,2,1,0:T(8,128)(2,1)} %gauge.7) | copy-start | bytes 786436
  66.4 6.9 %collective-permute-start.8 = (f16[2,264,128]{2,1,0:T(8,128)(2,1)S(1)}, f16[2,264,128]{2,1,0:T(8,128)(2,1)S(1)}, u32[]{:S(2)}, u32[]{:S(2)}) collective-permute-start(f16[2,264,128]{2,1,0:T(8,128)(2,1)S(1)} %pad_maximum_fusion.2), channel_id=1, source_target_pairs={{0,2},{1,3},{2,0},{3,1},{4,6},{5,7},{6,4},{7,5},{8,10},{9,11},{10,... | collective-permute-start | bytes 405512 | tf_op jit(solution)/shard_map/ppermute | solution.py:315
  76.1 7.8 %collective-permute-start.10 = (f16[2,264,128]{2,1,0:T(8,128)(2,1)S(1)}, f16[2,264,128]{2,1,0:T(8,128)(2,1)S(1)}, u32[]{:S(2)}, u32[]{:S(2)}) collective-permute-start(f16[2,264,128]{2,1,0:T(8,128)(2,1)S(1)} %pad_maximum_fusion.4), channel_id=1, source_target_pairs={{240,0},{244,4},{248,8},{252,12},{0,16},{4,20},{8,24},{12,28},{16,... | collective-permute-start | bytes 405512 | tf_op jit(solution)/shard_map/ppermute | solution.py:325
  76.2 9.4 %collective-permute-start.12 = (f32[8,2,128,128]{3,2,1,0:T(8,128)S(1)}, f32[8,2,128,128]{3,2,1,0:T(8,128)S(1)}, u32[]{:S(2)}, u32[]{:S(2)}) collective-permute-start(f32[8,2,128,128]{3,2,1,0:T(8,128)S(1)} %constant_dynamic-update-slice_fusion.refs_0_), channel_id=1, source_target_pairs={{0,1},{1,0},{2,3},{3,2},{4,5},{5,4},{6,7},{7,6},{8,9},{9,8},{10,11... | collective-permute-start | bytes 3145736 | tf_op jit(solution)/shard_map/ppermute | solution.py:328
  77.4 6.5 %collective-permute-start.9 = (f16[2,264,128]{2,1,0:T(8,128)(2,1)S(1)}, f16[2,264,128]{2,1,0:T(8,128)(2,1)S(1)}, u32[]{:S(2)}, u32[]{:S(2)}) collective-permute-start(f16[2,264,128]{2,1,0:T(8,128)(2,1)S(1)} %pad_maximum_fusion.3), channel_id=1, source_target_pairs={{12,0},{0,4},{4,8},{8,12},{28,16},{16,20},{20,24},{24,28},{44,32},... | collective-permute-start | bytes 405512 | tf_op jit(solution)/shard_map/ppermute | solution.py:326
  84.0 3.6 %collective-permute-start.11 = (f16[4,264,128]{2,1,0:T(8,128)(2,1)S(1)}, f16[4,264,128]{2,1,0:T(8,128)(2,1)S(1)}, u32[]{:S(2)}, u32[]{:S(2)}) collective-permute-start(f16[4,264,128]{2,1,0:T(8,128)(2,1)S(1)} %pad_maximum_fusion.1), channel_id=1, source_target_pairs={{0,1},{1,0},{2,3},{3,2},{4,5},{5,4},{6,7},{7,6},{8,9},{9,8},{10,11... | collective-permute-start | bytes 811016 | tf_op jit(solution)/shard_map/ppermute | solution.py:330

commit v4 on v3

--- a/solution.py
+++ b/solution.py
@@ -12,7 +12,6 @@
 GZ = 32
 F32 = jnp.float32
 BF16 = jnp.bfloat16
-PACKED_ROWS = 16
 SHIFT = 13
 VMEM = pltpu.VMEM
 CONTRACT_LAST = (((1,), (1,)), ((), ()))
@@ -55,11 +54,10 @@
     }
 
 
-def load(core, orbitals, gauge, part):
+def load(orbitals, part):
     nb, points = orbitals.shape[2:]
-    blocks = points // nb
-
-    def body(core, orbitals, gauge, out, block, sems):
+
+    def body(orbitals, out, sems):
         copies = [
             pltpu.make_async_copy(
                 orbitals.at[c, 2 * part + slot], out.at[c, slot * nb : (slot + 1) * nb], sems.at[2 * c + slot]
@@ -67,30 +65,24 @@
             for c in range(2)
             for slot in range(2)
         ]
-        copies.append(pltpu.make_async_copy(gauge.at[:, 2 * part + core[0]], block, sems.at[4]))
         for copy in copies:
             copy.start()
-        copies[4].wait()
-        for c in range(2):
-            for j in range(blocks):
-                rows = block[c, j * PACKED_ROWS : (j + 1) * PACKED_ROWS, :]
-                out[c, 2 * nb :, j * nb : (j + 1) * nb] = rows
-        for copy in copies[:4]:
+        for copy in copies:
             copy.wait()
 
     return pl.pallas_call(
         body,
         name="load",
-        out_shape=VMEM((2, 2 * nb + PACKED_ROWS, points), BF16),
-        in_specs=specs(pltpu.SMEM, pl.ANY, pl.ANY),
+        out_shape=VMEM((2, 2 * nb, points), BF16),
+        in_specs=specs(pl.ANY),
         out_specs=specs(VMEM)[0],
-        scratch_shapes=[VMEM((2, nb, nb), BF16), pltpu.SemaphoreType.DMA((5,))],
+        scratch_shapes=[pltpu.SemaphoreType.DMA((4,))],
         **small(2),
-    )(core, *[pltpu.with_memory_space_constraint(array, pltpu.HBM) for array in (orbitals, gauge)])
+    )(pltpu.with_memory_space_constraint(orbitals, pltpu.HBM))
 
 
 def correlate(meta, base, directions, cosines, sines, own, sources):
-    nb = (own[0].shape[1] - PACKED_ROWS) // 2
+    nb = own[0].shape[1] // 2
     points = own[0].shape[2]
 
     def body(meta, cosines, sines, front, rear, first, second, out, arrived, left, phased, sems):
@@ -187,11 +179,6 @@
     nb = gauge.shape[2]
     pairs = len(right_of)
 
-    def unpack(ref, c):
-        rows = ref.shape[1] - PACKED_ROWS
-        blocks = [ref[c, rows:, j * nb : (j + 1) * nb] for j in range(ref.shape[2] // nb)]
-        return jnp.concatenate(blocks, axis=0)
-
     def body(slots, raw, gauge, *refs):
         payloads, outs = refs[: len(packed)], refs[len(packed) :]
         for p in range(pairs):
@@ -199,7 +186,7 @@
             if right_of[p] is None:
                 right = [gauge[c, slots[3, columns[p]]] for c in range(2)]
             else:
-                right = [unpack(payloads[right_of[p]], c) for c in range(2)]
+                right = [payloads[right_of[p][0]][c, right_of[p][1]] for c in range(2)]
             out_re, out_im = rotate_pair([raw[p, c] for c in range(2)], [gauge[c, k] for c in range(2)], right)
             for out, rows in zip(outs, layout):
                 for row, (pair, adjoint) in enumerate(rows):
@@ -269,14 +256,17 @@
     sibling = [(g, g ^ 1) for g in range(ga_count)]
     across = [(g, g ^ 2) for g in range(ga_count)]
 
-    core_index = core.reshape(1).astype(jnp.int32)
-    front = load(core_index, orbitals, gauge, 0)
+    nb = orbitals.shape[2]
+    front = load(orbitals, 0)
     beyond_front = lax.ppermute(front, "ka", outer_back)
     beside_front = lax.ppermute(front, "ka", ring_back)
-    rear = load(core_index, orbitals, gauge, 1)
+    rear = load(orbitals, 1)
     beyond_rear = lax.ppermute(rear, "ka", outer_back)
     beside_rear = lax.ppermute(rear, "ka", ring_back)
     own = (front, rear)
+    gauge_half = lax.dynamic_index_in_dim(gauge.reshape(2, 2, 2, nb, nb), core, 2, keepdims=False)
+    gauge_beyond = lax.ppermute(gauge_half, "ka", outer_back)
+    gauge_beside = lax.ppermute(gauge_half, "ka", ring_back)
 
     fractions = grid_fractions(grid_part * plane_count, plane_count, plane_count * ga_count)
     my_table = lax.dynamic_slice_in_dim(neighbour, device * kloc, kloc, 0) % kloc
@@ -299,44 +289,44 @@
     angles = jnp.concatenate([phase_angles(my_shift[:, b, :], b, counts, fractions) for b in range(3)])
     cosines, sines = jnp.cos(angles), jnp.sin(angles)
 
-    def halves(base, directions, sources):
+    def halves(meta, base, directions, sources, late=()):
         give = correlate(meta, base, directions, cosines, sines, own, sources)
+        give, *late = lax.optimization_barrier((give, *late))
         got = lax.ppermute(give, "ga", sibling)
-        return got, correlate(meta, base + 2, directions, cosines, sines, own, sources)
-
-    got, keep = halves(0, (0, 0), own)
-    got_front, keep_front = halves(4, (1, 2), (beside_front, beyond_front))
+        return got, correlate(meta, base + 2, directions, cosines, sines, own, sources), late
+
+    got, keep, _ = halves(meta, 0, (0, 0), own)
+    got_front, keep_front, _ = halves(meta, 4, (1, 2), (beside_front, beyond_front))
     coded = encode(jnp.concatenate([keep + got, keep_front + got_front], axis=0))
     other = lax.ppermute(coded, "ga", across)
     coded, beside_rear, beyond_rear = lax.optimization_barrier((coded, beside_rear, beyond_rear))
-    got, keep = halves(8, (1, 2), (beside_rear, beyond_rear))
+    got, keep, gauges = halves(meta, 8, (1, 2), (beside_rear, beyond_rear), (gauge_beside, gauge_beyond))
     other, got = lax.optimization_barrier((other, got))
     coded_rear = encode(keep + got)
     other_rear = lax.ppermute(coded_rear, "ga", across)
 
     first, adj_x, adj_y = rotate(
-        meta, (2, 3, 6, 7), decode(coded) + decode(other), gauge, (beside_front, beyond_front), (None, None, 0, 1),
+        meta, (2, 3, 6, 7), decode(coded) + decode(other), gauge, gauges, (None, None, (0, 0), (1, 0)),
         [[(0, 0), (1, 0), (2, 0), (3, 0), (0, 1), (1, 1)], [(2, 1)], [(3, 1)]],
     )
     last, adj_x_rear, adj_y_rear = rotate(
-        meta, (10, 11), decode(coded_rear) + decode(other_rear), gauge, (beside_rear, beyond_rear), (0, 1),
+        meta, (10, 11), decode(coded_rear) + decode(other_rear), gauge, gauges, ((0, 1), (1, 1)),
         [[(0, 0), (1, 0)], [(0, 1)], [(1, 1)]],
     )
     adj_y = lax.ppermute(encode(jnp.concatenate([adj_y, adj_y_rear], axis=0)), "ka", outer_ahead)
     adj_x = lax.ppermute(encode(jnp.concatenate([adj_x, adj_x_rear], axis=0)), "ka", ring_ahead)
     fwd = jnp.concatenate([first, last], axis=0)
     fwd_sib = lax.ppermute(fwd, "ga", sibling)
-    adj = lax.optimization_barrier(jnp.concatenate([adj_x, adj_y], axis=0))
-    adj_sib = lax.ppermute(adj, "ga", sibling)
     targets = [
         [(0, 0, i), (0, 0, i + 1), (0, 1, i + 4), (0, 2, i + 5), (1, 0, i), (1, 0, i + 1), (0, 1, i + 8), (0, 2, i + 9)]
         for i in (2, 0)
     ]
     outs = place(targets, meta, (fwd, fwd_sib), None)
-    adj_sib, *outs = lax.optimization_barrier((adj_sib, *outs))
-    adj, adj_sib = decode(adj), decode(adj_sib)
+    adj_x, adj_y, *outs = lax.optimization_barrier((adj_x, adj_y, *outs))
+    adj = lax.optimization_barrier(jnp.concatenate([adj_x, adj_y], axis=0))
+    adj_sib = lax.ppermute(adj, "ga", sibling)
     targets = [[(1, 1, i + 4), (1, 1, i + 8), (1, 2, i + 5), (1, 2, i + 9)] for i in (2, 0)]
-    return tuple(place(targets, meta, (adj, adj_sib), outs))
+    return tuple(place(targets, meta, (decode(adj), decode(adj_sib)), outs))
 
 
 def solution(mesh):

time: 90.5 us -> 87 us (0.961)
  waiting for transfers between devices: 34.8 us -> 23.4 us
  starting transfers between devices: 26 us -> 31.9 us
  other arithmetic: 3.6 us -> 5.58 us
    ppermute x1, waiting for transfers between devices: 9.26 us -> 2.16 us  [shards(): beside_front = lax.ppermute(front, 'ka', ring_back)]
    ppermute x1, waiting for transfers between devices: 6.31 us -> 0.01 us  [shards(): beyond_rear = lax.ppermute(rear, 'ka', outer_back)]
    ppermute x1, waiting for transfers between devices: 6.27 us -> 11.2 us  [shards(): beyond_front = lax.ppermute(front, 'ka', outer_back)]
    ppermute x0 -> x2, starting transfers between devices: none -> 4.28 us  [the longest x1 2.58 us: shards(): gauge_beside = lax.ppermute(gauge_half, 'ka', ring_back)]
    ppermute x1, waiting for transfers between devices: 4.95 us -> 2.06 us  [shards(): beside_rear = lax.ppermute(rear, 'ka', ring_back)]
    ppermute x1, waiting for transfers between devices: 6.27 us -> 3.68 us  [shards(): lax.ppermute(encode(jnp.concatenate([adj_y, adj_y_rear], axis=0)), 'ka',...]
    pallas_call x6, Pallas kernels: 12.8 us -> 15.1 us  [correlate(): pl.pallas_call(body, name='correlate', out_shape=VMEM((2, 2, nb, nb), F32...]
    pallas_call x2, Pallas kernels: 4.11 us -> 2.39 us  [rotate(): pl.pallas_call(body, name='rotate', out_shape=tuple((VMEM((len(rows), 2,...]
  transfers between devices with their start and end apart: 13 -> 15, of which waited for: 7 -> 9; matrix products, arithmetic and copies ran while one was open for 4% -> 6% of each run, Pallas kernels for 20% -> 23%
where the time goes in v4:
time: 87 us; the launch traced here: 86.6 us
  starting transfers between devices  31.9 us (37%)
  Pallas kernels  23.6 us (27%)
  waiting for transfers between devices  23.4 us (27%)
  other arithmetic  5.58 us (6%)
  between operations  1.08 us (1%)
  local copies, waits for them, and re-layouts  1.02 us (1%)
    pallas_call x6, Pallas kernels, correlate(): pl.pallas_call(body, name='correlate', out_shape=VMEM((2, 2, nb, nb), F32...  15.1 us
    ppermute x1, waiting for transfers between devices, shards(): beyond_front = lax.ppermute(front, 'ka', outer_back)  11.2 us
    ppermute x3, starting transfers between devices, halves(): got = lax.ppermute(give, 'ga', sibling)  8.64 us
    ppermute x1, starting transfers between devices, shards(): beyond_front = lax.ppermute(front, 'ka', outer_back)  7.49 us
    ppermute x1, waiting for transfers between devices, shards(): lax.ppermute(encode(jnp.concatenate([adj_y, adj_y_rear], axis=0)), 'ka',...  3.68 us
    pallas_call x2, Pallas kernels, place(): pl.pallas_call(body, out_shape=(shape, shape), name='place', in_specs=spe...  3.6 us
    ppermute x1, starting transfers between devices, shards(): other_rear = lax.ppermute(coded_rear, 'ga', across)  2.71 us
    ppermute x1, starting transfers between devices, shards(): other = lax.ppermute(coded, 'ga', across)  2.71 us
  transfers between devices with their start and end apart: 15, of which 9 were waited for; matrix products, arithmetic and copies ran while one was open for 6% of the time, Pallas kernels for 23%

profile of v4, /device:TPU:1, one launch (start us, length us, event | category | flops | bytes accessed | tf_op | source)
XLA Modules:
  0.0 86.6 jit_solution(17482604177779552959)
XLA Ops:
  0.6 1.2 %load.2.front.first = bf16[2,256,1024]{2,1,0:T(8,128)(2,1)S(1)} custom-call(bf16[2,4,128,1024]{3,2,1,0:T(8,128)(2,1)} %orbitals.3), custom_call_target="tpu_custom_call" | custom-call | flops 1 | bytes 1 | tf_op jit(solution)/shard_map/load/pallas_call | solution.py:73
  1.9 7.5 %collective-permute-start.2 = (bf16[2,256,1024]{2,1,0:T(8,128)(2,1)S(1)}, bf16[2,256,1024]{2,1,0:T(8,128)(2,1)}, u32[]{:S(2)}, u32[]{:S(2)}) collective-permute-start(bf16[2,256,1024]{2,1,0:T(8,128)(2,1)S(1)} %load.2.front.first), channel_id=1, source_target_pairs={{0,240},{4,244},{8,248},{12,252},{16,0},{20,4},{24,8},{28,12},{32,... | collective-permute-start | bytes 3145736 | tf_op jit(solution)/shard_map/ppermute | solution.py:261
  9.4 2.5 %collective-permute-start.1 = (bf16[2,256,1024]{2,1,0:T(8,128)(2,1)S(1)}, bf16[2,256,1024]{2,1,0:T(8,128)(2,1)}, u32[]{:S(2)}, u32[]{:S(2)}) collective-permute-start(bf16[2,256,1024]{2,1,0:T(8,128)(2,1)S(1)} %load.2.front.first), channel_id=1, source_target_pairs={{0,12},{4,0},{8,4},{12,8},{16,28},{20,16},{24,20},{28,24},{32,44},... | collective-permute-start | bytes 3145736 | tf_op jit(solution)/shard_map/ppermute | solution.py:262
  11.9 1.2 %load.3.rear.second = bf16[2,256,1024]{2,1,0:T(8,128)(2,1)S(1)} custom-call(bf16[2,4,128,1024]{3,2,1,0:T(8,128)(2,1)} %orbitals.3), custom_call_target="tpu_custom_call" | custom-call | flops 1 | bytes 1 | tf_op jit(solution)/shard_map/load/pallas_call | solution.py:73
  13.1 0.2 collective-permute-start.5
  13.3 0.5 collective-permute-start.4
  14.2 0.1 select_reduce_fusion.1
  14.3 0.1 concatenate.67
  14.6 0.1 copy.46
  14.7 0.1 copy.47
  14.8 0.1 copy.48
  14.9 0.2 add_reduce_fusion.2
  15.1 0.3 convert_reduce_fusion.1
  15.3 0.1 add_multiply_fusion.2
  15.5 0.3 fusion.6
  15.7 2.4 %correlate.7 = f32[2,2,128,128]{3,2,1,0:T(8,128)} custom-call(s32[4,12]{1,0:T(4,128)S(1)} %pad_add_fusion.2.meta.slots, f32[12,1024]{1,0:T(8,128)S(1)} %get-tuple-element.60.cosines, f32[12,1024]{1,0:T(8,128)S(1)} %get-tuple-element.59.sines, bf16[2,256,1024]{2,1,0:T(8,128)(2,1)S(1)} %load.2.front.first, bf16[2,256,1024]{2,1,0:T(8,128)(2,1)S(1)} %load.3.rear.second, ...), custom_call_target="tpu_custom_call" | custom-call | flops 1 | bytes 1 | tf_op jit(solution)/shard_map/correlate/pallas_call | solution.py:119
  18.1 1.9 %collective-permute-start = (f32[2,2,128,128]{3,2,1,0:T(8,128)}, f32[2,2,128,128]{3,2,1,0:T(8,128)}, u32[]{:S(2)}, u32[]{:S(2)}) collective-permute-start(f32[2,2,128,128]{3,2,1,0:T(8,128)} %correlate.7), channel_id=1, source_target_pairs={{0,1},{1,0},{2,3},{3,2},{4,5},{5,4},{6,7},{7,6},{8,9},{9,8},{10,11... | collective-permute-start | bytes 786440 | tf_op jit(solution)/shard_map/ppermute | solution.py:295
  20.0 11.2 %collective-permute-done.2.second = bf16[2,256,1024]{2,1,0:T(8,128)(2,1)} collective-permute-done((bf16[2,256,1024]{2,1,0:T(8,128)(2,1)S(1)}, bf16[2,256,1024]{2,1,0:T(8,128)(2,1)}, u32[]{:S(2)}, u32[]{:S(2)}) %collective-permute-start.2) | collective-permute-done | bytes 1048608 | tf_op jit(solution)/shard_map/ppermute | solution.py:261
  31.2 2.2 %collective-permute-done.1.first = bf16[2,256,1024]{2,1,0:T(8,128)(2,1)} collective-permute-done((bf16[2,256,1024]{2,1,0:T(8,128)(2,1)S(1)}, bf16[2,256,1024]{2,1,0:T(8,128)(2,1)}, u32[]{:S(2)}, u32[]{:S(2)}) %collective-permute-start.1) | collective-permute-done | bytes 1048608 | tf_op jit(solution)/shard_map/ppermute | solution.py:262
  33.4 3.3 %correlate.9 = f32[2,2,128,128]{3,2,1,0:T(8,128)} custom-call(s32[4,12]{1,0:T(4,128)S(1)} %pad_add_fusion.2.meta.slots, f32[12,1024]{1,0:T(8,128)S(1)} %get-tuple-element.60.cosines, f32[12,1024]{1,0:T(8,128)S(1)} %get-tuple-element.59.sines, bf16[2,256,1024]{2,1,0:T(8,128)(2,1)S(1)} %load.2.front.first, bf16[2,256,1024]{2,1,0:T(8,128)(2,1)S(1)} %load.3.rear.second, ...), custom_call_target="tpu_custom_call" | custom-call | flops 1 | bytes 1 | tf_op jit(solution)/shard_map/correlate/pallas_call | solution.py:119
  36.7 3.4 %collective-permute-start.3 = (f32[2,2,128,128]{3,2,1,0:T(8,128)}, f32[2,2,128,128]{3,2,1,0:T(8,128)}, u32[]{:S(2)}, u32[]{:S(2)}) collective-permute-start(f32[2,2,128,128]{3,2,1,0:T(8,128)} %correlate.9), channel_id=1, source_target_pairs={{0,1},{1,0},{2,3},{3,2},{4,5},{5,4},{6,7},{7,6},{8,9},{9,8},{10,11... | collective-permute-start | bytes 786440 | tf_op jit(solution)/shard_map/ppermute | solution.py:295
  40.1 1.7 %collective-permute-start.8 = (bf16[2,2,128,128]{3,2,1,0:T(8,128)(2,1)S(1)}, bf16[2,2,128,128]{3,2,1,0:T(8,128)(2,1)S(1)}, u32[]{:S(2)}, u32[]{:S(2)}) collective-permute-start(bf16[2,2,128,128]{3,2,1,0:T(8,128)(2,1)S(1)} %dynamic-slice_bitcast_fusion), channel_id=1, source_target_pairs={{0,240},{4,244},{8,248},{12,252},{16,0},{20,4},{24,8},{28,12},{32,... | collective-permute-start | bytes 393224 | tf_op jit(solution)/shard_map/ppermute | solution.py:268
  41.8 1.7 %correlate.6 = f32[2,2,128,128]{3,2,1,0:T(8,128)S(1)} custom-call(s32[4,12]{1,0:T(4,128)S(1)} %pad_add_fusion.2.meta.slots, f32[12,1024]{1,0:T(8,128)S(1)} %get-tuple-element.60.cosines, f32[12,1024]{1,0:T(8,128)S(1)} %get-tuple-element.59.sines, bf16[2,256,1024]{2,1,0:T(8,128)(2,1)S(1)} %load.2.front.first, bf16[2,256,1024]{2,1,0:T(8,128)(2,1)S(1)} %load.3.rear.second, ...), custom_call_target="tpu_custom_call" | custom-call | flops 1 | bytes 1 | tf_op jit(solution)/shard_map/correlate/pallas_call | solution.py:119
  43.5 2.6 %collective-permute-start.7 = (bf16[2,2,128,128]{3,2,1,0:T(8,128)(2,1)S(1)}, bf16[2,2,128,128]{3,2,1,0:T(8,128)(2,1)S(1)}, u32[]{:S(2)}, u32[]{:S(2)}) collective-permute-start(bf16[2,2,128,128]{3,2,1,0:T(8,128)(2,1)S(1)} %dynamic-slice_bitcast_fusion), channel_id=1, source_target_pairs={{0,12},{4,0},{8,4},{12,8},{16,28},{20,16},{24,20},{28,24},{32,44},... | collective-permute-start | bytes 393224 | tf_op jit(solution)/shard_map/ppermute | solution.py:269
  46.1 1.0 %add.172 = f32[2,2,128,128]{3,2,1,0:T(8,128)S(1)} add(f32[2,2,128,128]{3,2,1,0:T(8,128)S(1)} %correlate.6, f32[2,2,128,128]{3,2,1,0:T(8,128)} %collective-permute-done) | non-fusion elementwise | flops 65536 | bytes 786432 | tf_op jit(solution)/shard_map/add | solution.py:300
  47.1 2.6 %correlate.8 = f32[2,2,128,128]{3,2,1,0:T(8,128)S(1)} custom-call(s32[4,12]{1,0:T(4,128)S(1)} %pad_add_fusion.2.meta.slots, f32[12,1024]{1,0:T(8,128)S(1)} %get-tuple-element.60.cosines, f32[12,1024]{1,0:T(8,128)S(1)} %get-tuple-element.59.sines, bf16[2,256,1024]{2,1,0:T(8,128)(2,1)S(1)} %load.2.front.first, bf16[2,256,1024]{2,1,0:T(8,128)(2,1)S(1)} %load.3.rear.second, ...), custom_call_target="tpu_custom_call" | custom-call | flops 1 | bytes 1 | tf_op jit(solution)/shard_map/correlate/pallas_call | solution.py:119
  49.6 1.0 %add.173 = f32[2,2,128,128]{3,2,1,0:T(8,128)S(1)} add(f32[2,2,128,128]{3,2,1,0:T(8,128)S(1)} %correlate.8, f32[2,2,128,128]{3,2,1,0:T(8,128)} %collective-permute-done.3) | non-fusion elementwise | flops 65536 | bytes 786432 | tf_op jit(solution)/shard_map/add | solution.py:300
  50.6 0.1 fusion.1
  50.8 0.1 fusion
  51.1 2.7 %collective-permute-start.6 = (f16[4,264,128]{2,1,0:T(8,128)(2,1)S(1)}, f16[4,264,128]{2,1,0:T(8,128)(2,1)S(1)}, u32[]{:S(2)}, u32[]{:S(2)}) collective-permute-start(f16[4,264,128]{2,1,0:T(8,128)(2,1)S(1)} %pad_maximum_fusion), channel_id=1, source_target_pairs={{0,2},{1,3},{2,0},{3,1},{4,6},{5,7},{6,4},{7,5},{8,10},{9,11},{10,... | collective-permute-start | bytes 811016 | tf_op jit(solution)/shard_map/ppermute | solution.py:301
  53.8 2.1 %collective-permute-done.4.first = bf16[2,256,1024]{2,1,0:T(8,128)(2,1)} collective-permute-done((bf16[2,256,1024]{2,1,0:T(8,128)(2,1)S(1)}, bf16[2,256,1024]{2,1,0:T(8,128)(2,1)}, u32[]{:S(2)}, u32[]{:S(2)}) %collective-permute-start.4) | collective-permute-done | bytes 1048608 | tf_op jit(solution)/shard_map/ppermute | solution.py:265
  55.8 2.6 %correlate.10 = f32[2,2,128,128]{3,2,1,0:T(8,128)S(1)} custom-call(s32[4,12]{1,0:T(4,128)S(1)} %pad_add_fusion.2.meta.slots, f32[12,1024]{1,0:T(8,128)S(1)} %get-tuple-element.60.cosines, f32[12,1024]{1,0:T(8,128)S(1)} %get-tuple-element.59.sines, bf16[2,256,1024]{2,1,0:T(8,128)(2,1)S(1)} %load.2.front.first, bf16[2,256,1024]{2,1,0:T(8,128)(2,1)S(1)} %load.3.rear.second, ...), custom_call_target="tpu_custom_call" | custom-call | flops 1 | bytes 1 | tf_op jit(solution)/shard_map/correlate/pallas_call | solution.py:119
  58.5 0.2 collective-permute-done.7.refs_0_
  58.6 3.4 %collective-permute-start.9 = (f32[2,2,128,128]{3,2,1,0:T(8,128)S(1)}, f32[2,2,128,128]{3,2,1,0:T(8,128)S(1)}, u32[]{:S(2)}, u32[]{:S(2)}) collective-permute-start(f32[2,2,128,128]{3,2,1,0:T(8,128)S(1)} %correlate.10), channel_id=1, source_target_pairs={{0,1},{1,0},{2,3},{3,2},{4,5},{5,4},{6,7},{7,6},{8,9},{9,8},{10,11... | collective-permute-start | bytes 786440 | tf_op jit(solution)/shard_map/ppermute | solution.py:295
  62.0 2.6 %correlate.11 = f32[2,2,128,128]{3,2,1,0:T(8,128)S(1)} custom-call(s32[4,12]{1,0:T(4,128)S(1)} %pad_add_fusion.2.meta.slots, f32[12,1024]{1,0:T(8,128)S(1)} %get-tuple-element.60.cosines, f32[12,1024]{1,0:T(8,128)S(1)} %get-tuple-element.59.sines, bf16[2,256,1024]{2,1,0:T(8,128)(2,1)S(1)} %load.2.front.first, bf16[2,256,1024]{2,1,0:T(8,128)(2,1)S(1)} %load.3.rear.second, ...), custom_call_target="tpu_custom_call" | custom-call | flops 1 | bytes 1 | tf_op jit(solution)/shard_map/correlate/pallas_call | solution.py:119
  64.6 0.1 exponential_reduce_fusion.1
  64.8 0.1 exponential_reduce_fusion
  64.9 0.1 abs_reduce_fusion
  65.0 0.1 multiply_convert_fusion
  65.3 2.7 %collective-permute-start.10 = (f16[2,264,128]{2,1,0:T(8,128)(2,1)S(1)}, f16[2,264,128]{2,1,0:T(8,128)(2,1)S(1)}, u32[]{:S(2)}, u32[]{:S(2)}) collective-permute-start(f16[2,264,128]{2,1,0:T(8,128)(2,1)S(1)} %pad_maximum_fusion.2), channel_id=1, source_target_pairs={{0,2},{1,3},{2,0},{3,1},{4,6},{5,7},{6,4},{7,5},{8,10},{9,11},{10,... | collective-permute-start | bytes 405512 | tf_op jit(solution)/shard_map/ppermute | solution.py:306
  68.0 0.1 multiply_add_fusion
  68.1 0.1 fusion.41
  68.2 1.3 %rotate.2 = (f32[6,2,128,128]{3,2,1,0:T(8,128)S(1)}, f32[1,2,128,128]{3,2,1,0:T(8,128)S(1)}, f32[1,2,128,128]{3,2,1,0:T(8,128)S(1)}) custom-call(s32[4,12]{1,0:T(4,128)S(1)} %pad_add_fusion.2.meta.slots, f32[4,2,128,128]{3,2,1,0:T(8,128)S(1)} %bitcast.33, bf16[2,4,128,128]{3,2,1,0:T(8,128)(2,1)S(1)} %copy-done, ...), custom_call_target="tpu_custom_call" | custom-call | flops 1 | bytes 1 | tf_op jit(solution)/shard_map/rotate/pallas_call | solution.py:200
  69.6 2.5 %collective-permute-done.10 = f16[2,264,128]{2,1,0:T(8,128)(2,1)S(1)} collective-permute-done((f16[2,264,128]{2,1,0:T(8,128)(2,1)S(1)}, f16[2,264,128]{2,1,0:T(8,128)(2,1)S(1)}, u32[]{:S(2)}, u32[]{:S(2)}) %collective-permute-start.10) | collective-permute-done | bytes 135200 | tf_op jit(solution)/shard_map/ppermute | solution.py:306
  72.0 0.1 fusion.42
  72.2 0.1 multiply_add_fusion.1
  72.3 1.1 %rotate.3 = (f32[2,2,128,128]{3,2,1,0:T(8,128)S(1)}, f32[1,2,128,128]{3,2,1,0:T(8,128)S(1)}, f32[1,2,128,128]{3,2,1,0:T(8,128)S(1)}) custom-call(s32[4,12]{1,0:T(4,128)S(1)} %pad_add_fusion.2.meta.slots, f32[2,2,128,128]{3,2,1,0:T(8,128)S(1)} %bitcast.37, bf16[2,4,128,128]{3,2,1,0:T(8,128)(2,1)S(1)} %copy-done, ...), custom_call_target="tpu_custom_call" | custom-call | flops 1 | bytes 1 | tf_op jit(solution)/shard_map/rotate/pallas_call | solution.py:200
  73.4 0.1 fusion.3
  73.6 0.9 %collective-permute-start.13 = (f32[8,2,128,128]{3,2,1,0:T(8,128)S(1)}, f32[8,2,128,128]{3,2,1,0:T(8,128)S(1)}, u32[]{:S(2)}, u32[]{:S(2)}) collective-permute-start(f32[8,2,128,128]{3,2,1,0:T(8,128)S(1)} %constant_dynamic-update-slice_fusion.refs_0_), channel_id=1, source_target_pairs={{0,1},{1,0},{2,3},{3,2},{4,5},{5,4},{6,7},{7,6},{8,9},{9,8},{10,11... | collective-permute-start | bytes 3145736 | tf_op jit(solution)/shard_map/ppermute | solution.py:319
  74.4 0.1 fusion.2
  74.7 0.1 fusion.5
  74.8 0.1 fusion.4
  75.1 1.1 %collective-permute-start.11 = (f16[2,264,128]{2,1,0:T(8,128)(2,1)S(1)}, f16[2,264,128]{2,1,0:T(8,128)(2,1)S(1)}, u32[]{:S(2)}, u32[]{:S(2)}) collective-permute-start(f16[2,264,128]{2,1,0:T(8,128)(2,1)S(1)} %pad_maximum_fusion.3), channel_id=1, source_target_pairs={{12,0},{0,4},{4,8},{8,12},{28,16},{16,20},{20,24},{24,28},{44,32},... | collective-permute-start | bytes 405512 | tf_op jit(solution)/shard_map/ppermute | solution.py:317
  76.2 0.5 collective-permute-done.13.refs_1_
  76.7 2.0 %place.2 = (f32[3,2,4,128,128]{4,3,2,1,0:T(8,128)}, f32[3,2,4,128,128]{4,3,2,1,0:T(8,128)}) custom-call(s32[4,12]{1,0:T(4,128)S(1)} %pad_add_fusion.2.meta.slots, f32[8,2,128,128]{3,2,1,0:T(8,128)S(1)} %constant_dynamic-update-slice_fusion.refs_0_, f32[8,2,128,128]{3,2,1,0:T(8,128)S(1)} %collective-permute-done.13.refs_1_), custom_call_target="tpu_custom_call" | custom-call | flops 1 | bytes 1 | tf_op jit(solution)/shard_map/place/pallas_call | solution.py:229
  78.7 3.7 %collective-permute-done.12 = f16[2,264,128]{2,1,0:T(8,128)(2,1)S(1)} collective-permute-done((f16[2,264,128]{2,1,0:T(8,128)(2,1)S(1)}, f16[2,264,128]{2,1,0:T(8,128)(2,1)S(1)}, u32[]{:S(2)}, u32[]{:S(2)}) %collective-permute-start.12) | collective-permute-done | bytes 135200 | tf_op jit(solution)/shard_map/ppermute | solution.py:316
  82.4 0.2 collective-permute-done.11
  82.7 0.7 collective-permute-start.14
  83.4 0.1 fusion.33
  83.5 0.1 convert_multiply_fusion.1
  83.6 0.9 %collective-permute-done.14 = f16[4,264,128]{2,1,0:T(8,128)(2,1)S(1)} collective-permute-done((f16[4,264,128]{2,1,0:T(8,128)(2,1)S(1)}, f16[4,264,128]{2,1,0:T(8,128)(2,1)S(1)}, u32[]{:S(2)}, u32[]{:S(2)}) %collective-permute-start.14) | collective-permute-done | bytes 270368 | tf_op jit(solution)/shard_map/ppermute | solution.py:327
  84.6 0.1 fusion.34
  84.7 0.1 convert_multiply_fusion
  84.8 1.6 %place.3 = (f32[3,2,4,128,128]{4,3,2,1,0:T(8,128)}, f32[3,2,4,128,128]{4,3,2,1,0:T(8,128)}) custom-call(s32[4,12]{1,0:T(4,128)S(1)} %pad_add_fusion.2.meta.slots, f32[4,2,128,128]{3,2,1,0:T(8,128)S(1)} %bitcast.34, f32[4,2,128,128]{3,2,1,0:T(8,128)S(1)} %bitcast.35, ...), custom_call_target="tpu_custom_call", output_to_operand_aliasing={{0}: (3, {}), {1}: (4, {})} | custom-call | flops 1 | bytes 1 | tf_op jit(solution)/shard_map/place/pallas_call | solution.py:229
  (43 shorter events, 1.4 us)
Async XLA Ops:
  1.9 12.1 %copy-start.2 = (s32[256,3]{0,1:T(4,128)S(1)}, s32[256,3]{0,1:T(4,128)}, u32[]{:S(2)}) copy-start(s32[256,3]{0,1:T(4,128)} %param.6) | copy-start | bytes 9220
  1.9 12.6 %copy-start.1 = (s32[256,3,3]{0,2,1:T(4,128)S(1)}, s32[256,3,3]{0,2,1:T(4,128)}, u32[]{:S(2)}) copy-start(s32[256,3,3]{0,2,1:T(4,128)} %param.7) | copy-start | bytes 27652
  1.9 29.3 %collective-permute-start.2 = (bf16[2,256,1024]{2,1,0:T(8,128)(2,1)S(1)}, bf16[2,256,1024]{2,1,0:T(8,128)(2,1)}, u32[]{:S(2)}, u32[]{:S(2)}) collective-permute-start(bf16[2,256,1024]{2,1,0:T(8,128)(2,1)S(1)} %load.2.front.first), channel_id=1, source_target_pairs={{0,240},{4,244},{8,248},{12,252},{16,0},{20,4},{24,8},{28,12},{32,... | collective-permute-start | bytes 3145736 | tf_op jit(solution)/shard_map/ppermute | solution.py:261
  9.4 24.0 %collective-permute-start.1 = (bf16[2,256,1024]{2,1,0:T(8,128)(2,1)S(1)}, bf16[2,256,1024]{2,1,0:T(8,128)(2,1)}, u32[]{:S(2)}, u32[]{:S(2)}) collective-permute-start(bf16[2,256,1024]{2,1,0:T(8,128)(2,1)S(1)} %load.2.front.first), channel_id=1, source_target_pairs={{0,12},{4,0},{8,4},{12,8},{16,28},{20,16},{24,20},{28,24},{32,44},... | collective-permute-start | bytes 3145736 | tf_op jit(solution)/shard_map/ppermute | solution.py:262
  13.1 40.7 %collective-permute-start.5 = (bf16[2,256,1024]{2,1,0:T(8,128)(2,1)S(1)}, bf16[2,256,1024]{2,1,0:T(8,128)(2,1)S(1)}, u32[]{:S(2)}, u32[]{:S(2)}) collective-permute-start(bf16[2,256,1024]{2,1,0:T(8,128)(2,1)S(1)} %load.3.rear.second), channel_id=1, source_target_pairs={{0,240},{4,244},{8,248},{12,252},{16,0},{20,4},{24,8},{28,12},{32,... | collective-permute-start | bytes 3145736 | tf_op jit(solution)/shard_map/ppermute | solution.py:264
  13.3 42.5 %collective-permute-start.4 = (bf16[2,256,1024]{2,1,0:T(8,128)(2,1)S(1)}, bf16[2,256,1024]{2,1,0:T(8,128)(2,1)}, u32[]{:S(2)}, u32[]{:S(2)}) collective-permute-start(bf16[2,256,1024]{2,1,0:T(8,128)(2,1)S(1)} %load.3.rear.second), channel_id=1, source_target_pairs={{0,12},{4,0},{8,4},{12,8},{16,28},{20,16},{24,20},{28,24},{32,44},... | collective-permute-start | bytes 3145736 | tf_op jit(solution)/shard_map/ppermute | solution.py:265
  18.1 21.9 %copy-start = (bf16[2,4,128,128]{3,2,1,0:T(8,128)(2,1)S(1)}, bf16[2,4,128,128]{3,2,1,0:T(8,128)(2,1)}, u32[]{:S(2)}) copy-start(bf16[2,4,128,128]{3,2,1,0:T(8,128)(2,1)} %gauge.3) | copy-start | bytes 786436
  18.1 25.3 %collective-permute-start = (f32[2,2,128,128]{3,2,1,0:T(8,128)}, f32[2,2,128,128]{3,2,1,0:T(8,128)}, u32[]{:S(2)}, u32[]{:S(2)}) collective-permute-start(f32[2,2,128,128]{3,2,1,0:T(8,128)} %correlate.7), channel_id=1, source_target_pairs={{0,1},{1,0},{2,3},{3,2},{4,5},{5,4},{6,7},{7,6},{8,9},{9,8},{10,11... | collective-permute-start | bytes 786440 | tf_op jit(solution)/shard_map/ppermute | solution.py:295
  36.7 13.0 %collective-permute-start.3 = (f32[2,2,128,128]{3,2,1,0:T(8,128)}, f32[2,2,128,128]{3,2,1,0:T(8,128)}, u32[]{:S(2)}, u32[]{:S(2)}) collective-permute-start(f32[2,2,128,128]{3,2,1,0:T(8,128)} %correlate.9), channel_id=1, source_target_pairs={{0,1},{1,0},{2,3},{3,2},{4,5},{5,4},{6,7},{7,6},{8,9},{9,8},{10,11... | collective-permute-start | bytes 786440 | tf_op jit(solution)/shard_map/ppermute | solution.py:295
  40.1 18.4 %collective-permute-start.8 = (bf16[2,2,128,128]{3,2,1,0:T(8,128)(2,1)S(1)}, bf16[2,2,128,128]{3,2,1,0:T(8,128)(2,1)S(1)}, u32[]{:S(2)}, u32[]{:S(2)}) collective-permute-start(bf16[2,2,128,128]{3,2,1,0:T(8,128)(2,1)S(1)} %dynamic-slice_bitcast_fusion), channel_id=1, source_target_pairs={{0,240},{4,244},{8,248},{12,252},{16,0},{20,4},{24,8},{28,12},{32,... | collective-permute-start | bytes 393224 | tf_op jit(solution)/shard_map/ppermute | solution.py:268
  43.5 15.2 %collective-permute-start.7 = (bf16[2,2,128,128]{3,2,1,0:T(8,128)(2,1)S(1)}, bf16[2,2,128,128]{3,2,1,0:T(8,128)(2,1)S(1)}, u32[]{:S(2)}, u32[]{:S(2)}) collective-permute-start(bf16[2,2,128,128]{3,2,1,0:T(8,128)(2,1)S(1)} %dynamic-slice_bitcast_fusion), channel_id=1, source_target_pairs={{0,12},{4,0},{8,4},{12,8},{16,28},{20,16},{24,20},{28,24},{32,44},... | collective-permute-start | bytes 393224 | tf_op jit(solution)/shard_map/ppermute | solution.py:269
  51.1 13.7 %collective-permute-start.6 = (f16[4,264,128]{2,1,0:T(8,128)(2,1)S(1)}, f16[4,264,128]{2,1,0:T(8,128)(2,1)S(1)}, u32[]{:S(2)}, u32[]{:S(2)}) collective-permute-start(f16[4,264,128]{2,1,0:T(8,128)(2,1)S(1)} %pad_maximum_fusion), channel_id=1, source_target_pairs={{0,2},{1,3},{2,0},{3,1},{4,6},{5,7},{6,4},{7,5},{8,10},{9,11},{10,... | collective-permute-start | bytes 811016 | tf_op jit(solution)/shard_map/ppermute | solution.py:301
  58.6 6.1 %collective-permute-start.9 = (f32[2,2,128,128]{3,2,1,0:T(8,128)S(1)}, f32[2,2,128,128]{3,2,1,0:T(8,128)S(1)}, u32[]{:S(2)}, u32[]{:S(2)}) collective-permute-start(f32[2,2,128,128]{3,2,1,0:T(8,128)S(1)} %correlate.10), channel_id=1, source_target_pairs={{0,1},{1,0},{2,3},{3,2},{4,5},{5,4},{6,7},{7,6},{8,9},{9,8},{10,11... | collective-permute-start | bytes 786440 | tf_op jit(solution)/shard_map/ppermute | solution.py:295
  65.3 6.8 %collective-permute-start.10 = (f16[2,264,128]{2,1,0:T(8,128)(2,1)S(1)}, f16[2,264,128]{2,1,0:T(8,128)(2,1)S(1)}, u32[]{:S(2)}, u32[]{:S(2)}) collective-permute-start(f16[2,264,128]{2,1,0:T(8,128)(2,1)S(1)} %pad_maximum_fusion.2), channel_id=1, source_target_pairs={{0,2},{1,3},{2,0},{3,1},{4,6},{5,7},{6,4},{7,5},{8,10},{9,11},{10,... | collective-permute-start | bytes 405512 | tf_op jit(solution)/shard_map/ppermute | solution.py:306
  73.6 3.2 %collective-permute-start.13 = (f32[8,2,128,128]{3,2,1,0:T(8,128)S(1)}, f32[8,2,128,128]{3,2,1,0:T(8,128)S(1)}, u32[]{:S(2)}, u32[]{:S(2)}) collective-permute-start(f32[8,2,128,128]{3,2,1,0:T(8,128)S(1)} %constant_dynamic-update-slice_fusion.refs_0_), channel_id=1, source_target_pairs={{0,1},{1,0},{2,3},{3,2},{4,5},{5,4},{6,7},{7,6},{8,9},{9,8},{10,11... | collective-permute-start | bytes 3145736 | tf_op jit(solution)/shard_map/ppermute | solution.py:319
  75.0 7.4 %collective-permute-start.12 = (f16[2,264,128]{2,1,0:T(8,128)(2,1)S(1)}, f16[2,264,128]{2,1,0:T(8,128)(2,1)S(1)}, u32[]{:S(2)}, u32[]{:S(2)}) collective-permute-start(f16[2,264,128]{2,1,0:T(8,128)(2,1)S(1)} %pad_maximum_fusion.4), channel_id=1, source_target_pairs={{240,0},{244,4},{248,8},{252,12},{0,16},{4,20},{8,24},{12,28},{16,... | collective-permute-start | bytes 405512 | tf_op jit(solution)/shard_map/ppermute | solution.py:316
  75.1 7.5 %collective-permute-start.11 = (f16[2,264,128]{2,1,0:T(8,128)(2,1)S(1)}, f16[2,264,128]{2,1,0:T(8,128)(2,1)S(1)}, u32[]{:S(2)}, u32[]{:S(2)}) collective-permute-start(f16[2,264,128]{2,1,0:T(8,128)(2,1)S(1)} %pad_maximum_fusion.3), channel_id=1, source_target_pairs={{12,0},{0,4},{4,8},{8,12},{28,16},{16,20},{20,24},{24,28},{44,32},... | collective-permute-start | bytes 405512 | tf_op jit(solution)/shard_map/ppermute | solution.py:317
  82.7 1.9 %collective-permute-start.14 = (f16[4,264,128]{2,1,0:T(8,128)(2,1)S(1)}, f16[4,264,128]{2,1,0:T(8,128)(2,1)S(1)}, u32[]{:S(2)}, u32[]{:S(2)}) collective-permute-start(f16[4,264,128]{2,1,0:T(8,128)(2,1)S(1)} %pad_maximum_fusion.1), channel_id=1, source_target_pairs={{0,1},{1,0},{2,3},{3,2},{4,5},{5,4},{6,7},{7,6},{8,9},{9,8},{10,11... | collective-permute-start | bytes 811016 | tf_op jit(solution)/shard_map/ppermute | solution.py:327

commit v5 on v4

--- a/solution.py
+++ b/solution.py
@@ -315,18 +315,18 @@
     )
     adj_y = lax.ppermute(encode(jnp.concatenate([adj_y, adj_y_rear], axis=0)), "ka", outer_ahead)
     adj_x = lax.ppermute(encode(jnp.concatenate([adj_x, adj_x_rear], axis=0)), "ka", ring_ahead)
-    fwd = jnp.concatenate([first, last], axis=0)
-    fwd_sib = lax.ppermute(fwd, "ga", sibling)
+    first_sib = lax.ppermute(first, "ga", sibling)
+    last_sib = lax.ppermute(last, "ga", sibling)
     targets = [
-        [(0, 0, i), (0, 0, i + 1), (0, 1, i + 4), (0, 2, i + 5), (1, 0, i), (1, 0, i + 1), (0, 1, i + 8), (0, 2, i + 9)]
-        for i in (2, 0)
+        [(0, 0, i), (0, 0, i + 1), (0, 1, i + 4), (0, 2, i + 5), (1, 0, i), (1, 0, i + 1)] for i in (2, 0)
     ]
-    outs = place(targets, meta, (fwd, fwd_sib), None)
+    outs = place(targets, meta, (first, first_sib), None)
     adj_x, adj_y, *outs = lax.optimization_barrier((adj_x, adj_y, *outs))
     adj = lax.optimization_barrier(jnp.concatenate([adj_x, adj_y], axis=0))
     adj_sib = lax.ppermute(adj, "ga", sibling)
     targets = [[(1, 1, i + 4), (1, 1, i + 8), (1, 2, i + 5), (1, 2, i + 9)] for i in (2, 0)]
-    return tuple(place(targets, meta, (decode(adj), decode(adj_sib)), outs))
+    targets += [[(0, 1, i + 8), (0, 2, i + 9)] for i in (2, 0)]
+    return tuple(place(targets, meta, (decode(adj), decode(adj_sib), last, last_sib), outs))
 
 
 def solution(mesh):

time: 87 us -> 86.3 us (level)
  waiting for transfers between devices: 23.4 us -> 21.4 us
  starting transfers between devices: 31.9 us -> 33.3 us
    ppermute x1, waiting for transfers between devices: 3.68 us -> 2.37 us  [shards(): lax.ppermute(encode(jnp.concatenate([adj_y, adj_y_rear], axis=0)), 'ka',...]
  transfers between devices with their start and end apart: 15 -> 16, of which waited for: 9 -> 8; matrix products, arithmetic and copies ran while one was open for 6% -> 7% of each run, Pallas kernels for 23% -> 24%
where the time goes in v5:
time: 86.3 us; the launch traced here: 85.8 us
  starting transfers between devices  33.3 us (39%)
  Pallas kernels  23.6 us (27%)
  waiting for transfers between devices  21.4 us (25%)
  other arithmetic  5.58 us (6%)
  between operations  1.08 us (1%)
  local copies, waits for them, and re-layouts  0.94 us (1%)
    pallas_call x6, Pallas kernels, correlate(): pl.pallas_call(body, name='correlate', out_shape=VMEM((2, 2, nb, nb), F32...  15.1 us
    ppermute x1, waiting for transfers between devices, shards(): beyond_front = lax.ppermute(front, 'ka', outer_back)  11.2 us
    ppermute x3, starting transfers between devices, halves(): got = lax.ppermute(give, 'ga', sibling)  8.62 us
    ppermute x1, starting transfers between devices, shards(): beyond_front = lax.ppermute(front, 'ka', outer_back)  7.49 us
    pallas_call x2, Pallas kernels, place(): pl.pallas_call(body, out_shape=(shape, shape), name='place', in_specs=spe...  3.6 us
    ppermute x1, starting transfers between devices, shards(): other_rear = lax.ppermute(coded_rear, 'ga', across)  2.71 us
    ppermute x1, starting transfers between devices, shards(): other = lax.ppermute(coded, 'ga', across)  2.71 us
    ppermute x1, starting transfers between devices, shards(): gauge_beside = lax.ppermute(gauge_half, 'ka', ring_back)  2.58 us
  transfers between devices with their start and end apart: 16, of which 8 were waited for; matrix products, arithmetic and copies ran while one was open for 7% of the time, Pallas kernels for 24%

profile of v5, /device:TPU:1, one launch (start us, length us, event | category | flops | bytes accessed | tf_op | source)
XLA Modules:
  0.0 85.8 jit_solution(16218938979995019160)
XLA Ops:
  0.6 1.2 %load.2.front.first = bf16[2,256,1024]{2,1,0:T(8,128)(2,1)S(1)} custom-call(bf16[2,4,128,1024]{3,2,1,0:T(8,128)(2,1)} %orbitals.3), custom_call_target="tpu_custom_call" | custom-call | flops 1 | bytes 1 | tf_op jit(solution)/shard_map/load/pallas_call | solution.py:73
  1.9 7.5 %collective-permute-start.2 = (bf16[2,256,1024]{2,1,0:T(8,128)(2,1)S(1)}, bf16[2,256,1024]{2,1,0:T(8,128)(2,1)}, u32[]{:S(2)}, u32[]{:S(2)}) collective-permute-start(bf16[2,256,1024]{2,1,0:T(8,128)(2,1)S(1)} %load.2.front.first), channel_id=1, source_target_pairs={{0,240},{4,244},{8,248},{12,252},{16,0},{20,4},{24,8},{28,12},{32,... | collective-permute-start | bytes 3145736 | tf_op jit(solution)/shard_map/ppermute | solution.py:261
  9.4 2.5 %collective-permute-start.1 = (bf16[2,256,1024]{2,1,0:T(8,128)(2,1)S(1)}, bf16[2,256,1024]{2,1,0:T(8,128)(2,1)}, u32[]{:S(2)}, u32[]{:S(2)}) collective-permute-start(bf16[2,256,1024]{2,1,0:T(8,128)(2,1)S(1)} %load.2.front.first), channel_id=1, source_target_pairs={{0,12},{4,0},{8,4},{12,8},{16,28},{20,16},{24,20},{28,24},{32,44},... | collective-permute-start | bytes 3145736 | tf_op jit(solution)/shard_map/ppermute | solution.py:262
  11.9 1.2 %load.3.rear.second = bf16[2,256,1024]{2,1,0:T(8,128)(2,1)S(1)} custom-call(bf16[2,4,128,1024]{3,2,1,0:T(8,128)(2,1)} %orbitals.3), custom_call_target="tpu_custom_call" | custom-call | flops 1 | bytes 1 | tf_op jit(solution)/shard_map/load/pallas_call | solution.py:73
  13.1 0.2 collective-permute-start.5
  13.3 0.5 collective-permute-start.4
  14.2 0.1 select_reduce_fusion.1
  14.3 0.1 concatenate.64
  14.6 0.1 copy.46
  14.7 0.1 copy.47
  14.8 0.1 copy.48
  14.9 0.2 add_reduce_fusion.2
  15.1 0.3 convert_reduce_fusion.1
  15.3 0.1 add_multiply_fusion.2
  15.5 0.3 fusion.6
  15.7 2.4 %correlate.7 = f32[2,2,128,128]{3,2,1,0:T(8,128)} custom-call(s32[4,12]{1,0:T(4,128)S(1)} %pad_add_fusion.2.meta.slots, f32[12,1024]{1,0:T(8,128)S(1)} %get-tuple-element.60.cosines, f32[12,1024]{1,0:T(8,128)S(1)} %get-tuple-element.59.sines, bf16[2,256,1024]{2,1,0:T(8,128)(2,1)S(1)} %load.2.front.first, bf16[2,256,1024]{2,1,0:T(8,128)(2,1)S(1)} %load.3.rear.second, ...), custom_call_target="tpu_custom_call" | custom-call | flops 1 | bytes 1 | tf_op jit(solution)/shard_map/correlate/pallas_call | solution.py:119
  18.1 1.9 %collective-permute-start = (f32[2,2,128,128]{3,2,1,0:T(8,128)}, f32[2,2,128,128]{3,2,1,0:T(8,128)}, u32[]{:S(2)}, u32[]{:S(2)}) collective-permute-start(f32[2,2,128,128]{3,2,1,0:T(8,128)} %correlate.7), channel_id=1, source_target_pairs={{0,1},{1,0},{2,3},{3,2},{4,5},{5,4},{6,7},{7,6},{8,9},{9,8},{10,11... | collective-permute-start | bytes 786440 | tf_op jit(solution)/shard_map/ppermute | solution.py:295
  20.0 11.2 %collective-permute-done.2.second = bf16[2,256,1024]{2,1,0:T(8,128)(2,1)} collective-permute-done((bf16[2,256,1024]{2,1,0:T(8,128)(2,1)S(1)}, bf16[2,256,1024]{2,1,0:T(8,128)(2,1)}, u32[]{:S(2)}, u32[]{:S(2)}) %collective-permute-start.2) | collective-permute-done | bytes 1048608 | tf_op jit(solution)/shard_map/ppermute | solution.py:261
  31.2 2.2 %collective-permute-done.1.first = bf16[2,256,1024]{2,1,0:T(8,128)(2,1)} collective-permute-done((bf16[2,256,1024]{2,1,0:T(8,128)(2,1)S(1)}, bf16[2,256,1024]{2,1,0:T(8,128)(2,1)}, u32[]{:S(2)}, u32[]{:S(2)}) %collective-permute-start.1) | collective-permute-done | bytes 1048608 | tf_op jit(solution)/shard_map/ppermute | solution.py:262
  33.4 3.3 %correlate.9 = f32[2,2,128,128]{3,2,1,0:T(8,128)} custom-call(s32[4,12]{1,0:T(4,128)S(1)} %pad_add_fusion.2.meta.slots, f32[12,1024]{1,0:T(8,128)S(1)} %get-tuple-element.60.cosines, f32[12,1024]{1,0:T(8,128)S(1)} %get-tuple-element.59.sines, bf16[2,256,1024]{2,1,0:T(8,128)(2,1)S(1)} %load.2.front.first, bf16[2,256,1024]{2,1,0:T(8,128)(2,1)S(1)} %load.3.rear.second, ...), custom_call_target="tpu_custom_call" | custom-call | flops 1 | bytes 1 | tf_op jit(solution)/shard_map/correlate/pallas_call | solution.py:119
  36.7 3.4 %collective-permute-start.3 = (f32[2,2,128,128]{3,2,1,0:T(8,128)}, f32[2,2,128,128]{3,2,1,0:T(8,128)}, u32[]{:S(2)}, u32[]{:S(2)}) collective-permute-start(f32[2,2,128,128]{3,2,1,0:T(8,128)} %correlate.9), channel_id=1, source_target_pairs={{0,1},{1,0},{2,3},{3,2},{4,5},{5,4},{6,7},{7,6},{8,9},{9,8},{10,11... | collective-permute-start | bytes 786440 | tf_op jit(solution)/shard_map/ppermute | solution.py:295
  40.1 1.7 %collective-permute-start.8 = (bf16[2,2,128,128]{3,2,1,0:T(8,128)(2,1)S(1)}, bf16[2,2,128,128]{3,2,1,0:T(8,128)(2,1)S(1)}, u32[]{:S(2)}, u32[]{:S(2)}) collective-permute-start(bf16[2,2,128,128]{3,2,1,0:T(8,128)(2,1)S(1)} %dynamic-slice_bitcast_fusion), channel_id=1, source_target_pairs={{0,240},{4,244},{8,248},{12,252},{16,0},{20,4},{24,8},{28,12},{32,... | collective-permute-start | bytes 393224 | tf_op jit(solution)/shard_map/ppermute | solution.py:268
  41.8 1.7 %correlate.6 = f32[2,2,128,128]{3,2,1,0:T(8,128)S(1)} custom-call(s32[4,12]{1,0:T(4,128)S(1)} %pad_add_fusion.2.meta.slots, f32[12,1024]{1,0:T(8,128)S(1)} %get-tuple-element.60.cosines, f32[12,1024]{1,0:T(8,128)S(1)} %get-tuple-element.59.sines, bf16[2,256,1024]{2,1,0:T(8,128)(2,1)S(1)} %load.2.front.first, bf16[2,256,1024]{2,1,0:T(8,128)(2,1)S(1)} %load.3.rear.second, ...), custom_call_target="tpu_custom_call" | custom-call | flops 1 | bytes 1 | tf_op jit(solution)/shard_map/correlate/pallas_call | solution.py:119
  43.5 2.6 %collective-permute-start.7 = (bf16[2,2,128,128]{3,2,1,0:T(8,128)(2,1)S(1)}, bf16[2,2,128,128]{3,2,1,0:T(8,128)(2,1)S(1)}, u32[]{:S(2)}, u32[]{:S(2)}) collective-permute-start(bf16[2,2,128,128]{3,2,1,0:T(8,128)(2,1)S(1)} %dynamic-slice_bitcast_fusion), channel_id=1, source_target_pairs={{0,12},{4,0},{8,4},{12,8},{16,28},{20,16},{24,20},{28,24},{32,44},... | collective-permute-start | bytes 393224 | tf_op jit(solution)/shard_map/ppermute | solution.py:269
  46.1 1.0 %add.172 = f32[2,2,128,128]{3,2,1,0:T(8,128)S(1)} add(f32[2,2,128,128]{3,2,1,0:T(8,128)S(1)} %correlate.6, f32[2,2,128,128]{3,2,1,0:T(8,128)} %collective-permute-done) | non-fusion elementwise | flops 65536 | bytes 786432 | tf_op jit(solution)/shard_map/add | solution.py:300
  47.1 2.6 %correlate.8 = f32[2,2,128,128]{3,2,1,0:T(8,128)S(1)} custom-call(s32[4,12]{1,0:T(4,128)S(1)} %pad_add_fusion.2.meta.slots, f32[12,1024]{1,0:T(8,128)S(1)} %get-tuple-element.60.cosines, f32[12,1024]{1,0:T(8,128)S(1)} %get-tuple-element.59.sines, bf16[2,256,1024]{2,1,0:T(8,128)(2,1)S(1)} %load.2.front.first, bf16[2,256,1024]{2,1,0:T(8,128)(2,1)S(1)} %load.3.rear.second, ...), custom_call_target="tpu_custom_call" | custom-call | flops 1 | bytes 1 | tf_op jit(solution)/shard_map/correlate/pallas_call | solution.py:119
  49.7 1.0 %add.173 = f32[2,2,128,128]{3,2,1,0:T(8,128)S(1)} add(f32[2,2,128,128]{3,2,1,0:T(8,128)S(1)} %correlate.8, f32[2,2,128,128]{3,2,1,0:T(8,128)} %collective-permute-done.3) | non-fusion elementwise | flops 65536 | bytes 786432 | tf_op jit(solution)/shard_map/add | solution.py:300
  50.7 0.1 fusion.1
  50.8 0.1 fusion
  51.1 2.7 %collective-permute-start.6 = (f16[4,264,128]{2,1,0:T(8,128)(2,1)S(1)}, f16[4,264,128]{2,1,0:T(8,128)(2,1)S(1)}, u32[]{:S(2)}, u32[]{:S(2)}) collective-permute-start(f16[4,264,128]{2,1,0:T(8,128)(2,1)S(1)} %pad_maximum_fusion), channel_id=1, source_target_pairs={{0,2},{1,3},{2,0},{3,1},{4,6},{5,7},{6,4},{7,5},{8,10},{9,11},{10,... | collective-permute-start | bytes 811016 | tf_op jit(solution)/shard_map/ppermute | solution.py:301
  53.8 2.0 %collective-permute-done.4.first = bf16[2,256,1024]{2,1,0:T(8,128)(2,1)} collective-permute-done((bf16[2,256,1024]{2,1,0:T(8,128)(2,1)S(1)}, bf16[2,256,1024]{2,1,0:T(8,128)(2,1)}, u32[]{:S(2)}, u32[]{:S(2)}) %collective-permute-start.4) | collective-permute-done | bytes 1048608 | tf_op jit(solution)/shard_map/ppermute | solution.py:265
  55.8 2.6 %correlate.10 = f32[2,2,128,128]{3,2,1,0:T(8,128)S(1)} custom-call(s32[4,12]{1,0:T(4,128)S(1)} %pad_add_fusion.2.meta.slots, f32[12,1024]{1,0:T(8,128)S(1)} %get-tuple-element.60.cosines, f32[12,1024]{1,0:T(8,128)S(1)} %get-tuple-element.59.sines, bf16[2,256,1024]{2,1,0:T(8,128)(2,1)S(1)} %load.2.front.first, bf16[2,256,1024]{2,1,0:T(8,128)(2,1)S(1)} %load.3.rear.second, ...), custom_call_target="tpu_custom_call" | custom-call | flops 1 | bytes 1 | tf_op jit(solution)/shard_map/correlate/pallas_call | solution.py:119
  58.4 0.2 collective-permute-done.7.refs_0_
  58.6 3.3 %collective-permute-start.9 = (f32[2,2,128,128]{3,2,1,0:T(8,128)S(1)}, f32[2,2,128,128]{3,2,1,0:T(8,128)S(1)}, u32[]{:S(2)}, u32[]{:S(2)}) collective-permute-start(f32[2,2,128,128]{3,2,1,0:T(8,128)S(1)} %correlate.10), channel_id=1, source_target_pairs={{0,1},{1,0},{2,3},{3,2},{4,5},{5,4},{6,7},{7,6},{8,9},{9,8},{10,11... | collective-permute-start | bytes 786440 | tf_op jit(solution)/shard_map/ppermute | solution.py:295
  62.0 2.6 %correlate.11 = f32[2,2,128,128]{3,2,1,0:T(8,128)S(1)} custom-call(s32[4,12]{1,0:T(4,128)S(1)} %pad_add_fusion.2.meta.slots, f32[12,1024]{1,0:T(8,128)S(1)} %get-tuple-element.60.cosines, f32[12,1024]{1,0:T(8,128)S(1)} %get-tuple-element.59.sines, bf16[2,256,1024]{2,1,0:T(8,128)(2,1)S(1)} %load.2.front.first, bf16[2,256,1024]{2,1,0:T(8,128)(2,1)S(1)} %load.3.rear.second, ...), custom_call_target="tpu_custom_call" | custom-call | flops 1 | bytes 1 | tf_op jit(solution)/shard_map/correlate/pallas_call | solution.py:119
  64.6 0.1 exponential_reduce_fusion.1
  64.7 0.1 exponential_reduce_fusion
  64.8 0.1 abs_reduce_fusion
  65.0 0.1 multiply_convert_fusion
  65.2 2.7 %collective-permute-start.10 = (f16[2,264,128]{2,1,0:T(8,128)(2,1)S(1)}, f16[2,264,128]{2,1,0:T(8,128)(2,1)S(1)}, u32[]{:S(2)}, u32[]{:S(2)}) collective-permute-start(f16[2,264,128]{2,1,0:T(8,128)(2,1)S(1)} %pad_maximum_fusion.2), channel_id=1, source_target_pairs={{0,2},{1,3},{2,0},{3,1},{4,6},{5,7},{6,4},{7,5},{8,10},{9,11},{10,... | collective-permute-start | bytes 405512 | tf_op jit(solution)/shard_map/ppermute | solution.py:306
  67.9 0.1 multiply_add_fusion
  68.1 1.3 %rotate.2 = (f32[6,2,128,128]{3,2,1,0:T(8,128)S(1)}, f32[1,2,128,128]{3,2,1,0:T(8,128)S(1)}, f32[1,2,128,128]{3,2,1,0:T(8,128)S(1)}) custom-call(s32[4,12]{1,0:T(4,128)S(1)} %pad_add_fusion.2.meta.slots, f32[4,2,128,128]{3,2,1,0:T(8,128)S(1)} %bitcast.35, bf16[2,4,128,128]{3,2,1,0:T(8,128)(2,1)S(1)} %copy-done, ...), custom_call_target="tpu_custom_call" | custom-call | flops 1 | bytes 1 | tf_op jit(solution)/shard_map/rotate/pallas_call | solution.py:200
  69.3 0.4 collective-permute-start.13
  69.7 0.1 fusion.41
  69.8 2.2 %collective-permute-done.10 = f16[2,264,128]{2,1,0:T(8,128)(2,1)S(1)} collective-permute-done((f16[2,264,128]{2,1,0:T(8,128)(2,1)S(1)}, f16[2,264,128]{2,1,0:T(8,128)(2,1)S(1)}, u32[]{:S(2)}, u32[]{:S(2)}) %collective-permute-start.10) | collective-permute-done | bytes 135200 | tf_op jit(solution)/shard_map/ppermute | solution.py:306
  72.0 0.1 fusion.42
  72.1 0.1 multiply_add_fusion.1
  72.2 1.1 %rotate.3 = (f32[2,2,128,128]{3,2,1,0:T(8,128)S(1)}, f32[1,2,128,128]{3,2,1,0:T(8,128)S(1)}, f32[1,2,128,128]{3,2,1,0:T(8,128)S(1)}) custom-call(s32[4,12]{1,0:T(4,128)S(1)} %pad_add_fusion.2.meta.slots, f32[2,2,128,128]{3,2,1,0:T(8,128)S(1)} %bitcast.37, bf16[2,4,128,128]{3,2,1,0:T(8,128)(2,1)S(1)} %copy-done, ...), custom_call_target="tpu_custom_call" | custom-call | flops 1 | bytes 1 | tf_op jit(solution)/shard_map/rotate/pallas_call | solution.py:200
  73.4 0.1 fusion.3
  73.5 0.1 fusion.2
  73.7 0.1 fusion.5
  73.8 0.1 fusion.4
  74.2 1.2 %collective-permute-start.11 = (f16[2,264,128]{2,1,0:T(8,128)(2,1)S(1)}, f16[2,264,128]{2,1,0:T(8,128)(2,1)S(1)}, u32[]{:S(2)}, u32[]{:S(2)}) collective-permute-start(f16[2,264,128]{2,1,0:T(8,128)(2,1)S(1)} %pad_maximum_fusion.3), channel_id=1, source_target_pairs={{12,0},{0,4},{4,8},{8,12},{28,16},{16,20},{20,24},{24,28},{44,32},... | collective-permute-start | bytes 405512 | tf_op jit(solution)/shard_map/ppermute | solution.py:317
  75.3 1.1 %collective-permute-start.15 = (f32[2,2,128,128]{3,2,1,0:T(8,128)S(1)}, f32[2,2,128,128]{3,2,1,0:T(8,128)S(1)}, u32[]{:S(2)}, u32[]{:S(2)}) collective-permute-start(f32[2,2,128,128]{3,2,1,0:T(8,128)S(1)} %get-tuple-element.39.refs_2_), channel_id=1, source_target_pairs={{0,1},{1,0},{2,3},{3,2},{4,5},{5,4},{6,7},{7,6},{8,9},{9,8},{10,11... | collective-permute-start | bytes 786440 | tf_op jit(solution)/shard_map/ppermute | solution.py:319
  76.4 1.8 %place.2 = (f32[3,2,4,128,128]{4,3,2,1,0:T(8,128)}, f32[3,2,4,128,128]{4,3,2,1,0:T(8,128)}) custom-call(s32[4,12]{1,0:T(4,128)S(1)} %pad_add_fusion.2.meta.slots, f32[6,2,128,128]{3,2,1,0:T(8,128)S(1)} %get-tuple-element.34.refs_0_, f32[6,2,128,128]{3,2,1,0:T(8,128)S(1)} %collective-permute-done.13.refs_1_), custom_call_target="tpu_custom_call" | custom-call | flops 1 | bytes 1 | tf_op jit(solution)/shard_map/place/pallas_call | solution.py:229
  78.2 2.4 %collective-permute-done.12 = f16[2,264,128]{2,1,0:T(8,128)(2,1)S(1)} collective-permute-done((f16[2,264,128]{2,1,0:T(8,128)(2,1)S(1)}, f16[2,264,128]{2,1,0:T(8,128)(2,1)S(1)}, u32[]{:S(2)}, u32[]{:S(2)}) %collective-permute-start.12) | collective-permute-done | bytes 135200 | tf_op jit(solution)/shard_map/ppermute | solution.py:316
  80.6 0.3 collective-permute-done.11
  81.0 1.5 %collective-permute-start.14 = (f16[4,264,128]{2,1,0:T(8,128)(2,1)S(1)}, f16[4,264,128]{2,1,0:T(8,128)(2,1)S(1)}, u32[]{:S(2)}, u32[]{:S(2)}) collective-permute-start(f16[4,264,128]{2,1,0:T(8,128)(2,1)S(1)} %pad_maximum_fusion.1), channel_id=1, source_target_pairs={{0,1},{1,0},{2,3},{3,2},{4,5},{5,4},{6,7},{7,6},{8,9},{9,8},{10,11... | collective-permute-start | bytes 811016 | tf_op jit(solution)/shard_map/ppermute | solution.py:326
  82.4 0.1 fusion.33
  82.6 0.1 convert_multiply_fusion.1
  82.7 0.9 %collective-permute-done.14 = f16[4,264,128]{2,1,0:T(8,128)(2,1)S(1)} collective-permute-done((f16[4,264,128]{2,1,0:T(8,128)(2,1)S(1)}, f16[4,264,128]{2,1,0:T(8,128)(2,1)S(1)}, u32[]{:S(2)}, u32[]{:S(2)}) %collective-permute-start.14) | collective-permute-done | bytes 270368 | tf_op jit(solution)/shard_map/ppermute | solution.py:326
  83.6 0.1 fusion.34
  83.7 0.1 convert_multiply_fusion
  83.9 1.8 %place.3 = (f32[3,2,4,128,128]{4,3,2,1,0:T(8,128)}, f32[3,2,4,128,128]{4,3,2,1,0:T(8,128)}) custom-call(s32[4,12]{1,0:T(4,128)S(1)} %pad_add_fusion.2.meta.slots, f32[4,2,128,128]{3,2,1,0:T(8,128)S(1)} %bitcast.33, f32[4,2,128,128]{3,2,1,0:T(8,128)S(1)} %bitcast.34, ...), custom_call_target="tpu_custom_call", output_to_operand_aliasing={{0}: (5, {}), {1}: (6, {})} | custom-call | flops 1 | bytes 1 | tf_op jit(solution)/shard_map/place/pallas_call | solution.py:229
  (43 shorter events, 1.3 us)
Async XLA Ops:
  1.9 12.1 %copy-start.2 = (s32[256,3]{0,1:T(4,128)S(1)}, s32[256,3]{0,1:T(4,128)}, u32[]{:S(2)}) copy-start(s32[256,3]{0,1:T(4,128)} %param.6) | copy-start | bytes 9220
  1.9 12.6 %copy-start.1 = (s32[256,3,3]{0,2,1:T(4,128)S(1)}, s32[256,3,3]{0,2,1:T(4,128)}, u32[]{:S(2)}) copy-start(s32[256,3,3]{0,2,1:T(4,128)} %param.7) | copy-start | bytes 27652
  1.9 29.3 %collective-permute-start.2 = (bf16[2,256,1024]{2,1,0:T(8,128)(2,1)S(1)}, bf16[2,256,1024]{2,1,0:T(8,128)(2,1)}, u32[]{:S(2)}, u32[]{:S(2)}) collective-permute-start(bf16[2,256,1024]{2,1,0:T(8,128)(2,1)S(1)} %load.2.front.first), channel_id=1, source_target_pairs={{0,240},{4,244},{8,248},{12,252},{16,0},{20,4},{24,8},{28,12},{32,... | collective-permute-start | bytes 3145736 | tf_op jit(solution)/shard_map/ppermute | solution.py:261
  9.4 24.0 %collective-permute-start.1 = (bf16[2,256,1024]{2,1,0:T(8,128)(2,1)S(1)}, bf16[2,256,1024]{2,1,0:T(8,128)(2,1)}, u32[]{:S(2)}, u32[]{:S(2)}) collective-permute-start(bf16[2,256,1024]{2,1,0:T(8,128)(2,1)S(1)} %load.2.front.first), channel_id=1, source_target_pairs={{0,12},{4,0},{8,4},{12,8},{16,28},{20,16},{24,20},{28,24},{32,44},... | collective-permute-start | bytes 3145736 | tf_op jit(solution)/shard_map/ppermute | solution.py:262
  13.1 40.7 %collective-permute-start.5 = (bf16[2,256,1024]{2,1,0:T(8,128)(2,1)S(1)}, bf16[2,256,1024]{2,1,0:T(8,128)(2,1)S(1)}, u32[]{:S(2)}, u32[]{:S(2)}) collective-permute-start(bf16[2,256,1024]{2,1,0:T(8,128)(2,1)S(1)} %load.3.rear.second), channel_id=1, source_target_pairs={{0,240},{4,244},{8,248},{12,252},{16,0},{20,4},{24,8},{28,12},{32,... | collective-permute-start | bytes 3145736 | tf_op jit(solution)/shard_map/ppermute | solution.py:264
  13.3 42.5 %collective-permute-start.4 = (bf16[2,256,1024]{2,1,0:T(8,128)(2,1)S(1)}, bf16[2,256,1024]{2,1,0:T(8,128)(2,1)}, u32[]{:S(2)}, u32[]{:S(2)}) collective-permute-start(bf16[2,256,1024]{2,1,0:T(8,128)(2,1)S(1)} %load.3.rear.second), channel_id=1, source_target_pairs={{0,12},{4,0},{8,4},{12,8},{16,28},{20,16},{24,20},{28,24},{32,44},... | collective-permute-start | bytes 3145736 | tf_op jit(solution)/shard_map/ppermute | solution.py:265
  18.1 22.0 %copy-start = (bf16[2,4,128,128]{3,2,1,0:T(8,128)(2,1)S(1)}, bf16[2,4,128,128]{3,2,1,0:T(8,128)(2,1)}, u32[]{:S(2)}) copy-start(bf16[2,4,128,128]{3,2,1,0:T(8,128)(2,1)} %gauge.3) | copy-start | bytes 786436
  18.1 25.4 %collective-permute-start = (f32[2,2,128,128]{3,2,1,0:T(8,128)}, f32[2,2,128,128]{3,2,1,0:T(8,128)}, u32[]{:S(2)}, u32[]{:S(2)}) collective-permute-start(f32[2,2,128,128]{3,2,1,0:T(8,128)} %correlate.7), channel_id=1, source_target_pairs={{0,1},{1,0},{2,3},{3,2},{4,5},{5,4},{6,7},{7,6},{8,9},{9,8},{10,11... | collective-permute-start | bytes 786440 | tf_op jit(solution)/shard_map/ppermute | solution.py:295
  36.7 13.0 %collective-permute-start.3 = (f32[2,2,128,128]{3,2,1,0:T(8,128)}, f32[2,2,128,128]{3,2,1,0:T(8,128)}, u32[]{:S(2)}, u32[]{:S(2)}) collective-permute-start(f32[2,2,128,128]{3,2,1,0:T(8,128)} %correlate.9), channel_id=1, source_target_pairs={{0,1},{1,0},{2,3},{3,2},{4,5},{5,4},{6,7},{7,6},{8,9},{9,8},{10,11... | collective-permute-start | bytes 786440 | tf_op jit(solution)/shard_map/ppermute | solution.py:295
  40.1 18.3 %collective-permute-start.8 = (bf16[2,2,128,128]{3,2,1,0:T(8,128)(2,1)S(1)}, bf16[2,2,128,128]{3,2,1,0:T(8,128)(2,1)S(1)}, u32[]{:S(2)}, u32[]{:S(2)}) collective-permute-start(bf16[2,2,128,128]{3,2,1,0:T(8,128)(2,1)S(1)} %dynamic-slice_bitcast_fusion), channel_id=1, source_target_pairs={{0,240},{4,244},{8,248},{12,252},{16,0},{20,4},{24,8},{28,12},{32,... | collective-permute-start | bytes 393224 | tf_op jit(solution)/shard_map/ppermute | solution.py:268
  43.5 15.1 %collective-permute-start.7 = (bf16[2,2,128,128]{3,2,1,0:T(8,128)(2,1)S(1)}, bf16[2,2,128,128]{3,2,1,0:T(8,128)(2,1)S(1)}, u32[]{:S(2)}, u32[]{:S(2)}) collective-permute-start(bf16[2,2,128,128]{3,2,1,0:T(8,128)(2,1)S(1)} %dynamic-slice_bitcast_fusion), channel_id=1, source_target_pairs={{0,12},{4,0},{8,4},{12,8},{16,28},{20,16},{24,20},{28,24},{32,44},... | collective-permute-start | bytes 393224 | tf_op jit(solution)/shard_map/ppermute | solution.py:269
  51.1 13.6 %collective-permute-start.6 = (f16[4,264,128]{2,1,0:T(8,128)(2,1)S(1)}, f16[4,264,128]{2,1,0:T(8,128)(2,1)S(1)}, u32[]{:S(2)}, u32[]{:S(2)}) collective-permute-start(f16[4,264,128]{2,1,0:T(8,128)(2,1)S(1)} %pad_maximum_fusion), channel_id=1, source_target_pairs={{0,2},{1,3},{2,0},{3,1},{4,6},{5,7},{6,4},{7,5},{8,10},{9,11},{10,... | collective-permute-start | bytes 811016 | tf_op jit(solution)/shard_map/ppermute | solution.py:301
  58.6 6.1 %collective-permute-start.9 = (f32[2,2,128,128]{3,2,1,0:T(8,128)S(1)}, f32[2,2,128,128]{3,2,1,0:T(8,128)S(1)}, u32[]{:S(2)}, u32[]{:S(2)}) collective-permute-start(f32[2,2,128,128]{3,2,1,0:T(8,128)S(1)} %correlate.10), channel_id=1, source_target_pairs={{0,1},{1,0},{2,3},{3,2},{4,5},{5,4},{6,7},{7,6},{8,9},{9,8},{10,11... | collective-permute-start | bytes 786440 | tf_op jit(solution)/shard_map/ppermute | solution.py:295
  65.2 6.8 %collective-permute-start.10 = (f16[2,264,128]{2,1,0:T(8,128)(2,1)S(1)}, f16[2,264,128]{2,1,0:T(8,128)(2,1)S(1)}, u32[]{:S(2)}, u32[]{:S(2)}) collective-permute-start(f16[2,264,128]{2,1,0:T(8,128)(2,1)S(1)} %pad_maximum_fusion.2), channel_id=1, source_target_pairs={{0,2},{1,3},{2,0},{3,1},{4,6},{5,7},{6,4},{7,5},{8,10},{9,11},{10,... | collective-permute-start | bytes 405512 | tf_op jit(solution)/shard_map/ppermute | solution.py:306
  69.3 7.1 %collective-permute-start.13 = (f32[6,2,128,128]{3,2,1,0:T(8,128)S(1)}, f32[6,2,128,128]{3,2,1,0:T(8,128)S(1)}, u32[]{:S(2)}, u32[]{:S(2)}) collective-permute-start(f32[6,2,128,128]{3,2,1,0:T(8,128)S(1)} %get-tuple-element.34.refs_0_), channel_id=1, source_target_pairs={{0,1},{1,0},{2,3},{3,2},{4,5},{5,4},{6,7},{7,6},{8,9},{9,8},{10,11... | collective-permute-start | bytes 2359304 | tf_op jit(solution)/shard_map/ppermute | solution.py:318
  74.1 6.5 %collective-permute-start.12 = (f16[2,264,128]{2,1,0:T(8,128)(2,1)S(1)}, f16[2,264,128]{2,1,0:T(8,128)(2,1)S(1)}, u32[]{:S(2)}, u32[]{:S(2)}) collective-permute-start(f16[2,264,128]{2,1,0:T(8,128)(2,1)S(1)} %pad_maximum_fusion.4), channel_id=1, source_target_pairs={{240,0},{244,4},{248,8},{252,12},{0,16},{4,20},{8,24},{12,28},{16,... | collective-permute-start | bytes 405512 | tf_op jit(solution)/shard_map/ppermute | solution.py:316
  74.2 6.7 %collective-permute-start.11 = (f16[2,264,128]{2,1,0:T(8,128)(2,1)S(1)}, f16[2,264,128]{2,1,0:T(8,128)(2,1)S(1)}, u32[]{:S(2)}, u32[]{:S(2)}) collective-permute-start(f16[2,264,128]{2,1,0:T(8,128)(2,1)S(1)} %pad_maximum_fusion.3), channel_id=1, source_target_pairs={{12,0},{0,4},{4,8},{8,12},{28,16},{16,20},{20,24},{24,28},{44,32},... | collective-permute-start | bytes 405512 | tf_op jit(solution)/shard_map/ppermute | solution.py:317
  75.3 8.5 %collective-permute-start.15 = (f32[2,2,128,128]{3,2,1,0:T(8,128)S(1)}, f32[2,2,128,128]{3,2,1,0:T(8,128)S(1)}, u32[]{:S(2)}, u32[]{:S(2)}) collective-permute-start(f32[2,2,128,128]{3,2,1,0:T(8,128)S(1)} %get-tuple-element.39.refs_2_), channel_id=1, source_target_pairs={{0,1},{1,0},{2,3},{3,2},{4,5},{5,4},{6,7},{7,6},{8,9},{9,8},{10,11... | collective-permute-start | bytes 786440 | tf_op jit(solution)/shard_map/ppermute | solution.py:319
  81.0 2.7 %collective-permute-start.14 = (f16[4,264,128]{2,1,0:T(8,128)(2,1)S(1)}, f16[4,264,128]{2,1,0:T(8,128)(2,1)S(1)}, u32[]{:S(2)}, u32[]{:S(2)}) collective-permute-start(f16[4,264,128]{2,1,0:T(8,128)(2,1)S(1)} %pad_maximum_fusion.1), channel_id=1, source_target_pairs={{0,1},{1,0},{2,3},{3,2},{4,5},{5,4},{6,7},{7,6},{8,9},{9,8},{10,11... | collective-permute-start | bytes 811016 | tf_op jit(solution)/shard_map/ppermute | solution.py:326

commit v6 on v5

--- a/solution.py
+++ b/solution.py
@@ -81,17 +81,25 @@
     )(pltpu.with_memory_space_constraint(orbitals, pltpu.HBM))
 
 
-def correlate(meta, base, directions, cosines, sines, own, sources):
+def correlate(meta, base, directions, cosines, sines, own, sources, arrived=None):
     nb = own[0].shape[1] // 2
     points = own[0].shape[2]
 
-    def body(meta, cosines, sines, front, rear, first, second, out, arrived, left, phased, sems):
+    copying = arrived is None
+
+    def body(meta, cosines, sines, front, rear, *refs):
         copies = []
-        for p, source in enumerate((first, second)):
-            rows = pl.ds(pl.multiple_of(meta[0, base + p] * nb, nb), nb)
-            copies += [pltpu.make_async_copy(source.at[c, rows], arrived.at[p, c], sems.at[p, c]) for c in range(2)]
-        for copy in copies:
-            copy.start()
+        if copying:
+            first, second, out, ahead, left, phased, arrived, sems = refs
+            for n, (column, into) in enumerate(((base, arrived), (base + 2, ahead))):
+                for p, source in enumerate((first, second)):
+                    rows = pl.ds(pl.multiple_of(meta[0, column + p] * nb, nb), nb)
+                    for c in range(2):
+                        copies.append(pltpu.make_async_copy(source.at[c, rows], into.at[p, c], sems.at[n, p, c]))
+            for copy in copies:
+                copy.start()
+        else:
+            arrived, out, left, phased = refs
         for p in range(2):
             k = meta[1, base + p]
             lefts, shifted = left.at[p], phased.at[p]
@@ -106,8 +114,8 @@
             row = directions[p] * 4 + k
             cosine = cosines[pl.ds(row, 1), :]
             sine = sines[pl.ds(row, 1), :]
-            for c in range(2):
-                copies[2 * p + c].wait()
+            for copy in copies[2 * p : 2 * p + 2]:
+                copy.wait()
             source_re = arrived[p, 0].astype(F32)
             source_im = arrived[p, 1].astype(F32)
             shifted[0:nb, :] = (cosine * source_re + sine * source_im).astype(BF16)
@@ -115,21 +123,23 @@
             full = lax.dot_general(lefts[...], shifted[...], CONTRACT_LAST, preferred_element_type=F32)
             out[p, 0] = full[:nb, :nb] + full[nb:, nb:]
             out[p, 1] = full[:nb, nb:] - full[nb:, :nb]
-
+        for copy in copies[4:]:
+            copy.wait()
+
+    result = VMEM((2, 2, nb, nb), F32)
+    blocks = VMEM((2, 2, nb, points), BF16)
+    scratch = [VMEM((2, 2 * nb, points), BF16), VMEM((2, 2 * nb, points), BF16)]
+    if copying:
+        scratch += [blocks, pltpu.SemaphoreType.DMA((2, 2, 2))]
     return pl.pallas_call(
         body,
         name="correlate",
-        out_shape=VMEM((2, 2, nb, nb), F32),
-        in_specs=specs(pltpu.SMEM, *[VMEM] * 4, pl.ANY, pl.ANY),
-        out_specs=specs(VMEM)[0],
-        scratch_shapes=[
-            VMEM((2, 2, nb, points), BF16),
-            VMEM((2, 2 * nb, points), BF16),
-            VMEM((2, 2 * nb, points), BF16),
-            pltpu.SemaphoreType.DMA((2, 2)),
-        ],
+        out_shape=(result, blocks) if copying else result,
+        in_specs=specs(pltpu.SMEM, *[VMEM] * 4, *([pl.ANY, pl.ANY] if copying else [VMEM])),
+        out_specs=tuple(specs(VMEM, VMEM)) if copying else specs(VMEM)[0],
+        scratch_shapes=scratch,
         **small(8),
-    )(meta, *vmem(cosines, sines, *own), *sources)
+    )(meta, *vmem(cosines, sines, *own), *(sources if copying else vmem(arrived)))
 
 
 def split_parts(values):
@@ -290,10 +300,10 @@
     cosines, sines = jnp.cos(angles), jnp.sin(angles)
 
     def halves(meta, base, directions, sources, late=()):
-        give = correlate(meta, base, directions, cosines, sines, own, sources)
+        give, ahead = correlate(meta, base, directions, cosines, sines, own, sources)
         give, *late = lax.optimization_barrier((give, *late))
         got = lax.ppermute(give, "ga", sibling)
-        return got, correlate(meta, base + 2, directions, cosines, sines, own, sources), late
+        return got, correlate(meta, base + 2, directions, cosines, sines, own, None, ahead), late
 
     got, keep, _ = halves(meta, 0, (0, 0), own)
     got_front, keep_front, _ = halves(meta, 4, (1, 2), (beside_front, beyond_front))

time: 86.3 us -> 85.4 us (0.990)
  local copies, waits for them, and re-layouts: 0.94 us -> 4.37 us
  waiting for transfers between devices: 21.4 us -> 18.1 us
  Pallas kernels: 23.6 us -> 21.7 us
    unnamed x6 -> x14, local copies, waits for them, and re-layouts: 0.02 us -> 3.44 us
    ppermute x1, waiting for transfers between devices: 2.02 us -> 0.01 us  [shards(): beside_rear = lax.ppermute(rear, 'ka', ring_back)]
    pallas_call x6, Pallas kernels: 15.1 us -> 13.3 us  [correlate(): pl.pallas_call(body, name='correlate', out_shape=(result, blocks) if copy...]
    ppermute x1, waiting for transfers between devices: 2.16 us -> 1.19 us  [shards(): beside_front = lax.ppermute(front, 'ka', ring_back)]
    ppermute x1, starting transfers between devices: 1.7 us -> 2.56 us  [shards(): gauge_beyond = lax.ppermute(gauge_half, 'ka', outer_back)]
  transfers between devices with their start and end apart: 16 -> 16, of which waited for: 8 -> 6; matrix products, arithmetic and copies ran while one was open for 7% -> 7% of each run, Pallas kernels for 24% -> 22%
where the time goes in v6:
time: 85.4 us; the launch traced here: 84.9 us
  starting transfers between devices  34.1 us (40%)
  Pallas kernels  21.7 us (25%)
  waiting for transfers between devices  18.1 us (21%)
  other arithmetic  5.58 us (7%)
  local copies, waits for them, and re-layouts  4.37 us (5%)
  between operations  1.11 us (1%)
    pallas_call x6, Pallas kernels, correlate(): pl.pallas_call(body, name='correlate', out_shape=(result, blocks) if copy...  13.3 us
    ppermute x1, waiting for transfers between devices, shards(): beyond_front = lax.ppermute(front, 'ka', outer_back)  11.1 us
    ppermute x3, starting transfers between devices, halves(): got = lax.ppermute(give, 'ga', sibling)  8.61 us
    ppermute x1, starting transfers between devices, shards(): beyond_front = lax.ppermute(front, 'ka', outer_back)  7.49 us
    pallas_call x2, Pallas kernels, place(): pl.pallas_call(body, out_shape=(shape, shape), name='place', in_specs=spe...  3.6 us
    unnamed x14, local copies, waits for them, and re-layouts  3.44 us
    ppermute x1, starting transfers between devices, shards(): other = lax.ppermute(coded, 'ga', across)  2.71 us
    ppermute x1, starting transfers between devices, shards(): other_rear = lax.ppermute(coded_rear, 'ga', across)  2.71 us
  transfers between devices with their start and end apart: 16, of which 6 were waited for; matrix products, arithmetic and copies ran while one was open for 7% of the time, Pallas kernels for 22%

profile of v6, /device:TPU:1, one launch (start us, length us, event | category | flops | bytes accessed | tf_op | source)
XLA Modules:
  0.0 84.9 jit_solution(5546050478814626911)
XLA Ops:
  0.6 1.2 %load.2.front.refs_0_ = bf16[2,256,1024]{2,1,0:T(8,128)(2,1)S(1)} custom-call(bf16[2,4,128,1024]{3,2,1,0:T(8,128)(2,1)} %orbitals.3), custom_call_target="tpu_custom_call" | custom-call | flops 1 | bytes 1 | tf_op jit(solution)/shard_map/load/pallas_call | solution.py:73
  1.9 7.5 %collective-permute-start.2 = (bf16[2,256,1024]{2,1,0:T(8,128)(2,1)S(1)}, bf16[2,256,1024]{2,1,0:T(8,128)(2,1)S(1)}, u32[]{:S(2)}, u32[]{:S(2)}) collective-permute-start(bf16[2,256,1024]{2,1,0:T(8,128)(2,1)S(1)} %load.2.front.refs_0_), channel_id=1, source_target_pairs={{0,240},{4,244},{8,248},{12,252},{16,0},{20,4},{24,8},{28,12},{32,... | collective-permute-start | bytes 3145736 | tf_op jit(solution)/shard_map/ppermute | solution.py:271
  9.4 2.5 %collective-permute-start.1 = (bf16[2,256,1024]{2,1,0:T(8,128)(2,1)S(1)}, bf16[2,256,1024]{2,1,0:T(8,128)(2,1)}, u32[]{:S(2)}, u32[]{:S(2)}) collective-permute-start(bf16[2,256,1024]{2,1,0:T(8,128)(2,1)S(1)} %load.2.front.refs_0_), channel_id=1, source_target_pairs={{0,12},{4,0},{8,4},{12,8},{16,28},{20,16},{24,20},{28,24},{32,44},... | collective-permute-start | bytes 3145736 | tf_op jit(solution)/shard_map/ppermute | solution.py:272
  11.9 1.2 %load.3.rear.refs_1_ = bf16[2,256,1024]{2,1,0:T(8,128)(2,1)S(1)} custom-call(bf16[2,4,128,1024]{3,2,1,0:T(8,128)(2,1)} %orbitals.3), custom_call_target="tpu_custom_call" | custom-call | flops 1 | bytes 1 | tf_op jit(solution)/shard_map/load/pallas_call | solution.py:73
  13.1 0.2 collective-permute-start.5
  13.3 0.5 collective-permute-start.4
  14.3 0.1 concatenate.64
  14.6 0.1 copy.46
  14.7 0.1 copy.47
  14.8 0.1 copy.48
  14.9 0.2 add_reduce_fusion.2
  15.1 0.3 convert_reduce_fusion.1
  15.3 0.1 add_multiply_fusion.2
  15.5 0.3 fusion.6
  15.7 2.5 %correlate.6 = (f32[2,2,128,128]{3,2,1,0:T(8,128)}, bf16[2,2,128,1024]{3,2,1,0:T(8,128)(2,1)S(1)}) custom-call(s32[4,12]{1,0:T(4,128)S(1)} %pad_add_fusion.2.meta.slots, f32[12,1024]{1,0:T(8,128)S(1)} %get-tuple-element.72.cosines, f32[12,1024]{1,0:T(8,128)S(1)} %get-tuple-element.71.sines, bf16[2,256,1024]{2,1,0:T(8,128)(2,1)S(1)} %load.2.front.refs_0_, ...), custom_call_target="tpu_custom_call" | custom-call | flops 1 | bytes 1 | tf_op jit(solution)/shard_map/correlate/pallas_call | solution.py:134
  18.3 1.9 %collective-permute-start = (f32[2,2,128,128]{3,2,1,0:T(8,128)}, f32[2,2,128,128]{3,2,1,0:T(8,128)}, u32[]{:S(2)}, u32[]{:S(2)}) collective-permute-start(f32[2,2,128,128]{3,2,1,0:T(8,128)} %get-tuple-element.29), channel_id=1, source_target_pairs={{0,1},{1,0},{2,3},{3,2},{4,5},{5,4},{6,7},{7,6},{8,9},{9,8},{10,11... | collective-permute-start | bytes 786440 | tf_op jit(solution)/shard_map/ppermute | solution.py:305
  20.2 11.1 %collective-permute-done.2.refs_1_ = bf16[2,256,1024]{2,1,0:T(8,128)(2,1)S(1)} collective-permute-done((bf16[2,256,1024]{2,1,0:T(8,128)(2,1)S(1)}, bf16[2,256,1024]{2,1,0:T(8,128)(2,1)S(1)}, u32[]{:S(2)}, u32[]{:S(2)}) %collective-permute-start.2) | collective-permute-done | bytes 1048608 | tf_op jit(solution)/shard_map/ppermute | solution.py:271
  31.2 1.0 %copy-done.3 = bf16[2,256,1024]{2,1,0:T(8,128)(2,1)} copy-done((bf16[2,256,1024]{2,1,0:T(8,128)(2,1)}, bf16[2,256,1024]{2,1,0:T(8,128)(2,1)S(1)}, u32[]{:S(2)}) %copy-start.3) | copy-done | bytes 1048600
  32.2 1.2 %collective-permute-done.1.refs_0_ = bf16[2,256,1024]{2,1,0:T(8,128)(2,1)} collective-permute-done((bf16[2,256,1024]{2,1,0:T(8,128)(2,1)S(1)}, bf16[2,256,1024]{2,1,0:T(8,128)(2,1)}, u32[]{:S(2)}, u32[]{:S(2)}) %collective-permute-start.1) | collective-permute-done | bytes 1048608 | tf_op jit(solution)/shard_map/ppermute | solution.py:272
  33.4 1.2 %copy-done.4 = bf16[2,256,1024]{2,1,0:T(8,128)(2,1)S(1)} copy-done((bf16[2,256,1024]{2,1,0:T(8,128)(2,1)S(1)}, bf16[2,256,1024]{2,1,0:T(8,128)(2,1)}, u32[]{:S(2)}) %copy-start.4) | copy-done | bytes 1048600
  34.6 3.3 %correlate.8 = (f32[2,2,128,128]{3,2,1,0:T(8,128)}, bf16[2,2,128,1024]{3,2,1,0:T(8,128)(2,1)S(1)}) custom-call(s32[4,12]{1,0:T(4,128)S(1)} %pad_add_fusion.2.meta.slots, f32[12,1024]{1,0:T(8,128)S(1)} %get-tuple-element.72.cosines, f32[12,1024]{1,0:T(8,128)S(1)} %get-tuple-element.71.sines, bf16[2,256,1024]{2,1,0:T(8,128)(2,1)S(1)} %load.2.front.refs_0_, ...), custom_call_target="tpu_custom_call" | custom-call | flops 1 | bytes 1 | tf_op jit(solution)/shard_map/correlate/pallas_call | solution.py:134
  37.9 3.4 %collective-permute-start.3 = (f32[2,2,128,128]{3,2,1,0:T(8,128)}, f32[2,2,128,128]{3,2,1,0:T(8,128)}, u32[]{:S(2)}, u32[]{:S(2)}) collective-permute-start(f32[2,2,128,128]{3,2,1,0:T(8,128)} %get-tuple-element.31), channel_id=1, source_target_pairs={{0,1},{1,0},{2,3},{3,2},{4,5},{5,4},{6,7},{7,6},{8,9},{9,8},{10,11... | collective-permute-start | bytes 786440 | tf_op jit(solution)/shard_map/ppermute | solution.py:305
  41.4 2.6 %collective-permute-start.8 = (bf16[2,2,128,128]{3,2,1,0:T(8,128)(2,1)S(1)}, bf16[2,2,128,128]{3,2,1,0:T(8,128)(2,1)S(1)}, u32[]{:S(2)}, u32[]{:S(2)}) collective-permute-start(bf16[2,2,128,128]{3,2,1,0:T(8,128)(2,1)S(1)} %dynamic-slice_bitcast_fusion), channel_id=1, source_target_pairs={{0,240},{4,244},{8,248},{12,252},{16,0},{20,4},{24,8},{28,12},{32,... | collective-permute-start | bytes 393224 | tf_op jit(solution)/shard_map/ppermute | solution.py:278
  43.9 1.2 %copy-done.2 = bf16[2,2,128,1024]{3,2,1,0:T(8,128)(2,1)S(1)} copy-done((bf16[2,2,128,1024]{3,2,1,0:T(8,128)(2,1)S(1)}, bf16[2,2,128,1024]{3,2,1,0:T(8,128)(2,1)}, u32[]{:S(2)}) %copy-start.2) | copy-done | bytes 1048600
  45.2 1.6 %correlate.7 = f32[2,2,128,128]{3,2,1,0:T(8,128)S(1)} custom-call(s32[4,12]{1,0:T(4,128)S(1)} %pad_add_fusion.2.meta.slots, f32[12,1024]{1,0:T(8,128)S(1)} %get-tuple-element.72.cosines, f32[12,1024]{1,0:T(8,128)S(1)} %get-tuple-element.71.sines, bf16[2,256,1024]{2,1,0:T(8,128)(2,1)S(1)} %load.2.front.refs_0_, bf16[2,256,1024]{2,1,0:T(8,128)(2,1)S(1)} %load.3.rear.refs_1_, ...), custom_call_target="tpu_custom_call" | custom-call | flops 1 | bytes 1 | tf_op jit(solution)/shard_map/correlate/pallas_call | solution.py:134
  46.8 2.6 %collective-permute-start.7 = (bf16[2,2,128,128]{3,2,1,0:T(8,128)(2,1)S(1)}, bf16[2,2,128,128]{3,2,1,0:T(8,128)(2,1)S(1)}, u32[]{:S(2)}, u32[]{:S(2)}) collective-permute-start(bf16[2,2,128,128]{3,2,1,0:T(8,128)(2,1)S(1)} %dynamic-slice_bitcast_fusion), channel_id=1, source_target_pairs={{0,12},{4,0},{8,4},{12,8},{16,28},{20,16},{24,20},{28,24},{32,44},... | collective-permute-start | bytes 393224 | tf_op jit(solution)/shard_map/ppermute | solution.py:279
  49.3 1.0 %add.172 = f32[2,2,128,128]{3,2,1,0:T(8,128)S(1)} add(f32[2,2,128,128]{3,2,1,0:T(8,128)S(1)} %correlate.7, f32[2,2,128,128]{3,2,1,0:T(8,128)} %collective-permute-done) | non-fusion elementwise | flops 65536 | bytes 786432 | tf_op jit(solution)/shard_map/add | solution.py:310
  50.3 1.6 %correlate.9 = f32[2,2,128,128]{3,2,1,0:T(8,128)S(1)} custom-call(s32[4,12]{1,0:T(4,128)S(1)} %pad_add_fusion.2.meta.slots, f32[12,1024]{1,0:T(8,128)S(1)} %get-tuple-element.72.cosines, f32[12,1024]{1,0:T(8,128)S(1)} %get-tuple-element.71.sines, bf16[2,256,1024]{2,1,0:T(8,128)(2,1)S(1)} %load.2.front.refs_0_, bf16[2,256,1024]{2,1,0:T(8,128)(2,1)S(1)} %load.3.rear.refs_1_, ...), custom_call_target="tpu_custom_call" | custom-call | flops 1 | bytes 1 | tf_op jit(solution)/shard_map/correlate/pallas_call | solution.py:134
  51.9 1.0 %add.173 = f32[2,2,128,128]{3,2,1,0:T(8,128)S(1)} add(f32[2,2,128,128]{3,2,1,0:T(8,128)S(1)} %correlate.9, f32[2,2,128,128]{3,2,1,0:T(8,128)} %collective-permute-done.3) | non-fusion elementwise | flops 65536 | bytes 786432 | tf_op jit(solution)/shard_map/add | solution.py:310
  52.9 0.1 fusion.1
  53.0 0.1 fusion
  53.3 2.7 %collective-permute-start.6 = (f16[4,264,128]{2,1,0:T(8,128)(2,1)S(1)}, f16[4,264,128]{2,1,0:T(8,128)(2,1)S(1)}, u32[]{:S(2)}, u32[]{:S(2)}) collective-permute-start(f16[4,264,128]{2,1,0:T(8,128)(2,1)S(1)} %pad_maximum_fusion), channel_id=1, source_target_pairs={{0,2},{1,3},{2,0},{3,1},{4,6},{5,7},{6,4},{7,5},{8,10},{9,11},{10,... | collective-permute-start | bytes 811016 | tf_op jit(solution)/shard_map/ppermute | solution.py:311
  56.0 2.6 %correlate.10 = (f32[2,2,128,128]{3,2,1,0:T(8,128)S(1)}, bf16[2,2,128,1024]{3,2,1,0:T(8,128)(2,1)S(1)}) custom-call(s32[4,12]{1,0:T(4,128)S(1)} %pad_add_fusion.2.meta.slots, f32[12,1024]{1,0:T(8,128)S(1)} %get-tuple-element.72.cosines, f32[12,1024]{1,0:T(8,128)S(1)} %get-tuple-element.71.sines, bf16[2,256,1024]{2,1,0:T(8,128)(2,1)S(1)} %load.2.front.refs_0_, ...), custom_call_target="tpu_custom_call" | custom-call | flops 1 | bytes 1 | tf_op jit(solution)/shard_map/correlate/pallas_call | solution.py:134
  58.7 3.3 %collective-permute-start.9 = (f32[2,2,128,128]{3,2,1,0:T(8,128)S(1)}, f32[2,2,128,128]{3,2,1,0:T(8,128)S(1)}, u32[]{:S(2)}, u32[]{:S(2)}) collective-permute-start(f32[2,2,128,128]{3,2,1,0:T(8,128)S(1)} %get-tuple-element.36), channel_id=1, source_target_pairs={{0,1},{1,0},{2,3},{3,2},{4,5},{5,4},{6,7},{7,6},{8,9},{9,8},{10,11... | collective-permute-start | bytes 786440 | tf_op jit(solution)/shard_map/ppermute | solution.py:305
  62.1 1.6 %correlate.11 = f32[2,2,128,128]{3,2,1,0:T(8,128)S(1)} custom-call(s32[4,12]{1,0:T(4,128)S(1)} %pad_add_fusion.2.meta.slots, f32[12,1024]{1,0:T(8,128)S(1)} %get-tuple-element.72.cosines, f32[12,1024]{1,0:T(8,128)S(1)} %get-tuple-element.71.sines, bf16[2,256,1024]{2,1,0:T(8,128)(2,1)S(1)} %load.2.front.refs_0_, bf16[2,256,1024]{2,1,0:T(8,128)(2,1)S(1)} %load.3.rear.refs_1_, ...), custom_call_target="tpu_custom_call" | custom-call | flops 1 | bytes 1 | tf_op jit(solution)/shard_map/correlate/pallas_call | solution.py:134
  63.7 0.1 exponential_reduce_fusion.1
  63.8 0.1 exponential_reduce_fusion
  63.9 0.1 abs_reduce_fusion
  64.1 0.1 multiply_convert_fusion
  64.3 2.7 %collective-permute-start.10 = (f16[2,264,128]{2,1,0:T(8,128)(2,1)S(1)}, f16[2,264,128]{2,1,0:T(8,128)(2,1)S(1)}, u32[]{:S(2)}, u32[]{:S(2)}) collective-permute-start(f16[2,264,128]{2,1,0:T(8,128)(2,1)S(1)} %pad_maximum_fusion.2), channel_id=1, source_target_pairs={{0,2},{1,3},{2,0},{3,1},{4,6},{5,7},{6,4},{7,5},{8,10},{9,11},{10,... | collective-permute-start | bytes 405512 | tf_op jit(solution)/shard_map/ppermute | solution.py:316
  67.0 0.1 multiply_add_fusion
  67.2 1.3 %rotate.2 = (f32[6,2,128,128]{3,2,1,0:T(8,128)S(1)}, f32[1,2,128,128]{3,2,1,0:T(8,128)S(1)}, f32[1,2,128,128]{3,2,1,0:T(8,128)S(1)}) custom-call(s32[4,12]{1,0:T(4,128)S(1)} %pad_add_fusion.2.meta.slots, f32[4,2,128,128]{3,2,1,0:T(8,128)S(1)} %bitcast.35, bf16[2,4,128,128]{3,2,1,0:T(8,128)(2,1)S(1)} %copy-done, ...), custom_call_target="tpu_custom_call" | custom-call | flops 1 | bytes 1 | tf_op jit(solution)/shard_map/rotate/pallas_call | solution.py:210
  68.4 0.4 collective-permute-start.13
  68.8 0.1 fusion.41
  68.9 2.2 %collective-permute-done.10 = f16[2,264,128]{2,1,0:T(8,128)(2,1)S(1)} collective-permute-done((f16[2,264,128]{2,1,0:T(8,128)(2,1)S(1)}, f16[2,264,128]{2,1,0:T(8,128)(2,1)S(1)}, u32[]{:S(2)}, u32[]{:S(2)}) %collective-permute-start.10) | collective-permute-done | bytes 135200 | tf_op jit(solution)/shard_map/ppermute | solution.py:316
  71.1 0.1 fusion.42
  71.2 0.1 multiply_add_fusion.1
  71.3 1.1 %rotate.3 = (f32[2,2,128,128]{3,2,1,0:T(8,128)S(1)}, f32[1,2,128,128]{3,2,1,0:T(8,128)S(1)}, f32[1,2,128,128]{3,2,1,0:T(8,128)S(1)}) custom-call(s32[4,12]{1,0:T(4,128)S(1)} %pad_add_fusion.2.meta.slots, f32[2,2,128,128]{3,2,1,0:T(8,128)S(1)} %bitcast.37, bf16[2,4,128,128]{3,2,1,0:T(8,128)(2,1)S(1)} %copy-done, ...), custom_call_target="tpu_custom_call" | custom-call | flops 1 | bytes 1 | tf_op jit(solution)/shard_map/rotate/pallas_call | solution.py:210
  72.4 0.1 fusion.3
  72.6 0.1 fusion.2
  72.8 0.1 fusion.5
  72.9 0.1 fusion.4
  73.2 1.0 %collective-permute-start.11 = (f16[2,264,128]{2,1,0:T(8,128)(2,1)S(1)}, f16[2,264,128]{2,1,0:T(8,128)(2,1)S(1)}, u32[]{:S(2)}, u32[]{:S(2)}) collective-permute-start(f16[2,264,128]{2,1,0:T(8,128)(2,1)S(1)} %pad_maximum_fusion.3), channel_id=1, source_target_pairs={{12,0},{0,4},{4,8},{8,12},{28,16},{16,20},{20,24},{24,28},{44,32},... | collective-permute-start | bytes 405512 | tf_op jit(solution)/shard_map/ppermute | solution.py:327
  74.3 1.1 %collective-permute-start.15 = (f32[2,2,128,128]{3,2,1,0:T(8,128)S(1)}, f32[2,2,128,128]{3,2,1,0:T(8,128)S(1)}, u32[]{:S(2)}, u32[]{:S(2)}) collective-permute-start(f32[2,2,128,128]{3,2,1,0:T(8,128)S(1)} %get-tuple-element.51.refs_2_), channel_id=1, source_target_pairs={{0,1},{1,0},{2,3},{3,2},{4,5},{5,4},{6,7},{7,6},{8,9},{9,8},{10,11... | collective-permute-start | bytes 786440 | tf_op jit(solution)/shard_map/ppermute | solution.py:329
  75.4 1.8 %place.2 = (f32[3,2,4,128,128]{4,3,2,1,0:T(8,128)}, f32[3,2,4,128,128]{4,3,2,1,0:T(8,128)}) custom-call(s32[4,12]{1,0:T(4,128)S(1)} %pad_add_fusion.2.meta.slots, f32[6,2,128,128]{3,2,1,0:T(8,128)S(1)} %get-tuple-element.46.refs_0_, f32[6,2,128,128]{3,2,1,0:T(8,128)S(1)} %collective-permute-done.13.refs_1_), custom_call_target="tpu_custom_call" | custom-call | flops 1 | bytes 1 | tf_op jit(solution)/shard_map/place/pallas_call | solution.py:239
  77.2 2.4 %collective-permute-done.12 = f16[2,264,128]{2,1,0:T(8,128)(2,1)S(1)} collective-permute-done((f16[2,264,128]{2,1,0:T(8,128)(2,1)S(1)}, f16[2,264,128]{2,1,0:T(8,128)(2,1)S(1)}, u32[]{:S(2)}, u32[]{:S(2)}) %collective-permute-start.12) | collective-permute-done | bytes 135200 | tf_op jit(solution)/shard_map/ppermute | solution.py:326
  79.6 0.3 collective-permute-done.11
  80.0 1.5 %collective-permute-start.14 = (f16[4,264,128]{2,1,0:T(8,128)(2,1)S(1)}, f16[4,264,128]{2,1,0:T(8,128)(2,1)S(1)}, u32[]{:S(2)}, u32[]{:S(2)}) collective-permute-start(f16[4,264,128]{2,1,0:T(8,128)(2,1)S(1)} %pad_maximum_fusion.1), channel_id=1, source_target_pairs={{0,1},{1,0},{2,3},{3,2},{4,5},{5,4},{6,7},{7,6},{8,9},{9,8},{10,11... | collective-permute-start | bytes 811016 | tf_op jit(solution)/shard_map/ppermute | solution.py:336
  81.5 0.1 fusion.33
  81.6 0.1 convert_multiply_fusion.1
  81.7 0.9 %collective-permute-done.14 = f16[4,264,128]{2,1,0:T(8,128)(2,1)S(1)} collective-permute-done((f16[4,264,128]{2,1,0:T(8,128)(2,1)S(1)}, f16[4,264,128]{2,1,0:T(8,128)(2,1)S(1)}, u32[]{:S(2)}, u32[]{:S(2)}) %collective-permute-start.14) | collective-permute-done | bytes 270368 | tf_op jit(solution)/shard_map/ppermute | solution.py:336
  82.7 0.1 fusion.34
  82.8 0.1 convert_multiply_fusion
  82.9 1.8 %place.3 = (f32[3,2,4,128,128]{4,3,2,1,0:T(8,128)}, f32[3,2,4,128,128]{4,3,2,1,0:T(8,128)}) custom-call(s32[4,12]{1,0:T(4,128)S(1)} %pad_add_fusion.2.meta.slots, f32[4,2,128,128]{3,2,1,0:T(8,128)S(1)} %bitcast.33, f32[4,2,128,128]{3,2,1,0:T(8,128)S(1)} %bitcast.34, ...), custom_call_target="tpu_custom_call", output_to_operand_aliasing={{0}: (5, {}), {1}: (6, {})} | custom-call | flops 1 | bytes 1 | tf_op jit(solution)/shard_map/place/pallas_call | solution.py:239
  (51 shorter events, 1.4 us)
Async XLA Ops:
  1.9 12.1 %copy-start.6 = (s32[256,3]{0,1:T(4,128)S(1)}, s32[256,3]{0,1:T(4,128)}, u32[]{:S(2)}) copy-start(s32[256,3]{0,1:T(4,128)} %param.6) | copy-start | bytes 9220
  1.9 12.6 %copy-start.5 = (s32[256,3,3]{0,2,1:T(4,128)S(1)}, s32[256,3,3]{0,2,1:T(4,128)}, u32[]{:S(2)}) copy-start(s32[256,3,3]{0,2,1:T(4,128)} %param.7) | copy-start | bytes 27652
  1.9 29.3 %collective-permute-start.2 = (bf16[2,256,1024]{2,1,0:T(8,128)(2,1)S(1)}, bf16[2,256,1024]{2,1,0:T(8,128)(2,1)S(1)}, u32[]{:S(2)}, u32[]{:S(2)}) collective-permute-start(bf16[2,256,1024]{2,1,0:T(8,128)(2,1)S(1)} %load.2.front.refs_0_), channel_id=1, source_target_pairs={{0,240},{4,244},{8,248},{12,252},{16,0},{20,4},{24,8},{28,12},{32,... | collective-permute-start | bytes 3145736 | tf_op jit(solution)/shard_map/ppermute | solution.py:271
  9.4 24.0 %collective-permute-start.1 = (bf16[2,256,1024]{2,1,0:T(8,128)(2,1)S(1)}, bf16[2,256,1024]{2,1,0:T(8,128)(2,1)}, u32[]{:S(2)}, u32[]{:S(2)}) collective-permute-start(bf16[2,256,1024]{2,1,0:T(8,128)(2,1)S(1)} %load.2.front.refs_0_), channel_id=1, source_target_pairs={{0,12},{4,0},{8,4},{12,8},{16,28},{20,16},{24,20},{28,24},{32,44},... | collective-permute-start | bytes 3145736 | tf_op jit(solution)/shard_map/ppermute | solution.py:272
  13.1 43.0 %collective-permute-start.5 = (bf16[2,256,1024]{2,1,0:T(8,128)(2,1)S(1)}, bf16[2,256,1024]{2,1,0:T(8,128)(2,1)}, u32[]{:S(2)}, u32[]{:S(2)}) collective-permute-start(bf16[2,256,1024]{2,1,0:T(8,128)(2,1)S(1)} %load.3.rear.refs_1_), channel_id=1, source_target_pairs={{0,240},{4,244},{8,248},{12,252},{16,0},{20,4},{24,8},{28,12},{32,... | collective-permute-start | bytes 3145736 | tf_op jit(solution)/shard_map/ppermute | solution.py:274
  13.3 42.7 %collective-permute-start.4 = (bf16[2,256,1024]{2,1,0:T(8,128)(2,1)S(1)}, bf16[2,256,1024]{2,1,0:T(8,128)(2,1)}, u32[]{:S(2)}, u32[]{:S(2)}) collective-permute-start(bf16[2,256,1024]{2,1,0:T(8,128)(2,1)S(1)} %load.3.rear.refs_1_), channel_id=1, source_target_pairs={{0,12},{4,0},{8,4},{12,8},{16,28},{20,16},{24,20},{28,24},{32,44},... | collective-permute-start | bytes 3145736 | tf_op jit(solution)/shard_map/ppermute | solution.py:275
  18.3 19.7 %copy-start.1 = (bf16[2,2,128,1024]{3,2,1,0:T(8,128)(2,1)}, bf16[2,2,128,1024]{3,2,1,0:T(8,128)(2,1)S(1)}, u32[]{:S(2)}) copy-start(bf16[2,2,128,1024]{3,2,1,0:T(8,128)(2,1)S(1)} %get-tuple-element.28.refs_0_) | copy-start | bytes 3145732
  18.3 23.1 %copy-start = (bf16[2,4,128,128]{3,2,1,0:T(8,128)(2,1)S(1)}, bf16[2,4,128,128]{3,2,1,0:T(8,128)(2,1)}, u32[]{:S(2)}) copy-start(bf16[2,4,128,128]{3,2,1,0:T(8,128)(2,1)} %gauge.3) | copy-start | bytes 786436
  18.3 28.5 %collective-permute-start = (f32[2,2,128,128]{3,2,1,0:T(8,128)}, f32[2,2,128,128]{3,2,1,0:T(8,128)}, u32[]{:S(2)}, u32[]{:S(2)}) collective-permute-start(f32[2,2,128,128]{3,2,1,0:T(8,128)} %get-tuple-element.29), channel_id=1, source_target_pairs={{0,1},{1,0},{2,3},{3,2},{4,5},{5,4},{6,7},{7,6},{8,9},{9,8},{10,11... | collective-permute-start | bytes 786440 | tf_op jit(solution)/shard_map/ppermute | solution.py:305
  31.2 1.0 %copy-start.3 = (bf16[2,256,1024]{2,1,0:T(8,128)(2,1)}, bf16[2,256,1024]{2,1,0:T(8,128)(2,1)S(1)}, u32[]{:S(2)}) copy-start(bf16[2,256,1024]{2,1,0:T(8,128)(2,1)S(1)} %collective-permute-done.2.refs_1_) | copy-start | bytes 3145732
  33.4 1.2 %copy-start.4 = (bf16[2,256,1024]{2,1,0:T(8,128)(2,1)S(1)}, bf16[2,256,1024]{2,1,0:T(8,128)(2,1)}, u32[]{:S(2)}) copy-start(bf16[2,256,1024]{2,1,0:T(8,128)(2,1)} %copy-done.3) | copy-start | bytes 3145732
  37.9 14.0 %collective-permute-start.3 = (f32[2,2,128,128]{3,2,1,0:T(8,128)}, f32[2,2,128,128]{3,2,1,0:T(8,128)}, u32[]{:S(2)}, u32[]{:S(2)}) collective-permute-start(f32[2,2,128,128]{3,2,1,0:T(8,128)} %get-tuple-element.31), channel_id=1, source_target_pairs={{0,1},{1,0},{2,3},{3,2},{4,5},{5,4},{6,7},{7,6},{8,9},{9,8},{10,11... | collective-permute-start | bytes 786440 | tf_op jit(solution)/shard_map/ppermute | solution.py:305
  41.4 17.3 %collective-permute-start.8 = (bf16[2,2,128,128]{3,2,1,0:T(8,128)(2,1)S(1)}, bf16[2,2,128,128]{3,2,1,0:T(8,128)(2,1)S(1)}, u32[]{:S(2)}, u32[]{:S(2)}) collective-permute-start(bf16[2,2,128,128]{3,2,1,0:T(8,128)(2,1)S(1)} %dynamic-slice_bitcast_fusion), channel_id=1, source_target_pairs={{0,240},{4,244},{8,248},{12,252},{16,0},{20,4},{24,8},{28,12},{32,... | collective-permute-start | bytes 393224 | tf_op jit(solution)/shard_map/ppermute | solution.py:278
  43.9 1.2 %copy-start.2 = (bf16[2,2,128,1024]{3,2,1,0:T(8,128)(2,1)S(1)}, bf16[2,2,128,1024]{3,2,1,0:T(8,128)(2,1)}, u32[]{:S(2)}) copy-start(bf16[2,2,128,1024]{3,2,1,0:T(8,128)(2,1)} %copy-done.1) | copy-start | bytes 3145732
  46.8 12.0 %collective-permute-start.7 = (bf16[2,2,128,128]{3,2,1,0:T(8,128)(2,1)S(1)}, bf16[2,2,128,128]{3,2,1,0:T(8,128)(2,1)S(1)}, u32[]{:S(2)}, u32[]{:S(2)}) collective-permute-start(bf16[2,2,128,128]{3,2,1,0:T(8,128)(2,1)S(1)} %dynamic-slice_bitcast_fusion), channel_id=1, source_target_pairs={{0,12},{4,0},{8,4},{12,8},{16,28},{20,16},{24,20},{28,24},{32,44},... | collective-permute-start | bytes 393224 | tf_op jit(solution)/shard_map/ppermute | solution.py:279
  53.3 10.5 %collective-permute-start.6 = (f16[4,264,128]{2,1,0:T(8,128)(2,1)S(1)}, f16[4,264,128]{2,1,0:T(8,128)(2,1)S(1)}, u32[]{:S(2)}, u32[]{:S(2)}) collective-permute-start(f16[4,264,128]{2,1,0:T(8,128)(2,1)S(1)} %pad_maximum_fusion), channel_id=1, source_target_pairs={{0,2},{1,3},{2,0},{3,1},{4,6},{5,7},{6,4},{7,5},{8,10},{9,11},{10,... | collective-permute-start | bytes 811016 | tf_op jit(solution)/shard_map/ppermute | solution.py:311
  58.7 5.1 %collective-permute-start.9 = (f32[2,2,128,128]{3,2,1,0:T(8,128)S(1)}, f32[2,2,128,128]{3,2,1,0:T(8,128)S(1)}, u32[]{:S(2)}, u32[]{:S(2)}) collective-permute-start(f32[2,2,128,128]{3,2,1,0:T(8,128)S(1)} %get-tuple-element.36), channel_id=1, source_target_pairs={{0,1},{1,0},{2,3},{3,2},{4,5},{5,4},{6,7},{7,6},{8,9},{9,8},{10,11... | collective-permute-start | bytes 786440 | tf_op jit(solution)/shard_map/ppermute | solution.py:305
  64.3 6.8 %collective-permute-start.10 = (f16[2,264,128]{2,1,0:T(8,128)(2,1)S(1)}, f16[2,264,128]{2,1,0:T(8,128)(2,1)S(1)}, u32[]{:S(2)}, u32[]{:S(2)}) collective-permute-start(f16[2,264,128]{2,1,0:T(8,128)(2,1)S(1)} %pad_maximum_fusion.2), channel_id=1, source_target_pairs={{0,2},{1,3},{2,0},{3,1},{4,6},{5,7},{6,4},{7,5},{8,10},{9,11},{10,... | collective-permute-start | bytes 405512 | tf_op jit(solution)/shard_map/ppermute | solution.py:316
  68.4 7.0 %collective-permute-start.13 = (f32[6,2,128,128]{3,2,1,0:T(8,128)S(1)}, f32[6,2,128,128]{3,2,1,0:T(8,128)S(1)}, u32[]{:S(2)}, u32[]{:S(2)}) collective-permute-start(f32[6,2,128,128]{3,2,1,0:T(8,128)S(1)} %get-tuple-element.46.refs_0_), channel_id=1, source_target_pairs={{0,1},{1,0},{2,3},{3,2},{4,5},{5,4},{6,7},{7,6},{8,9},{9,8},{10,11... | collective-permute-start | bytes 2359304 | tf_op jit(solution)/shard_map/ppermute | solution.py:328
  73.2 6.5 %collective-permute-start.12 = (f16[2,264,128]{2,1,0:T(8,128)(2,1)S(1)}, f16[2,264,128]{2,1,0:T(8,128)(2,1)S(1)}, u32[]{:S(2)}, u32[]{:S(2)}) collective-permute-start(f16[2,264,128]{2,1,0:T(8,128)(2,1)S(1)} %pad_maximum_fusion.4), channel_id=1, source_target_pairs={{240,0},{244,4},{248,8},{252,12},{0,16},{4,20},{8,24},{12,28},{16,... | collective-permute-start | bytes 405512 | tf_op jit(solution)/shard_map/ppermute | solution.py:326
  73.2 6.7 %collective-permute-start.11 = (f16[2,264,128]{2,1,0:T(8,128)(2,1)S(1)}, f16[2,264,128]{2,1,0:T(8,128)(2,1)S(1)}, u32[]{:S(2)}, u32[]{:S(2)}) collective-permute-start(f16[2,264,128]{2,1,0:T(8,128)(2,1)S(1)} %pad_maximum_fusion.3), channel_id=1, source_target_pairs={{12,0},{0,4},{4,8},{8,12},{28,16},{16,20},{20,24},{24,28},{44,32},... | collective-permute-start | bytes 405512 | tf_op jit(solution)/shard_map/ppermute | solution.py:327
  74.3 8.6 %collective-permute-start.15 = (f32[2,2,128,128]{3,2,1,0:T(8,128)S(1)}, f32[2,2,128,128]{3,2,1,0:T(8,128)S(1)}, u32[]{:S(2)}, u32[]{:S(2)}) collective-permute-start(f32[2,2,128,128]{3,2,1,0:T(8,128)S(1)} %get-tuple-element.51.refs_2_), channel_id=1, source_target_pairs={{0,1},{1,0},{2,3},{3,2},{4,5},{5,4},{6,7},{7,6},{8,9},{9,8},{10,11... | collective-permute-start | bytes 786440 | tf_op jit(solution)/shard_map/ppermute | solution.py:329
  80.0 2.7 %collective-permute-start.14 = (f16[4,264,128]{2,1,0:T(8,128)(2,1)S(1)}, f16[4,264,128]{2,1,0:T(8,128)(2,1)S(1)}, u32[]{:S(2)}, u32[]{:S(2)}) collective-permute-start(f16[4,264,128]{2,1,0:T(8,128)(2,1)S(1)} %pad_maximum_fusion.1), channel_id=1, source_target_pairs={{0,1},{1,0},{2,3},{3,2},{4,5},{5,4},{6,7},{7,6},{8,9},{9,8},{10,11... | collective-permute-start | bytes 811016 | tf_op jit(solution)/shard_map/ppermute | solution.py:336

commit v7 on v6

--- a/solution.py
+++ b/solution.py
@@ -323,8 +323,9 @@
         meta, (10, 11), decode(coded_rear) + decode(other_rear), gauge, gauges, ((0, 1), (1, 1)),
         [[(0, 0), (1, 0)], [(0, 1)], [(1, 1)]],
     )
-    adj_y = lax.ppermute(encode(jnp.concatenate([adj_y, adj_y_rear], axis=0)), "ka", outer_ahead)
-    adj_x = lax.ppermute(encode(jnp.concatenate([adj_x, adj_x_rear], axis=0)), "ka", ring_ahead)
+    adjoints = encode(jnp.concatenate([adj_y, adj_y_rear, adj_x, adj_x_rear], axis=0))
+    adj_y = lax.ppermute(adjoints[:2], "ka", outer_ahead)
+    adj_x = lax.ppermute(adjoints[2:], "ka", ring_ahead)
     first_sib = lax.ppermute(first, "ga", sibling)
     last_sib = lax.ppermute(last, "ga", sibling)
     targets = [

time: 85.4 us -> 85.2 us (level)
  no operation moved by 1% of the time
where the time goes in v7:
time: 85.2 us; the launch traced here: 84.7 us
  starting transfers between devices  34.2 us (40%)
  Pallas kernels  21.7 us (25%)
  waiting for transfers between devices  18 us (21%)
  other arithmetic  5.4 us (6%)
  local copies, waits for them, and re-layouts  4.35 us (5%)
  between operations  1.1 us (1%)
    pallas_call x6, Pallas kernels, correlate(): pl.pallas_call(body, name='correlate', out_shape=(result, blocks) if copy...  13.3 us
    ppermute x1, waiting for transfers between devices, shards(): beyond_front = lax.ppermute(front, 'ka', outer_back)  11.1 us
    ppermute x3, starting transfers between devices, halves(): got = lax.ppermute(give, 'ga', sibling)  8.58 us
    ppermute x1, starting transfers between devices, shards(): beyond_front = lax.ppermute(front, 'ka', outer_back)  7.49 us
    pallas_call x2, Pallas kernels, place(): pl.pallas_call(body, out_shape=(shape, shape), name='place', in_specs=spe...  3.6 us
    unnamed x14, local copies, waits for them, and re-layouts  3.44 us
    ppermute x1, starting transfers between devices, shards(): other_rear = lax.ppermute(coded_rear, 'ga', across)  2.72 us
    ppermute x1, starting transfers between devices, shards(): other = lax.ppermute(coded, 'ga', across)  2.71 us
  transfers between devices with their start and end apart: 16, of which 6 were waited for; matrix products, arithmetic and copies ran while one was open for 7% of the time, Pallas kernels for 22%

profile of v7, /device:TPU:1, one launch (start us, length us, event | category | flops | bytes accessed | tf_op | source)
XLA Modules:
  0.0 84.7 jit_solution(5156179479342982304)
XLA Ops:
  0.6 1.2 %load.2.front.refs_0_ = bf16[2,256,1024]{2,1,0:T(8,128)(2,1)S(1)} custom-call(bf16[2,4,128,1024]{3,2,1,0:T(8,128)(2,1)} %orbitals.3), custom_call_target="tpu_custom_call" | custom-call | flops 1 | bytes 1 | tf_op jit(solution)/shard_map/load/pallas_call | solution.py:73
  1.9 7.5 %collective-permute-start.2 = (bf16[2,256,1024]{2,1,0:T(8,128)(2,1)S(1)}, bf16[2,256,1024]{2,1,0:T(8,128)(2,1)S(1)}, u32[]{:S(2)}, u32[]{:S(2)}) collective-permute-start(bf16[2,256,1024]{2,1,0:T(8,128)(2,1)S(1)} %load.2.front.refs_0_), channel_id=1, source_target_pairs={{0,240},{4,244},{8,248},{12,252},{16,0},{20,4},{24,8},{28,12},{32,... | collective-permute-start | bytes 3145736 | tf_op jit(solution)/shard_map/ppermute | solution.py:271
  9.4 2.5 %collective-permute-start.1 = (bf16[2,256,1024]{2,1,0:T(8,128)(2,1)S(1)}, bf16[2,256,1024]{2,1,0:T(8,128)(2,1)}, u32[]{:S(2)}, u32[]{:S(2)}) collective-permute-start(bf16[2,256,1024]{2,1,0:T(8,128)(2,1)S(1)} %load.2.front.refs_0_), channel_id=1, source_target_pairs={{0,12},{4,0},{8,4},{12,8},{16,28},{20,16},{24,20},{28,24},{32,44},... | collective-permute-start | bytes 3145736 | tf_op jit(solution)/shard_map/ppermute | solution.py:272
  11.9 1.2 %load.3.rear.refs_1_ = bf16[2,256,1024]{2,1,0:T(8,128)(2,1)S(1)} custom-call(bf16[2,4,128,1024]{3,2,1,0:T(8,128)(2,1)} %orbitals.3), custom_call_target="tpu_custom_call" | custom-call | flops 1 | bytes 1 | tf_op jit(solution)/shard_map/load/pallas_call | solution.py:73
  13.1 0.2 collective-permute-start.5
  13.3 0.5 collective-permute-start.4
  14.1 0.1 select_reduce_fusion.4
  14.2 0.1 select_reduce_fusion.1
  14.3 0.1 concatenate.54
  14.6 0.1 copy.46
  14.7 0.1 copy.47
  14.8 0.1 copy.48
  14.9 0.2 add_reduce_fusion.2
  15.1 0.3 convert_reduce_fusion.1
  15.3 0.1 add_multiply_fusion.2
  15.5 0.3 fusion.4
  15.7 2.5 %correlate.6 = (f32[2,2,128,128]{3,2,1,0:T(8,128)}, bf16[2,2,128,1024]{3,2,1,0:T(8,128)(2,1)S(1)}) custom-call(s32[4,12]{1,0:T(4,128)S(1)} %pad_add_fusion.2.meta.slots, f32[12,1024]{1,0:T(8,128)S(1)} %get-tuple-element.74.cosines, f32[12,1024]{1,0:T(8,128)S(1)} %get-tuple-element.73.sines, bf16[2,256,1024]{2,1,0:T(8,128)(2,1)S(1)} %load.2.front.refs_0_, ...), custom_call_target="tpu_custom_call" | custom-call | flops 1 | bytes 1 | tf_op jit(solution)/shard_map/correlate/pallas_call | solution.py:134
  18.3 1.9 %collective-permute-start = (f32[2,2,128,128]{3,2,1,0:T(8,128)}, f32[2,2,128,128]{3,2,1,0:T(8,128)}, u32[]{:S(2)}, u32[]{:S(2)}) collective-permute-start(f32[2,2,128,128]{3,2,1,0:T(8,128)} %get-tuple-element.29), channel_id=1, source_target_pairs={{0,1},{1,0},{2,3},{3,2},{4,5},{5,4},{6,7},{7,6},{8,9},{9,8},{10,11... | collective-permute-start | bytes 786440 | tf_op jit(solution)/shard_map/ppermute | solution.py:305
  20.2 11.1 %collective-permute-done.2.refs_1_ = bf16[2,256,1024]{2,1,0:T(8,128)(2,1)S(1)} collective-permute-done((bf16[2,256,1024]{2,1,0:T(8,128)(2,1)S(1)}, bf16[2,256,1024]{2,1,0:T(8,128)(2,1)S(1)}, u32[]{:S(2)}, u32[]{:S(2)}) %collective-permute-start.2) | collective-permute-done | bytes 1048608 | tf_op jit(solution)/shard_map/ppermute | solution.py:271
  31.2 1.0 %copy-done.3 = bf16[2,256,1024]{2,1,0:T(8,128)(2,1)} copy-done((bf16[2,256,1024]{2,1,0:T(8,128)(2,1)}, bf16[2,256,1024]{2,1,0:T(8,128)(2,1)S(1)}, u32[]{:S(2)}) %copy-start.3) | copy-done | bytes 1048600
  32.2 1.2 %collective-permute-done.1.refs_0_ = bf16[2,256,1024]{2,1,0:T(8,128)(2,1)} collective-permute-done((bf16[2,256,1024]{2,1,0:T(8,128)(2,1)S(1)}, bf16[2,256,1024]{2,1,0:T(8,128)(2,1)}, u32[]{:S(2)}, u32[]{:S(2)}) %collective-permute-start.1) | collective-permute-done | bytes 1048608 | tf_op jit(solution)/shard_map/ppermute | solution.py:272
  33.4 1.2 %copy-done.4 = bf16[2,256,1024]{2,1,0:T(8,128)(2,1)S(1)} copy-done((bf16[2,256,1024]{2,1,0:T(8,128)(2,1)S(1)}, bf16[2,256,1024]{2,1,0:T(8,128)(2,1)}, u32[]{:S(2)}) %copy-start.4) | copy-done | bytes 1048600
  34.6 3.3 %correlate.8 = (f32[2,2,128,128]{3,2,1,0:T(8,128)}, bf16[2,2,128,1024]{3,2,1,0:T(8,128)(2,1)S(1)}) custom-call(s32[4,12]{1,0:T(4,128)S(1)} %pad_add_fusion.2.meta.slots, f32[12,1024]{1,0:T(8,128)S(1)} %get-tuple-element.74.cosines, f32[12,1024]{1,0:T(8,128)S(1)} %get-tuple-element.73.sines, bf16[2,256,1024]{2,1,0:T(8,128)(2,1)S(1)} %load.2.front.refs_0_, ...), custom_call_target="tpu_custom_call" | custom-call | flops 1 | bytes 1 | tf_op jit(solution)/shard_map/correlate/pallas_call | solution.py:134
  38.0 3.4 %collective-permute-start.3 = (f32[2,2,128,128]{3,2,1,0:T(8,128)}, f32[2,2,128,128]{3,2,1,0:T(8,128)}, u32[]{:S(2)}, u32[]{:S(2)}) collective-permute-start(f32[2,2,128,128]{3,2,1,0:T(8,128)} %get-tuple-element.31), channel_id=1, source_target_pairs={{0,1},{1,0},{2,3},{3,2},{4,5},{5,4},{6,7},{7,6},{8,9},{9,8},{10,11... | collective-permute-start | bytes 786440 | tf_op jit(solution)/shard_map/ppermute | solution.py:305
  41.4 2.6 %collective-permute-start.8 = (bf16[2,2,128,128]{3,2,1,0:T(8,128)(2,1)S(1)}, bf16[2,2,128,128]{3,2,1,0:T(8,128)(2,1)S(1)}, u32[]{:S(2)}, u32[]{:S(2)}) collective-permute-start(bf16[2,2,128,128]{3,2,1,0:T(8,128)(2,1)S(1)} %dynamic-slice_bitcast_fusion), channel_id=1, source_target_pairs={{0,240},{4,244},{8,248},{12,252},{16,0},{20,4},{24,8},{28,12},{32,... | collective-permute-start | bytes 393224 | tf_op jit(solution)/shard_map/ppermute | solution.py:278
  44.0 1.2 %copy-done.2 = bf16[2,2,128,1024]{3,2,1,0:T(8,128)(2,1)S(1)} copy-done((bf16[2,2,128,1024]{3,2,1,0:T(8,128)(2,1)S(1)}, bf16[2,2,128,1024]{3,2,1,0:T(8,128)(2,1)}, u32[]{:S(2)}) %copy-start.2) | copy-done | bytes 1048600
  45.2 1.6 %correlate.7 = f32[2,2,128,128]{3,2,1,0:T(8,128)S(1)} custom-call(s32[4,12]{1,0:T(4,128)S(1)} %pad_add_fusion.2.meta.slots, f32[12,1024]{1,0:T(8,128)S(1)} %get-tuple-element.74.cosines, f32[12,1024]{1,0:T(8,128)S(1)} %get-tuple-element.73.sines, bf16[2,256,1024]{2,1,0:T(8,128)(2,1)S(1)} %load.2.front.refs_0_, bf16[2,256,1024]{2,1,0:T(8,128)(2,1)S(1)} %load.3.rear.refs_1_, ...), custom_call_target="tpu_custom_call" | custom-call | flops 1 | bytes 1 | tf_op jit(solution)/shard_map/correlate/pallas_call | solution.py:134
  46.8 2.6 %collective-permute-start.7 = (bf16[2,2,128,128]{3,2,1,0:T(8,128)(2,1)S(1)}, bf16[2,2,128,128]{3,2,1,0:T(8,128)(2,1)S(1)}, u32[]{:S(2)}, u32[]{:S(2)}) collective-permute-start(bf16[2,2,128,128]{3,2,1,0:T(8,128)(2,1)S(1)} %dynamic-slice_bitcast_fusion), channel_id=1, source_target_pairs={{0,12},{4,0},{8,4},{12,8},{16,28},{20,16},{24,20},{28,24},{32,44},... | collective-permute-start | bytes 393224 | tf_op jit(solution)/shard_map/ppermute | solution.py:279
  49.3 1.0 %add.172 = f32[2,2,128,128]{3,2,1,0:T(8,128)S(1)} add(f32[2,2,128,128]{3,2,1,0:T(8,128)S(1)} %correlate.7, f32[2,2,128,128]{3,2,1,0:T(8,128)} %collective-permute-done) | non-fusion elementwise | flops 65536 | bytes 786432 | tf_op jit(solution)/shard_map/add | solution.py:310
  50.3 1.6 %correlate.9 = f32[2,2,128,128]{3,2,1,0:T(8,128)S(1)} custom-call(s32[4,12]{1,0:T(4,128)S(1)} %pad_add_fusion.2.meta.slots, f32[12,1024]{1,0:T(8,128)S(1)} %get-tuple-element.74.cosines, f32[12,1024]{1,0:T(8,128)S(1)} %get-tuple-element.73.sines, bf16[2,256,1024]{2,1,0:T(8,128)(2,1)S(1)} %load.2.front.refs_0_, bf16[2,256,1024]{2,1,0:T(8,128)(2,1)S(1)} %load.3.rear.refs_1_, ...), custom_call_target="tpu_custom_call" | custom-call | flops 1 | bytes 1 | tf_op jit(solution)/shard_map/correlate/pallas_call | solution.py:134
  51.9 1.0 %add.173 = f32[2,2,128,128]{3,2,1,0:T(8,128)S(1)} add(f32[2,2,128,128]{3,2,1,0:T(8,128)S(1)} %correlate.9, f32[2,2,128,128]{3,2,1,0:T(8,128)} %collective-permute-done.3) | non-fusion elementwise | flops 65536 | bytes 786432 | tf_op jit(solution)/shard_map/add | solution.py:310
  52.9 0.1 fusion.1
  53.1 0.1 fusion
  53.4 2.7 %collective-permute-start.6 = (f16[4,264,128]{2,1,0:T(8,128)(2,1)S(1)}, f16[4,264,128]{2,1,0:T(8,128)(2,1)S(1)}, u32[]{:S(2)}, u32[]{:S(2)}) collective-permute-start(f16[4,264,128]{2,1,0:T(8,128)(2,1)S(1)} %pad_maximum_fusion), channel_id=1, source_target_pairs={{0,2},{1,3},{2,0},{3,1},{4,6},{5,7},{6,4},{7,5},{8,10},{9,11},{10,... | collective-permute-start | bytes 811016 | tf_op jit(solution)/shard_map/ppermute | solution.py:311
  56.1 2.6 %correlate.10 = (f32[2,2,128,128]{3,2,1,0:T(8,128)S(1)}, bf16[2,2,128,1024]{3,2,1,0:T(8,128)(2,1)S(1)}) custom-call(s32[4,12]{1,0:T(4,128)S(1)} %pad_add_fusion.2.meta.slots, f32[12,1024]{1,0:T(8,128)S(1)} %get-tuple-element.74.cosines, f32[12,1024]{1,0:T(8,128)S(1)} %get-tuple-element.73.sines, bf16[2,256,1024]{2,1,0:T(8,128)(2,1)S(1)} %load.2.front.refs_0_, ...), custom_call_target="tpu_custom_call" | custom-call | flops 1 | bytes 1 | tf_op jit(solution)/shard_map/correlate/pallas_call | solution.py:134
  58.7 3.3 %collective-permute-start.9 = (f32[2,2,128,128]{3,2,1,0:T(8,128)S(1)}, f32[2,2,128,128]{3,2,1,0:T(8,128)S(1)}, u32[]{:S(2)}, u32[]{:S(2)}) collective-permute-start(f32[2,2,128,128]{3,2,1,0:T(8,128)S(1)} %get-tuple-element.36), channel_id=1, source_target_pairs={{0,1},{1,0},{2,3},{3,2},{4,5},{5,4},{6,7},{7,6},{8,9},{9,8},{10,11... | collective-permute-start | bytes 786440 | tf_op jit(solution)/shard_map/ppermute | solution.py:305
  62.0 1.6 %correlate.11 = f32[2,2,128,128]{3,2,1,0:T(8,128)S(1)} custom-call(s32[4,12]{1,0:T(4,128)S(1)} %pad_add_fusion.2.meta.slots, f32[12,1024]{1,0:T(8,128)S(1)} %get-tuple-element.74.cosines, f32[12,1024]{1,0:T(8,128)S(1)} %get-tuple-element.73.sines, bf16[2,256,1024]{2,1,0:T(8,128)(2,1)S(1)} %load.2.front.refs_0_, bf16[2,256,1024]{2,1,0:T(8,128)(2,1)S(1)} %load.3.rear.refs_1_, ...), custom_call_target="tpu_custom_call" | custom-call | flops 1 | bytes 1 | tf_op jit(solution)/shard_map/correlate/pallas_call | solution.py:134
  63.6 0.1 exponential_reduce_fusion.1
  63.8 0.1 exponential_reduce_fusion
  63.9 0.1 abs_reduce_fusion
  64.0 0.1 multiply_convert_fusion
  64.3 2.7 %collective-permute-start.10 = (f16[2,264,128]{2,1,0:T(8,128)(2,1)S(1)}, f16[2,264,128]{2,1,0:T(8,128)(2,1)S(1)}, u32[]{:S(2)}, u32[]{:S(2)}) collective-permute-start(f16[2,264,128]{2,1,0:T(8,128)(2,1)S(1)} %pad_maximum_fusion.3), channel_id=1, source_target_pairs={{0,2},{1,3},{2,0},{3,1},{4,6},{5,7},{6,4},{7,5},{8,10},{9,11},{10,... | collective-permute-start | bytes 405512 | tf_op jit(solution)/shard_map/ppermute | solution.py:316
  67.0 0.1 multiply_add_fusion
  67.1 1.3 %rotate.2 = (f32[6,2,128,128]{3,2,1,0:T(8,128)S(1)}, f32[1,2,128,128]{3,2,1,0:T(8,128)S(1)}, f32[1,2,128,128]{3,2,1,0:T(8,128)S(1)}) custom-call(s32[4,12]{1,0:T(4,128)S(1)} %pad_add_fusion.2.meta.slots, f32[4,2,128,128]{3,2,1,0:T(8,128)S(1)} %bitcast.35, bf16[2,4,128,128]{3,2,1,0:T(8,128)(2,1)S(1)} %copy-done, ...), custom_call_target="tpu_custom_call" | custom-call | flops 1 | bytes 1 | tf_op jit(solution)/shard_map/rotate/pallas_call | solution.py:210
  68.4 0.4 collective-permute-start.13
  68.9 0.1 fusion.39
  69.0 2.0 %collective-permute-done.10 = f16[2,264,128]{2,1,0:T(8,128)(2,1)S(1)} collective-permute-done((f16[2,264,128]{2,1,0:T(8,128)(2,1)S(1)}, f16[2,264,128]{2,1,0:T(8,128)(2,1)S(1)}, u32[]{:S(2)}, u32[]{:S(2)}) %collective-permute-start.10) | collective-permute-done | bytes 135200 | tf_op jit(solution)/shard_map/ppermute | solution.py:316
  71.0 0.1 fusion.40
  71.1 0.1 multiply_add_fusion.1
  71.2 1.1 %rotate.3 = (f32[2,2,128,128]{3,2,1,0:T(8,128)S(1)}, f32[1,2,128,128]{3,2,1,0:T(8,128)S(1)}, f32[1,2,128,128]{3,2,1,0:T(8,128)S(1)}) custom-call(s32[4,12]{1,0:T(4,128)S(1)} %pad_add_fusion.2.meta.slots, f32[2,2,128,128]{3,2,1,0:T(8,128)S(1)} %bitcast.37, bf16[2,4,128,128]{3,2,1,0:T(8,128)(2,1)S(1)} %copy-done, ...), custom_call_target="tpu_custom_call" | custom-call | flops 1 | bytes 1 | tf_op jit(solution)/shard_map/rotate/pallas_call | solution.py:210
  72.3 0.1 fusion.3
  72.5 0.1 fusion.2
  72.9 1.2 %collective-permute-start.11 = (f16[2,264,128]{2,1,0:T(8,128)(2,1)S(1)}, f16[2,264,128]{2,1,0:T(8,128)(2,1)S(1)}, u32[]{:S(2)}, u32[]{:S(2)}) collective-permute-start(f16[2,264,128]{2,1,0:T(8,128)(2,1)S(1)} %get-tuple-element.72), channel_id=1, source_target_pairs={{12,0},{0,4},{4,8},{8,12},{28,16},{16,20},{20,24},{24,28},{44,32},... | collective-permute-start | bytes 405512 | tf_op jit(solution)/shard_map/ppermute | solution.py:328
  74.2 1.1 %collective-permute-start.15 = (f32[2,2,128,128]{3,2,1,0:T(8,128)S(1)}, f32[2,2,128,128]{3,2,1,0:T(8,128)S(1)}, u32[]{:S(2)}, u32[]{:S(2)}) collective-permute-start(f32[2,2,128,128]{3,2,1,0:T(8,128)S(1)} %get-tuple-element.51.refs_2_), channel_id=1, source_target_pairs={{0,1},{1,0},{2,3},{3,2},{4,5},{5,4},{6,7},{7,6},{8,9},{9,8},{10,11... | collective-permute-start | bytes 786440 | tf_op jit(solution)/shard_map/ppermute | solution.py:330
  75.2 1.8 %place.2 = (f32[3,2,4,128,128]{4,3,2,1,0:T(8,128)}, f32[3,2,4,128,128]{4,3,2,1,0:T(8,128)}) custom-call(s32[4,12]{1,0:T(4,128)S(1)} %pad_add_fusion.2.meta.slots, f32[6,2,128,128]{3,2,1,0:T(8,128)S(1)} %get-tuple-element.46.refs_0_, f32[6,2,128,128]{3,2,1,0:T(8,128)S(1)} %collective-permute-done.13.refs_1_), custom_call_target="tpu_custom_call" | custom-call | flops 1 | bytes 1 | tf_op jit(solution)/shard_map/place/pallas_call | solution.py:239
  77.0 2.2 %collective-permute-done.12 = f16[2,264,128]{2,1,0:T(8,128)(2,1)S(1)} collective-permute-done((f16[2,264,128]{2,1,0:T(8,128)(2,1)S(1)}, f16[2,264,128]{2,1,0:T(8,128)(2,1)S(1)}, u32[]{:S(2)}, u32[]{:S(2)}) %collective-permute-start.12) | collective-permute-done | bytes 135200 | tf_op jit(solution)/shard_map/ppermute | solution.py:327
  79.3 0.5 collective-permute-done.11
  79.8 1.5 %collective-permute-start.14 = (f16[4,264,128]{2,1,0:T(8,128)(2,1)S(1)}, f16[4,264,128]{2,1,0:T(8,128)(2,1)S(1)}, u32[]{:S(2)}, u32[]{:S(2)}) collective-permute-start(f16[4,264,128]{2,1,0:T(8,128)(2,1)S(1)} %pad_maximum_fusion.2), channel_id=1, source_target_pairs={{0,1},{1,0},{2,3},{3,2},{4,5},{5,4},{6,7},{7,6},{8,9},{9,8},{10,11... | collective-permute-start | bytes 811016 | tf_op jit(solution)/shard_map/ppermute | solution.py:337
  81.3 0.1 fusion.31
  81.4 0.1 convert_multiply_fusion.1
  81.5 0.9 %collective-permute-done.14 = f16[4,264,128]{2,1,0:T(8,128)(2,1)S(1)} collective-permute-done((f16[4,264,128]{2,1,0:T(8,128)(2,1)S(1)}, f16[4,264,128]{2,1,0:T(8,128)(2,1)S(1)}, u32[]{:S(2)}, u32[]{:S(2)}) %collective-permute-start.14) | collective-permute-done | bytes 270368 | tf_op jit(solution)/shard_map/ppermute | solution.py:337
  82.5 0.1 fusion.32
  82.6 0.1 convert_multiply_fusion
  82.7 1.8 %place.3 = (f32[3,2,4,128,128]{4,3,2,1,0:T(8,128)}, f32[3,2,4,128,128]{4,3,2,1,0:T(8,128)}) custom-call(s32[4,12]{1,0:T(4,128)S(1)} %pad_add_fusion.2.meta.slots, f32[4,2,128,128]{3,2,1,0:T(8,128)S(1)} %bitcast.33, f32[4,2,128,128]{3,2,1,0:T(8,128)S(1)} %bitcast.34, ...), custom_call_target="tpu_custom_call", output_to_operand_aliasing={{0}: (5, {}), {1}: (6, {})} | custom-call | flops 1 | bytes 1 | tf_op jit(solution)/shard_map/place/pallas_call | solution.py:239
  (47 shorter events, 1.2 us)
Async XLA Ops:
  1.9 12.1 %copy-start.6 = (s32[256,3]{0,1:T(4,128)S(1)}, s32[256,3]{0,1:T(4,128)}, u32[]{:S(2)}) copy-start(s32[256,3]{0,1:T(4,128)} %param.6) | copy-start | bytes 9220
  1.9 12.6 %copy-start.5 = (s32[256,3,3]{0,2,1:T(4,128)S(1)}, s32[256,3,3]{0,2,1:T(4,128)}, u32[]{:S(2)}) copy-start(s32[256,3,3]{0,2,1:T(4,128)} %param.7) | copy-start | bytes 27652
  1.9 29.3 %collective-permute-start.2 = (bf16[2,256,1024]{2,1,0:T(8,128)(2,1)S(1)}, bf16[2,256,1024]{2,1,0:T(8,128)(2,1)S(1)}, u32[]{:S(2)}, u32[]{:S(2)}) collective-permute-start(bf16[2,256,1024]{2,1,0:T(8,128)(2,1)S(1)} %load.2.front.refs_0_), channel_id=1, source_target_pairs={{0,240},{4,244},{8,248},{12,252},{16,0},{20,4},{24,8},{28,12},{32,... | collective-permute-start | bytes 3145736 | tf_op jit(solution)/shard_map/ppermute | solution.py:271
  9.4 24.0 %collective-permute-start.1 = (bf16[2,256,1024]{2,1,0:T(8,128)(2,1)S(1)}, bf16[2,256,1024]{2,1,0:T(8,128)(2,1)}, u32[]{:S(2)}, u32[]{:S(2)}) collective-permute-start(bf16[2,256,1024]{2,1,0:T(8,128)(2,1)S(1)} %load.2.front.refs_0_), channel_id=1, source_target_pairs={{0,12},{4,0},{8,4},{12,8},{16,28},{20,16},{24,20},{28,24},{32,44},... | collective-permute-start | bytes 3145736 | tf_op jit(solution)/shard_map/ppermute | solution.py:272
  13.1 43.0 %collective-permute-start.5 = (bf16[2,256,1024]{2,1,0:T(8,128)(2,1)S(1)}, bf16[2,256,1024]{2,1,0:T(8,128)(2,1)}, u32[]{:S(2)}, u32[]{:S(2)}) collective-permute-start(bf16[2,256,1024]{2,1,0:T(8,128)(2,1)S(1)} %load.3.rear.refs_1_), channel_id=1, source_target_pairs={{0,240},{4,244},{8,248},{12,252},{16,0},{20,4},{24,8},{28,12},{32,... | collective-permute-start | bytes 3145736 | tf_op jit(solution)/shard_map/ppermute | solution.py:274
  13.3 42.7 %collective-permute-start.4 = (bf16[2,256,1024]{2,1,0:T(8,128)(2,1)S(1)}, bf16[2,256,1024]{2,1,0:T(8,128)(2,1)}, u32[]{:S(2)}, u32[]{:S(2)}) collective-permute-start(bf16[2,256,1024]{2,1,0:T(8,128)(2,1)S(1)} %load.3.rear.refs_1_), channel_id=1, source_target_pairs={{0,12},{4,0},{8,4},{12,8},{16,28},{20,16},{24,20},{28,24},{32,44},... | collective-permute-start | bytes 3145736 | tf_op jit(solution)/shard_map/ppermute | solution.py:275
  18.3 19.7 %copy-start.1 = (bf16[2,2,128,1024]{3,2,1,0:T(8,128)(2,1)}, bf16[2,2,128,1024]{3,2,1,0:T(8,128)(2,1)S(1)}, u32[]{:S(2)}) copy-start(bf16[2,2,128,1024]{3,2,1,0:T(8,128)(2,1)S(1)} %get-tuple-element.28.refs_0_) | copy-start | bytes 3145732
  18.3 23.1 %copy-start = (bf16[2,4,128,128]{3,2,1,0:T(8,128)(2,1)S(1)}, bf16[2,4,128,128]{3,2,1,0:T(8,128)(2,1)}, u32[]{:S(2)}) copy-start(bf16[2,4,128,128]{3,2,1,0:T(8,128)(2,1)} %gauge.3) | copy-start | bytes 786436
  18.3 28.5 %collective-permute-start = (f32[2,2,128,128]{3,2,1,0:T(8,128)}, f32[2,2,128,128]{3,2,1,0:T(8,128)}, u32[]{:S(2)}, u32[]{:S(2)}) collective-permute-start(f32[2,2,128,128]{3,2,1,0:T(8,128)} %get-tuple-element.29), channel_id=1, source_target_pairs={{0,1},{1,0},{2,3},{3,2},{4,5},{5,4},{6,7},{7,6},{8,9},{9,8},{10,11... | collective-permute-start | bytes 786440 | tf_op jit(solution)/shard_map/ppermute | solution.py:305
  31.2 1.0 %copy-start.3 = (bf16[2,256,1024]{2,1,0:T(8,128)(2,1)}, bf16[2,256,1024]{2,1,0:T(8,128)(2,1)S(1)}, u32[]{:S(2)}) copy-start(bf16[2,256,1024]{2,1,0:T(8,128)(2,1)S(1)} %collective-permute-done.2.refs_1_) | copy-start | bytes 3145732
  33.4 1.2 %copy-start.4 = (bf16[2,256,1024]{2,1,0:T(8,128)(2,1)S(1)}, bf16[2,256,1024]{2,1,0:T(8,128)(2,1)}, u32[]{:S(2)}) copy-start(bf16[2,256,1024]{2,1,0:T(8,128)(2,1)} %copy-done.3) | copy-start | bytes 3145732
  38.0 14.0 %collective-permute-start.3 = (f32[2,2,128,128]{3,2,1,0:T(8,128)}, f32[2,2,128,128]{3,2,1,0:T(8,128)}, u32[]{:S(2)}, u32[]{:S(2)}) collective-permute-start(f32[2,2,128,128]{3,2,1,0:T(8,128)} %get-tuple-element.31), channel_id=1, source_target_pairs={{0,1},{1,0},{2,3},{3,2},{4,5},{5,4},{6,7},{7,6},{8,9},{9,8},{10,11... | collective-permute-start | bytes 786440 | tf_op jit(solution)/shard_map/ppermute | solution.py:305
  41.4 17.3 %collective-permute-start.8 = (bf16[2,2,128,128]{3,2,1,0:T(8,128)(2,1)S(1)}, bf16[2,2,128,128]{3,2,1,0:T(8,128)(2,1)S(1)}, u32[]{:S(2)}, u32[]{:S(2)}) collective-permute-start(bf16[2,2,128,128]{3,2,1,0:T(8,128)(2,1)S(1)} %dynamic-slice_bitcast_fusion), channel_id=1, source_target_pairs={{0,240},{4,244},{8,248},{12,252},{16,0},{20,4},{24,8},{28,12},{32,... | collective-permute-start | bytes 393224 | tf_op jit(solution)/shard_map/ppermute | solution.py:278
  43.9 1.2 %copy-start.2 = (bf16[2,2,128,1024]{3,2,1,0:T(8,128)(2,1)S(1)}, bf16[2,2,128,1024]{3,2,1,0:T(8,128)(2,1)}, u32[]{:S(2)}) copy-start(bf16[2,2,128,1024]{3,2,1,0:T(8,128)(2,1)} %copy-done.1) | copy-start | bytes 3145732
  46.8 11.9 %collective-permute-start.7 = (bf16[2,2,128,128]{3,2,1,0:T(8,128)(2,1)S(1)}, bf16[2,2,128,128]{3,2,1,0:T(8,128)(2,1)S(1)}, u32[]{:S(2)}, u32[]{:S(2)}) collective-permute-start(bf16[2,2,128,128]{3,2,1,0:T(8,128)(2,1)S(1)} %dynamic-slice_bitcast_fusion), channel_id=1, source_target_pairs={{0,12},{4,0},{8,4},{12,8},{16,28},{20,16},{24,20},{28,24},{32,44},... | collective-permute-start | bytes 393224 | tf_op jit(solution)/shard_map/ppermute | solution.py:279
  53.4 10.4 %collective-permute-start.6 = (f16[4,264,128]{2,1,0:T(8,128)(2,1)S(1)}, f16[4,264,128]{2,1,0:T(8,128)(2,1)S(1)}, u32[]{:S(2)}, u32[]{:S(2)}) collective-permute-start(f16[4,264,128]{2,1,0:T(8,128)(2,1)S(1)} %pad_maximum_fusion), channel_id=1, source_target_pairs={{0,2},{1,3},{2,0},{3,1},{4,6},{5,7},{6,4},{7,5},{8,10},{9,11},{10,... | collective-permute-start | bytes 811016 | tf_op jit(solution)/shard_map/ppermute | solution.py:311
  58.7 5.0 %collective-permute-start.9 = (f32[2,2,128,128]{3,2,1,0:T(8,128)S(1)}, f32[2,2,128,128]{3,2,1,0:T(8,128)S(1)}, u32[]{:S(2)}, u32[]{:S(2)}) collective-permute-start(f32[2,2,128,128]{3,2,1,0:T(8,128)S(1)} %get-tuple-element.36), channel_id=1, source_target_pairs={{0,1},{1,0},{2,3},{3,2},{4,5},{5,4},{6,7},{7,6},{8,9},{9,8},{10,11... | collective-permute-start | bytes 786440 | tf_op jit(solution)/shard_map/ppermute | solution.py:305
  64.3 6.7 %collective-permute-start.10 = (f16[2,264,128]{2,1,0:T(8,128)(2,1)S(1)}, f16[2,264,128]{2,1,0:T(8,128)(2,1)S(1)}, u32[]{:S(2)}, u32[]{:S(2)}) collective-permute-start(f16[2,264,128]{2,1,0:T(8,128)(2,1)S(1)} %pad_maximum_fusion.3), channel_id=1, source_target_pairs={{0,2},{1,3},{2,0},{3,1},{4,6},{5,7},{6,4},{7,5},{8,10},{9,11},{10,... | collective-permute-start | bytes 405512 | tf_op jit(solution)/shard_map/ppermute | solution.py:316
  68.4 6.8 %collective-permute-start.13 = (f32[6,2,128,128]{3,2,1,0:T(8,128)S(1)}, f32[6,2,128,128]{3,2,1,0:T(8,128)S(1)}, u32[]{:S(2)}, u32[]{:S(2)}) collective-permute-start(f32[6,2,128,128]{3,2,1,0:T(8,128)S(1)} %get-tuple-element.46.refs_0_), channel_id=1, source_target_pairs={{0,1},{1,0},{2,3},{3,2},{4,5},{5,4},{6,7},{7,6},{8,9},{9,8},{10,11... | collective-permute-start | bytes 2359304 | tf_op jit(solution)/shard_map/ppermute | solution.py:329
  72.9 6.4 %collective-permute-start.12 = (f16[2,264,128]{2,1,0:T(8,128)(2,1)S(1)}, f16[2,264,128]{2,1,0:T(8,128)(2,1)S(1)}, u32[]{:S(2)}, u32[]{:S(2)}) collective-permute-start(f16[2,264,128]{2,1,0:T(8,128)(2,1)S(1)} %get-tuple-element.71), channel_id=1, source_target_pairs={{240,0},{244,4},{248,8},{252,12},{0,16},{4,20},{8,24},{12,28},{16,... | collective-permute-start | bytes 405512 | tf_op jit(solution)/shard_map/ppermute | solution.py:327
  72.9 6.8 %collective-permute-start.11 = (f16[2,264,128]{2,1,0:T(8,128)(2,1)S(1)}, f16[2,264,128]{2,1,0:T(8,128)(2,1)S(1)}, u32[]{:S(2)}, u32[]{:S(2)}) collective-permute-start(f16[2,264,128]{2,1,0:T(8,128)(2,1)S(1)} %get-tuple-element.72), channel_id=1, source_target_pairs={{12,0},{0,4},{4,8},{8,12},{28,16},{16,20},{20,24},{24,28},{44,32},... | collective-permute-start | bytes 405512 | tf_op jit(solution)/shard_map/ppermute | solution.py:328
  74.2 8.6 %collective-permute-start.15 = (f32[2,2,128,128]{3,2,1,0:T(8,128)S(1)}, f32[2,2,128,128]{3,2,1,0:T(8,128)S(1)}, u32[]{:S(2)}, u32[]{:S(2)}) collective-permute-start(f32[2,2,128,128]{3,2,1,0:T(8,128)S(1)} %get-tuple-element.51.refs_2_), channel_id=1, source_target_pairs={{0,1},{1,0},{2,3},{3,2},{4,5},{5,4},{6,7},{7,6},{8,9},{9,8},{10,11... | collective-permute-start | bytes 786440 | tf_op jit(solution)/shard_map/ppermute | solution.py:330
  79.8 2.6 %collective-permute-start.14 = (f16[4,264,128]{2,1,0:T(8,128)(2,1)S(1)}, f16[4,264,128]{2,1,0:T(8,128)(2,1)S(1)}, u32[]{:S(2)}, u32[]{:S(2)}) collective-permute-start(f16[4,264,128]{2,1,0:T(8,128)(2,1)S(1)} %pad_maximum_fusion.2), channel_id=1, source_target_pairs={{0,1},{1,0},{2,3},{3,2},{4,5},{5,4},{6,7},{7,6},{8,9},{9,8},{10,11... | collective-permute-start | bytes 811016 | tf_op jit(solution)/shard_map/ppermute | solution.py:337
